TPU v7x, 256 devices: a whole 4x4x8 slice. The times are simulated.
256 devices in a mesh: dp: 64 (over z, x, core), tensor: 4 (over y).
Axes of the slice: x: 4, y: 4, z: 8, core: 2. Of those that a mesh axis runs over, the one named last changes fastest.
Arguments:
- tokens: bfloat16 [24576, 8192], P('dp', 'tensor'), may hold values from -600 to 600
- norm_scale_vector: bfloat16 [8192], P('tensor'), may hold values from 0.5 to 2
- gate_matrix: bfloat16 [8192, 2048], P('dp', 'tensor'), may hold values from -0.0625 to 0.0625
- up_matrix: bfloat16 [8192, 2048], P('dp', 'tensor'), may hold values from -0.0625 to 0.0625
- adapter_down_factors: bfloat16 [64, 8192, 256], P('dp', 'tensor'), may hold values from -0.0625 to 0.0625
- adapter_up_factors: bfloat16 [64, 2, 128, 2048], P('dp', None, None, 'tensor'), may hold values from -0.5 to 0.5
- row_judges: int32 [24576, 1], P('dp'), may hold values from 0 to 63; in each aligned block of 384 rows (0 to 383, 384 to 767, ...) at most 12 rows name the same one
Outputs:
- hidden: bfloat16 [24576, 2048], P('dp', 'tensor')
Inputs may be any that keep to these rules, and one draw needn't show every extreme that they name: `row_judges`: among the 384 rows of one index of dp no judge is named more than 12 times, and on some index some judge is named exactly 12 times.
All inputs are finite; a program needn't handle non-finite values.
Results may differ from a plain program's by a relative error of at most 0.0063.
Values may be sent and summed in bfloat16 or wider, within the bound.
No kernel may reach another device: no remote copies, remote signals or barrier semaphores. Data moves between devices by JAX's collectives and lax.ppermute only.
A program may use at most 128 MiB of HBM per device.

v0:
```python
import jax
import jax.numpy as jnp
from jax import lax
from jax.sharding import PartitionSpec as P

EPSILON = 1e-06
ADAPTER_SCALE = 0.5


def body(
    tokens,
    norm_scale_vector,
    gate_matrix,
    up_matrix,
    adapter_down_factors,
    adapter_up_factors,
    row_judges,
):
    row_count = tokens.shape[0]
    part_width = tokens.shape[1]
    owners = lax.axis_size("dp")
    capacity = 2 * row_count // owners
    column_span = gate_matrix.shape[1]
    narrow_projection = adapter_up_factors.shape[2]
    wide_tokens = tokens.astype(jnp.float32)
    square_sum = lax.psum(jnp.sum(wide_tokens * wide_tokens, axis=1), "tensor")
    factor = lax.rsqrt(square_sum / (part_width * lax.axis_size("tensor")) + EPSILON)
    normed_part = (wide_tokens * factor[:, None] * norm_scale_vector.astype(jnp.float32)).astype(
        jnp.bfloat16
    )
    normalized_input = lax.all_gather(normed_part, "tensor", axis=1, tiled=True)

    def add_piece(weight_piece):
        return jnp.dot(normalized_input, weight_piece, preferred_element_type=jnp.float32)

    gate_plain = add_piece(lax.all_gather(gate_matrix, "dp", axis=0, tiled=True))
    up_plain = add_piece(lax.all_gather(up_matrix, "dp", axis=0, tiled=True))
    labels = row_judges[:, 0]
    owner_ids = jnp.arange(owners, dtype=jnp.int32)
    matches = (labels[:, None] == owner_ids[None, :]).astype(jnp.int32)
    before = jnp.cumsum(matches, axis=0) - matches
    place_in = jnp.sum(before * matches, axis=1)
    slot_index = labels * capacity + place_in
    outgoing = (
        jnp.zeros((owners * capacity, part_width), jnp.bfloat16).at[slot_index].set(normed_part)
    )
    outgoing = outgoing.reshape(owners, capacity, part_width)
    judge_down_factor = adapter_down_factors[0]
    judge_up_factor = adapter_up_factors[0]
    partial_sums = jnp.einsum(
        "sid,dr->sir",
        lax.all_to_all(outgoing, "dp", split_axis=0, concat_axis=0, tiled=True),
        judge_down_factor,
        preferred_element_type=jnp.float32,
    )
    down_projected = lax.psum(partial_sums, "tensor").astype(jnp.bfloat16)
    gate_adjustment = jnp.einsum(
        "sir,rf->sif",
        down_projected[:, :, :narrow_projection],
        judge_up_factor[0],
        preferred_element_type=jnp.float32,
    ).astype(jnp.bfloat16)
    up_adjustment = jnp.einsum(
        "sir,rf->sif",
        down_projected[:, :, narrow_projection:],
        judge_up_factor[1],
        preferred_element_type=jnp.float32,
    ).astype(jnp.bfloat16)
    deltas = jnp.concatenate([gate_adjustment, up_adjustment], axis=2)
    returned = lax.all_to_all(deltas, "dp", split_axis=0, concat_axis=0, tiled=True)
    returned_rows = returned.reshape(owners * capacity, 2 * column_span)
    judge_adjustments = returned_rows[slot_index]
    gate_combined = gate_plain + ADAPTER_SCALE * judge_adjustments[:, :column_span].astype(
        jnp.float32
    )
    up_combined = up_plain + ADAPTER_SCALE * judge_adjustments[:, column_span:].astype(jnp.float32)
    return (jax.nn.silu(gate_combined) * up_combined).astype(jnp.bfloat16)


def solution(mesh):
    placed = (
        P("dp", "tensor"),
        P("tensor"),
        P("dp", "tensor"),
        P("dp", "tensor"),
        P("dp", "tensor", None),
        P("dp", None, None, "tensor"),
        P("dp", None),
    )
    return jax.shard_map(
        body, mesh=mesh, in_specs=placed, out_specs=P("dp", "tensor"), check_vma=False
    )
```

profile of v0, /device:TPU:1, one launch (start us, length us, event | category | flops | bytes accessed | tf_op | source)
XLA Modules:
  0.0 289.8 jit_solution(4303549950230186500)
XLA Ops:
  6.5 0.0 copy-start
  6.5 0.8 convert_element_type.35
  7.3 1.8 fusion
  9.1 9.7 %psum.14 = f32[384]{0:T(512)S(1)} all-reduce(f32[384]{0:T(512)S(1)} %fusion), channel_id=1, replica_groups=mesh['dp'=64,'tensor'=4] {'tensor'}, use_global_device_ids=true, to_apply=%region_1.0 | all-reduce | flops 384 | bytes 3072 | tf_op jit(solution)/shard_map/psum | solution.py:26
  18.8 3.0 %fusion.2 = bf16[384,2048]{1,0:T(8,128)(2,1)} fusion(bf16[384,2048]{1,0:T(8,128)(2,1)} %param.7, f32[2048]{0:T(1024)S(1)} %convert_element_type.35, f32[384]{0:T(512)S(1)} %add_rsqrt_fusion), kind=kLoop, calls=%fused_computation.6 | loop fusion | flops 3145728 | bytes 3155456 | tf_op jit(solution)/shard_map/convert_element_type | solution.py:28
  21.8 0.0 all-gather.4.cloned.1.call-update
  21.8 0.0 all-gather.6.cloned.1.call-start
  21.9 0.7 all-gather.6.cloned.1.call-update
  22.6 0.0 all-gather.8.cloned.1.call-start
  22.6 0.7 all-gather.8.cloned.1.call-update
  23.4 0.9 reduce-window.6
  24.3 0.2 slice_reduce_fusion
  24.5 0.1 fusion.18
  24.7 5.2 %scatter_custom_fusion = bf16[768,2048]{1,0:T(8,128)(2,1)} fusion(s32[384]{0:T(512)S(1)} %fusion.20, bf16[]{:T(256)} %constant.6.clone.1, bf16[384,2048]{1,0:T(8,128)(2,1)S(1)} %copy-done.1, f32[2048]{0:T(1024)S(1)} %convert_element_type.35, f32[384]{0:T(512)S(1)} %add_rsqrt_fusion), kind=kCustom, calls=%fused_computation.10 | custom fusion | flops 3145728 | bytes 4728834 | tf_op jit(solution)/shard_map/scatter | solution.py:45
  29.9 6.1 %reshape.30 = bf16[64,12,2048]{2,1,0:T(8,128)(2,1)} reshape(bf16[768,2048]{1,0:T(8,128)(2,1)} %scatter_custom_fusion) | data formatting | bytes 6291456 | tf_op jit(solution)/shard_map/reshape | solution.py:47
  36.0 113.8 %all_to_all.10 = bf16[64,12,2048]{2,1,0:T(8,128)(2,1)S(1)} all-to-all(bf16[64,12,2048]{2,1,0:T(8,128)(2,1)} %reshape.30), channel_id=1, replica_groups=mesh['dp'=64,'tensor'=4] {'dp'}, dimensions={0} | all-to-all | bytes 6291456 | tf_op jit(solution)/shard_map/all_to_all | solution.py:52
  149.8 0.0 copy-done
  149.8 3.5 %fusion.3 = f32[64,12,256]{2,0,1:T(8,128)S(1)} fusion(bf16[64,12,2048]{2,1,0:T(8,128)(2,1)S(1)} %all_to_all.10, bf16[1,2048,256]{2,1,0:T(8,128)(2,1)S(1)} %copy-done), kind=kOutput, calls=%fused_computation.7 | convolution fusion | flops 805306368 | bytes 4980736 | tf_op jit(solution)/shard_map/sid,dr->sir/dot_general | solution.py:50
  153.3 20.8 %all-reduce.1 = bf16[64,12,256]{2,0,1:T(8,128)(2,1)S(1)} all-reduce(f32[64,12,256]{2,0,1:T(8,128)S(1)} %fusion.3), channel_id=1, replica_groups=mesh['dp'=64,'tensor'=4] {'tensor'}, use_global_device_ids=true, to_apply=%region_6.7 | all-reduce | flops 196608 | bytes 1179648 | tf_op jit(solution)/shard_map/psum | solution.py:56
  174.1 0.3 convolution_convert_fusion
  174.5 0.3 convolution_convert_fusion.1
  174.8 0.2 pad_maximum_fusion
  175.0 2.3 copy.13
  177.3 11.8 %all-to-all-start.1 = ((bf16[64,12,1024]{2,1,0:T(8,128)(2,1)}), bf16[64,12,1024]{2,1,0:T(8,128)(2,1)}, u32[]{:S(2)}, u32[]{:S(2)}) async-start(bf16[64,12,1024]{2,1,0:T(8,128)(2,1)} %copy.13), calls=%async_computation.1 | async-start | bytes 4194304 | tf_op jit(solution)/shard_map/all_to_all | solution.py:70
  189.1 54.5 %all-to-all-done.1 = bf16[64,12,1024]{2,1,0:T(8,128)(2,1)} async-done(((bf16[64,12,1024]{2,1,0:T(8,128)(2,1)}), bf16[64,12,1024]{2,1,0:T(8,128)(2,1)}, u32[]{:S(2)}, u32[]{:S(2)}) %all-to-all-start.1) | async-done | bytes 1572896 | tf_op jit(solution)/shard_map/all_to_all | solution.py:70
  243.6 2.5 reshape.31
  246.1 2.1 gather_fusion
  248.2 0.0 all-gather.4.cloned.1.call-done
  248.3 0.0 all-gather.6.cloned.1.call-done
  248.3 8.0 %convolution_add_fusion.1 = f32[384,512]{1,0:T(8,128)S(1)} fusion(bf16[384,8192]{1,0:T(8,128)(2,1)} %all-gather.4.cloned.1.call-done, bf16[8192,512]{1,0:T(8,128)(2,1)} %all-gather.6.cloned.1.call-done, bf16[384,1024]{1,0:T(8,128)(2,1)S(1)} %gather_fusion), kind=kOutput, calls=%fused_computation.16 | convolution fusion | flops 3221815296 | bytes 15859712 | tf_op jit(solution)/shard_map/dot_general | solution.py:34
  256.3 17.6 %all-gather.8.cloned.1.call-done = bf16[8192,512]{1,0:T(8,128)(2,1)} async-done(((bf16[128,512]{1,0:T(8,128)(2,1)}), bf16[8192,512]{1,0:T(8,128)(2,1)}) %all-gather.8.cloned.1.call-update) | async-done | bytes 8388624 | tf_op jit(solution)/shard_map/all_gather | solution.py:37
  273.9 9.4 %fusion.8 = bf16[384,512]{1,0:T(8,128)(2,1)} fusion(bf16[384,8192]{1,0:T(8,128)(2,1)} %all-gather.4.cloned.1.call-done, bf16[8192,512]{1,0:T(8,128)(2,1)} %all-gather.8.cloned.1.call-done, f32[384,512]{1,0:T(8,128)S(1)} %convolution_add_fusion.1, bf16[384,1024]{1,0:T(8,128)(2,1)S(1)} %gather_fusion), kind=kOutput, calls=%fused_computation.17 | convolution fusion | flops 3222994944 | bytes 16252928 | tf_op jit(solution)/shard_map/dot_general | solution.py:34
  (13 shorter events, 0.1 us)
Async XLA Ops:
  6.5 143.3 %copy-start = (bf16[1,2048,256]{2,1,0:T(8,128)(2,1)S(1)}, bf16[1,2048,256]{2,1,0:T(8,128)(2,1)}, u32[]{:S(2)}) copy-start(bf16[1,2048,256]{2,1,0:T(8,128)(2,1)} %param.11) | copy-start | bytes 3145732
  6.5 241.7 %all-gather.4.cloned.1.call-start = ((), (), s32[]{:S(2)}) async-start(), calls=%async_computation.2 | async-start | bytes 7864320 | tf_op jit(solution)/shard_map/all_gather | solution.py:31
  7.3 16.0 %copy-start.3 = (s32[384,1]{0,1:T(1,128)S(1)}, s32[384,1]{0,1:T(1,128)}, u32[]{:S(2)}) copy-start(s32[384,1]{0,1:T(1,128)} %param.13) | copy-start | bytes 4612
  9.1 15.6 %copy-start.1 = (bf16[384,2048]{1,0:T(8,128)(2,1)S(1)}, bf16[384,2048]{1,0:T(8,128)(2,1)}, u32[]{:S(2)}) copy-start(bf16[384,2048]{1,0:T(8,128)(2,1)} %param.7) | copy-start | bytes 4718596
  21.8 226.4 %all-gather.6.cloned.1.call-start = ((), (), s32[]{:S(2)}) async-start(), calls=%async_computation.3 | async-start | bytes 8519680 | tf_op jit(solution)/shard_map/all_gather | solution.py:36
  22.6 251.3 %all-gather.8.cloned.1.call-start = ((), (), s32[]{:S(2)}) async-start(), calls=%async_computation.4 | async-start | bytes 8519680 | tf_op jit(solution)/shard_map/all_gather | solution.py:37
  149.8 24.3 %copy-start.2 = (bf16[1,2,128,512]{3,2,1,0:T(8,128)(2,1)S(1)}, bf16[1,2,128,512]{3,2,1,0:T(8,128)(2,1)}, u32[]{:S(2)}) copy-start(bf16[1,2,128,512]{3,2,1,0:T(8,128)(2,1)} %param.12) | copy-start | bytes 786436
  177.3 66.3 %all-to-all-start.1 = ((bf16[64,12,1024]{2,1,0:T(8,128)(2,1)}), bf16[64,12,1024]{2,1,0:T(8,128)(2,1)}, u32[]{:S(2)}, u32[]{:S(2)}) async-start(bf16[64,12,1024]{2,1,0:T(8,128)(2,1)} %copy.13), calls=%async_computation.1 | async-start | bytes 4194304 | tf_op jit(solution)/shard_map/all_to_all | solution.py:70
Sparse Core Ops, SparseCore 0:
  22.0 70.8 all-gather.3
  95.7 90.0 all-gather.5
  188.5 85.3 all-gather.7
where the time goes:
time: 290 us
  blocking collectives  144 us (50%)
  waiting for transfers between devices  73.5 us (25%)
  matrix products  21.6 us (7%)
  local copies, waits for them, and re-layouts  13.2 us (5%)
  between operations  13.2 us (5%)
  other arithmetic  12.1 us (4%)
  starting transfers between devices  11.9 us (4%)
    all_to_all x1, blocking collectives, body(): lax.all_to_all(outgoing, 'dp', split_axis=0, concat_axis=0, tiled=True)  114 us
    all_to_all x1, waiting for transfers between devices, body(): lax.all_to_all(deltas, 'dp', split_axis=0, concat_axis=0, tiled=True)  54.5 us
    psum x1, blocking collectives, body(): down_projected = lax.psum(partial_sums, 'tensor').astype(jnp.bfloat16)  20.8 us
    all_gather x1, waiting for transfers between devices, body(): up_plain = add_piece(lax.all_gather(up_matrix, 'dp', axis=0, tiled=True))  17.6 us
    dot_general x2, matrix products, add_piece(): jnp.dot(normalized_input, weight_piece, preferred_element_type=jnp.float32)  17.4 us
    all_to_all x1, starting transfers between devices, body(): lax.all_to_all(deltas, 'dp', split_axis=0, concat_axis=0, tiled=True)  11.8 us
    psum x1, blocking collectives, body(): square_sum = lax.psum(jnp.sum(wide_tokens * wide_tokens, axis=1), 'tensor')  9.69 us
    reshape x1, local copies, waits for them, and re-layouts, body(): outgoing = outgoing.reshape(owners, capacity, part_width)  6.07 us
  transfers between devices with their start and end apart: 4, of which 2 were waited for; matrix products, arithmetic and copies ran while one was open for 11% of the time, Pallas kernels for 0%

commit v1 on v0

v1 whole, which is shorter than its diff:
```python
import jax
import jax.numpy as jnp
from jax import lax
from jax.sharding import Mesh, PartitionSpec as P

EPSILON = 1e-06
ADAPTER_SCALE = 0.5
SWAP = [(0, 1), (1, 0)]
CHIP = ("z", "x")


def shift(array, distance, size):
    return lax.ppermute(array, "y", [(i, (i + distance) % size) for i in range(size)])


def dot(a, b):
    return jnp.dot(a, b, preferred_element_type=jnp.float32)


def body(tokens, scale, gate_matrix, up_matrix, down, up_factors, row_judges):
    f32, bf16 = jnp.float32, jnp.bfloat16
    rows, width = tokens.shape
    chips = lax.axis_size("z") * lax.axis_size("x")
    judges = 2 * chips
    cap = 2 * rows // judges
    ny = lax.axis_size("y")
    core, y = lax.axis_index("c"), lax.axis_index("y")
    half = width // 2
    span = gate_matrix.shape[1]
    cols = span // 2
    rank_width = down.shape[2] // 2

    wide = tokens.astype(f32)
    scaled = (wide * scale.astype(f32)).astype(bf16)
    squares = jnp.sum(wide * wide, axis=1)
    weights = lax.all_gather(
        jnp.concatenate([gate_matrix, up_matrix], axis=1), CHIP + ("c",), axis=0, tiled=True
    )
    everything = lax.all_gather(scaled, "y", axis=1, tiled=True)

    labels = row_judges[:, 0]
    matches = (labels[:, None] == jnp.arange(judges, dtype=jnp.int32)[None, :]).astype(bf16)
    at = jnp.arange(rows, dtype=jnp.int32)
    before = dot((at[:, None] > at[None, :]).astype(bf16), matches)
    place = jnp.sum(before * matches.astype(f32), axis=1).astype(jnp.int32)
    own_slot = labels * (2 * cap) + core * cap + place
    other_slot = lax.ppermute(own_slot, "c", SWAP)
    slots = jnp.concatenate([own_slot, other_slot])
    count = judges * 2 * cap
    slot_at = jnp.arange(count, dtype=jnp.int32)
    choose = (slot_at[:, None] == slots[None, :]).astype(bf16)

    own_half = lax.dynamic_slice_in_dim(scaled, core * half, half, 1)
    sent_half = lax.dynamic_slice_in_dim(scaled, (1 - core) * half, half, 1)
    both = jnp.concatenate([own_half, lax.ppermute(sent_half, "c", SWAP)], axis=0)
    outgoing = dot(choose, both).astype(bf16).reshape(chips, 4 * cap, half)
    arrived = lax.all_to_all(outgoing, CHIP, 0, 0, tiled=True).reshape(count, half)

    down_own = lax.dynamic_slice_in_dim(down[0], core * half, half, 0)
    down_sent = lax.dynamic_slice_in_dim(down[0], (1 - core) * half, half, 0)
    down_both = jnp.concatenate([down_own, lax.ppermute(down_sent, "c", SWAP)], axis=1)
    up_own = lax.dynamic_slice_in_dim(up_factors[0], core * cols, cols, 2)
    up_sent = lax.dynamic_slice_in_dim(up_factors[0], (1 - core) * cols, cols, 2)
    up_both = jnp.concatenate([up_own, lax.ppermute(up_sent, "c", SWAP)], axis=2)

    mine = ((slot_at // (2 * cap)) % 2 == core)[:, None]

    def pick(both_judges):
        w = both_judges.shape[1] // 2
        return jnp.where(mine, both_judges[:, :w], both_judges[:, w:])

    partial = pick(dot(arrived, down_both))
    mid = count // 2
    kept = lax.dynamic_slice_in_dim(partial, core * mid, mid, 0)
    passed = lax.dynamic_slice_in_dim(partial, (1 - core) * mid, mid, 0)
    partial = kept + lax.ppermute(passed, "c", SWAP)
    piece = mid // ny

    def piece_at(owner):
        return lax.dynamic_slice_in_dim(partial, (owner % ny) * piece, piece, 0)

    total = piece_at(y)
    for d in range(1, ny):
        total = total + shift(piece_at(y + d), d, ny)
    total = total.astype(bf16)
    code = jnp.zeros((mid, 2 * rank_width), bf16)
    code = lax.dynamic_update_slice_in_dim(code, total, y * piece, 0)
    for d in range(1, ny):
        code = lax.dynamic_update_slice_in_dim(
            code, shift(total, d, ny), ((y - d) % ny) * piece, 0
        )
    code_other = lax.ppermute(code, "c", SWAP)
    first = jnp.where(core == 0, code, code_other)
    second = jnp.where(core == 0, code_other, code)
    codes = jnp.concatenate([first, second], axis=0)

    gate_delta = pick(dot(codes[:, :rank_width], up_both[0]))
    up_delta = pick(dot(codes[:, rank_width:], up_both[1]))
    deltas = jnp.concatenate([gate_delta, up_delta], axis=1).astype(bf16)
    returned = lax.all_to_all(
        deltas.reshape(chips, 4 * cap, span), CHIP, 0, 0, tiled=True
    ).reshape(count, span)
    by_row = lax.dot_general(
        choose, returned, (((0,), (0,)), ((), ())), preferred_element_type=f32
    ).astype(bf16)
    here = by_row[:rows]
    there = lax.ppermute(by_row[rows:], "c", SWAP)
    low = jnp.where(core == 0, here, there).astype(f32)
    high = jnp.where(core == 0, there, here).astype(f32)

    sums = squares
    for d in range(1, ny):
        sums = sums + shift(squares, d, ny)
    factor = lax.rsqrt(sums / (width * ny) + EPSILON)[:, None]

    plain = dot(everything, weights)
    gate_add = jnp.concatenate([low[:, :cols], high[:, :cols]], axis=1)
    up_add = jnp.concatenate([low[:, cols:], high[:, cols:]], axis=1)
    gate = (plain[:, :span] + ADAPTER_SCALE * gate_add) * factor
    up = (plain[:, span:] + ADAPTER_SCALE * up_add) * factor
    return (jax.nn.silu(gate) * up).astype(bf16)


def solution(mesh):
    cut = Mesh(mesh.devices.reshape(8, 4, 2, 4), ("z", "x", "c", "y"))
    dp = ("z", "x", "c")
    placed = (
        P(dp, "y"),
        P("y"),
        P(dp, "y"),
        P(dp, "y"),
        P(dp, "y", None),
        P(dp, None, None, "y"),
        P(dp, None),
    )
    return jax.shard_map(body, mesh=cut, in_specs=placed, out_specs=P(dp, "y"), check_vma=False)
```

time: 290 us -> 236 us (0.81)
  blocking collectives: 144 us -> 62.2 us
  waiting for transfers between devices: 73.5 us -> 95.1 us
  starting transfers between devices: 11.9 us -> 32.3 us
  local copies, waits for them, and re-layouts: 13.2 us -> 3.54 us
  other arithmetic: 12.1 us -> 7.37 us
    all_to_all x1, blocking collectives: 114 us -> 62.2 us  [body(): lax.all_to_all(deltas.reshape(chips, 4 * cap, span), CHIP, 0, 0, tiled=True)]
    psum x2 -> x0, blocking collectives: 30.5 us -> none  [the longest x1 20.8 us: body(): down_projected = lax.psum(partial_sums, 'tensor').astype(jnp.bfloat16)]
    ppermute x0 -> x16, starting transfers between devices: none -> 23 us  [the longest x9 12.7 us: shift(): lax.ppermute(array, 'y', [(i, (i + distance) % size) for i in range(size)])]
    ppermute x0 -> x16, waiting for transfers between devices: none -> 21.2 us  [the longest x9 15 us: shift(): lax.ppermute(array, 'y', [(i, (i + distance) % size) for i in range(size)])]
    all_to_all x1, waiting for transfers between devices: 54.5 us -> 65.9 us  [body(): lax.all_to_all(outgoing, CHIP, 0, 0, tiled=True).reshape(count, half)]
    all_gather x3 -> x2, waiting for transfers between devices: 17.6 us -> 7.89 us  [the longest x1 7.87 us: body(): lax.all_gather(jnp.concatenate([gate_matrix, up_matrix], axis=1), CHIP +...]
    reshape x2 -> x0, local copies, waits for them, and re-layouts: 8.6 us -> none  [the longest x1 6.07 us: body(): outgoing = outgoing.reshape(owners, capacity, part_width)]
    scatter x1 -> x0, other arithmetic: 5.24 us -> none  [body(): jnp.zeros((owners * capacity, part_width), jnp.bfloat16).at[slot_index]]
  transfers between devices with their start and end apart: 4 -> 19, of which waited for: 2 -> 15; matrix products, arithmetic and copies ran while one was open for 11% -> 6% of each run, Pallas kernels for 0% -> 0%
where the time goes in v1:
time: 236 us
  waiting for transfers between devices  95.1 us (40%)
  blocking collectives  62.2 us (26%)
  starting transfers between devices  32.3 us (14%)
  matrix products  21.9 us (9%)
  between operations  13.6 us (6%)
  other arithmetic  7.37 us (3%)
  local copies, waits for them, and re-layouts  3.54 us (2%)
    all_to_all x1, waiting for transfers between devices, body(): lax.all_to_all(outgoing, CHIP, 0, 0, tiled=True).reshape(count, half)  65.9 us
    all_to_all x1, blocking collectives, body(): lax.all_to_all(deltas.reshape(chips, 4 * cap, span), CHIP, 0, 0, tiled=True)  62.2 us
    dot_general x6, matrix products, dot(): return jnp.dot(a, b, preferred_element_type=jnp.float32)  20.4 us
    ppermute x9, waiting for transfers between devices, shift(): lax.ppermute(array, 'y', [(i, (i + distance) % size) for i in range(size)])  15 us
    ppermute x9, starting transfers between devices, shift(): lax.ppermute(array, 'y', [(i, (i + distance) % size) for i in range(size)])  12.7 us
    all_to_all x1, starting transfers between devices, body(): lax.all_to_all(outgoing, CHIP, 0, 0, tiled=True).reshape(count, half)  9.3 us
    all_gather x1, waiting for transfers between devices, body(): lax.all_gather(jnp.concatenate([gate_matrix, up_matrix], axis=1), CHIP +...  7.87 us
  transfers between devices with their start and end apart: 19, of which 15 were waited for; matrix products, arithmetic and copies ran while one was open for 6% of the time, Pallas kernels for 0%

profile of v1, /device:TPU:1, one launch (start us, length us, event | category | flops | bytes accessed | tf_op | source)
XLA Modules:
  0.0 236.0 jit_solution(2027003536621728320)
XLA Ops:
  7.2 3.1 %fusion.4 = (f32[384]{0:T(512)S(1)}, bf16[384,2048]{1,0:T(8,128)(2,1)}) fusion(bf16[384,2048]{1,0:T(8,128)(2,1)} %param.7, f32[2048]{0:T(1024)S(1)} %convert_element_type.41), kind=kLoop, calls=%fused_computation.7 | loop fusion | flops 3931776 | bytes 3155456 | tf_op jit(solution)/shard_map/reduce_sum | solution.py:35
  10.4 0.7 pad_maximum_fusion.3
  11.9 3.3 %collective-permute-start.1 = (bf16[384,1024]{1,0:T(8,128)(2,1)S(1)}, bf16[384,1024]{1,0:T(8,128)(2,1)S(1)}, u32[]{:S(2)}, u32[]{:S(2)}) collective-permute-start(bf16[384,1024]{1,0:T(8,128)(2,1)S(1)} %get-tuple-element.10), channel_id=1, source_target_pairs={{0,4},{4,0},{1,5},{5,1},{2,6},{6,2},{3,7},{7,3},{8,12},{12,8},{9,1... | collective-permute-start | bytes 2359304 | tf_op jit(solution)/shard_map/ppermute | solution.py:55
  16.1 1.1 collective-permute-done
  17.2 4.0 %fusion.2 = bf16[1536,1024]{1,0:T(8,128)(2,1)} fusion(s32[768]{0:T(1024)S(1)} %pad_add_fusion, bf16[384,1024]{1,0:T(8,128)(2,1)S(1)} %collective-permute-done.1, bf16[384,1024]{1,0:T(8,128)(2,1)S(1)} %get-tuple-element.9), kind=kOutput, calls=%fused_computation.5 | convolution fusion | flops 2421817344 | bytes 4721664 | tf_op jit(solution)/shard_map/dot_general | solution.py:17
  21.2 9.3 %all-to-all-start = ((bf16[32,48,1024]{2,1,0:T(8,128)(2,1)}), bf16[32,48,1024]{2,1,0:T(8,128)(2,1)S(1)}, u32[]{:S(2)}, u32[]{:S(2)}) async-start(bf16[32,48,1024]{2,1,0:T(8,128)(2,1)} %bitcast.24), calls=%async_computation | async-start | bytes 6291456 | tf_op jit(solution)/shard_map/all_to_all | solution.py:57
  30.6 2.4 %dynamic-slice_bitcast_fusion.1 = (bf16[1024,256]{1,0:T(8,128)(2,1)}, bf16[1024,256]{1,0:T(8,128)(2,1)}) fusion(bf16[1,2048,256]{2,1,0:T(8,128)(2,1)} %param.11, s32[]{:T(128)S(6)} %select_n.132, s32[]{:T(128)S(6)} %select_n.133), kind=kLoop, calls=%fused_computation.39 | loop fusion | bytes 2097160 | tf_op jit(solution)/shard_map/dynamic_slice | solution.py:59
  33.6 1.9 collective-permute-done.2
  35.5 65.9 %all-to-all-done = bf16[32,48,1024]{2,1,0:T(8,128)(2,1)S(1)} async-done(((bf16[32,48,1024]{2,1,0:T(8,128)(2,1)}), bf16[32,48,1024]{2,1,0:T(8,128)(2,1)S(1)}, u32[]{:S(2)}, u32[]{:S(2)}) %all-to-all-start) | async-done | bytes 3145760 | tf_op jit(solution)/shard_map/all_to_all | solution.py:57
  101.4 3.0 %fusion.14 = f32[1536,512]{1,0:T(8,128)S(1)} fusion(bf16[1536,1024]{1,0:T(8,128)(2,1)S(1)} %bitcast.23, bf16[1024,256]{1,0:T(8,128)(2,1)} %collective-permute-done.2, bf16[1024,256]{1,0:T(8,128)(2,1)} %get-tuple-element.13), kind=kOutput, calls=%fused_computation.22 | convolution fusion | flops 1612709888 | bytes 7340032 | tf_op jit(solution)/shard_map/dot_general | solution.py:17
  104.8 2.5 %collective-permute-start.3 = (f32[768,256]{1,0:T(8,128)S(1)}, f32[768,256]{1,0:T(8,128)S(1)}, u32[]{:S(2)}, u32[]{:S(2)}) collective-permute-start(f32[768,256]{1,0:T(8,128)S(1)} %constant_dynamic-slice_fusion.3), channel_id=1, source_target_pairs={{0,4},{4,0},{1,5},{5,1},{2,6},{6,2},{3,7},{7,3},{8,12},{12,8},{9,1... | collective-permute-start | bytes 2359304 | tf_op jit(solution)/shard_map/ppermute | solution.py:76
  107.2 1.9 collective-permute-done.3
  109.3 1.4 collective-permute-start.4
  110.7 2.6 %collective-permute-start.5 = (f32[192,256]{1,0:T(8,128)S(1)}, f32[192,256]{1,0:T(8,128)S(1)}, u32[]{:S(2)}, u32[]{:S(2)}) collective-permute-start(f32[192,256]{1,0:T(8,128)S(1)} %get-tuple-element.23), channel_id=1, source_target_pairs={{0,2},{1,3},{2,0},{3,1},{4,6},{5,7},{6,4},{7,5},{8,10},{9,11},{10,... | collective-permute-start | bytes 589832 | tf_op jit(solution)/shard_map/ppermute | solution.py:13
  113.3 1.1 collective-permute-start.6
  114.4 2.6 %collective-permute-done.4 = f32[192,256]{1,0:T(8,128)S(1)} collective-permute-done((f32[192,256]{1,0:T(8,128)S(1)}, f32[192,256]{1,0:T(8,128)S(1)}, u32[]{:S(2)}, u32[]{:S(2)}) %collective-permute-start.4) | collective-permute-done | bytes 196640 | tf_op jit(solution)/shard_map/ppermute | solution.py:13
  117.0 5.2 %collective-permute-done.5 = f32[192,256]{1,0:T(8,128)S(1)} collective-permute-done((f32[192,256]{1,0:T(8,128)S(1)}, f32[192,256]{1,0:T(8,128)S(1)}, u32[]{:S(2)}, u32[]{:S(2)}) %collective-permute-start.5) | collective-permute-done | bytes 196640 | tf_op jit(solution)/shard_map/ppermute | solution.py:13
  122.3 1.1 collective-permute-start.7
  123.4 2.7 %collective-permute-start.8 = (bf16[192,256]{1,0:T(8,128)(2,1)S(1)}, bf16[192,256]{1,0:T(8,128)(2,1)S(1)}, u32[]{:S(2)}, u32[]{:S(2)}) collective-permute-start(bf16[192,256]{1,0:T(8,128)(2,1)S(1)} %get-tuple-element.6), channel_id=1, source_target_pairs={{0,2},{1,3},{2,0},{3,1},{4,6},{5,7},{6,4},{7,5},{8,10},{9,11},{10,... | collective-permute-start | bytes 294920 | tf_op jit(solution)/shard_map/ppermute | solution.py:13
  126.6 0.9 collective-permute-done.7
  127.5 3.2 %collective-permute-done.8 = bf16[192,256]{1,0:T(8,128)(2,1)S(1)} collective-permute-done((bf16[192,256]{1,0:T(8,128)(2,1)S(1)}, bf16[192,256]{1,0:T(8,128)(2,1)S(1)}, u32[]{:S(2)}, u32[]{:S(2)}) %collective-permute-start.8) | collective-permute-done | bytes 98336 | tf_op jit(solution)/shard_map/ppermute | solution.py:13
  131.0 1.7 collective-permute-start.10
  132.8 1.2 collective-permute-done.10
  135.3 0.9 fusion.8
  136.4 62.2 %all_to_all.10 = bf16[32,48,512]{2,1,0:T(8,128)(2,1)S(1)} all-to-all(bf16[32,48,512]{2,1,0:T(8,128)(2,1)S(1)} %pad_maximum_fusion), channel_id=1, replica_groups=mesh['z'=8,'x'=4,'c'=2,'y'=4] {'z','x'}, dimensions={0} | all-to-all | bytes 3145728 | tf_op jit(solution)/shard_map/all_to_all | solution.py:100
  198.6 1.4 fusion.12
  200.1 1.5 collective-permute-start.12
  202.2 2.7 %collective-permute-start.14 = (f32[384]{0:T(512)S(1)}, f32[384]{0:T(512)S(1)}, u32[]{:S(2)}, u32[]{:S(2)}) collective-permute-start(f32[384]{0:T(512)S(1)} %get-tuple-element.7), channel_id=1, source_target_pairs={{0,2},{1,3},{2,0},{3,1},{4,6},{5,7},{6,4},{7,5},{8,10},{9,11},{10,... | collective-permute-start | bytes 4616 | tf_op jit(solution)/shard_map/ppermute | solution.py:13
  206.2 1.5 collective-permute-done.15
  208.1 7.9 %all-gather.5.cloned.1.call-done = bf16[8192,1024]{1,0:T(8,128)(2,1)} async-done(((bf16[128,1024]{1,0:T(8,128)(2,1)}), bf16[8192,1024]{1,0:T(8,128)(2,1)}) %all-gather.5.cloned.1.call-update) | async-done | bytes 16777232 | tf_op jit(solution)/shard_map/all_gather | solution.py:36
  215.9 12.0 %fusion.46 = f32[384,1024]{1,0:T(8,128)S(1)} fusion(bf16[384,8192]{1,0:T(8,128)(2,1)} %all-gather.3.cloned.1.call-done, bf16[8192,1024]{1,0:T(8,128)(2,1)} %all-gather.5.cloned.1.call-done), kind=kOutput, calls=%fused_computation.94 | convolution fusion | flops 6442450944 | bytes 24641536 | tf_op jit(solution)/shard_map/dot_general | solution.py:17
  228.0 1.2 fusion.20
  (53 shorter events, 8.2 us)
Async XLA Ops:
  6.5 201.5 %all-gather.3.cloned.1.call-start = ((), (), s32[]{:S(2)}) async-start(), calls=%async_computation.2 | async-start | bytes 7864320 | tf_op jit(solution)/shard_map/all_gather | solution.py:39
  7.2 3.1 %copy-start.2 = (bf16[128,512]{1,0:T(8,128)(2,1)S(1)}, bf16[128,512]{1,0:T(8,128)(2,1)}, u32[]{:S(2)}) copy-start(bf16[128,512]{1,0:T(8,128)(2,1)} %param.10) | copy-start | bytes 393220
  7.2 3.2 %copy-start.3 = (bf16[128,512]{1,0:T(8,128)(2,1)S(1)}, bf16[128,512]{1,0:T(8,128)(2,1)}, u32[]{:S(2)}) copy-start(bf16[128,512]{1,0:T(8,128)(2,1)} %param.9) | copy-start | bytes 393220
  10.3 1.5 copy-start
  10.3 205.6 %all-gather.5.cloned.1.call-start = ((), (), s32[]{:S(2)}) async-start(), calls=%async_computation.3 | async-start | bytes 17039360 | tf_op jit(solution)/shard_map/all_gather | solution.py:36
  11.8 3.5 %copy-start.4 = (s32[384,1]{0,1:T(1,128)S(1)}, s32[384,1]{0,1:T(1,128)}, u32[]{:S(2)}) copy-start(s32[384,1]{0,1:T(1,128)} %param.13) | copy-start | bytes 4612
  11.9 5.3 %collective-permute-start.1 = (bf16[384,1024]{1,0:T(8,128)(2,1)S(1)}, bf16[384,1024]{1,0:T(8,128)(2,1)S(1)}, u32[]{:S(2)}, u32[]{:S(2)}) collective-permute-start(bf16[384,1024]{1,0:T(8,128)(2,1)S(1)} %get-tuple-element.10), channel_id=1, source_target_pairs={{0,4},{4,0},{1,5},{5,1},{2,6},{6,2},{3,7},{7,3},{8,12},{12,8},{9,1... | collective-permute-start | bytes 2359304 | tf_op jit(solution)/shard_map/ppermute | solution.py:55
  15.5 1.7 collective-permute-start
  21.2 80.1 %all-to-all-start = ((bf16[32,48,1024]{2,1,0:T(8,128)(2,1)}), bf16[32,48,1024]{2,1,0:T(8,128)(2,1)S(1)}, u32[]{:S(2)}, u32[]{:S(2)}) async-start(bf16[32,48,1024]{2,1,0:T(8,128)(2,1)} %bitcast.24), calls=%async_computation | async-start | bytes 6291456 | tf_op jit(solution)/shard_map/all_to_all | solution.py:57
  32.9 2.5 %collective-permute-start.2 = (bf16[1024,256]{1,0:T(8,128)(2,1)}, bf16[1024,256]{1,0:T(8,128)(2,1)}, u32[]{:S(2)}, u32[]{:S(2)}) collective-permute-start(bf16[1024,256]{1,0:T(8,128)(2,1)} %get-tuple-element.14), channel_id=1, source_target_pairs={{0,4},{4,0},{1,5},{5,1},{2,6},{6,2},{3,7},{7,3},{8,12},{12,8},{9,1... | collective-permute-start | bytes 1572872 | tf_op jit(solution)/shard_map/ppermute | solution.py:61
  104.8 4.4 %collective-permute-start.3 = (f32[768,256]{1,0:T(8,128)S(1)}, f32[768,256]{1,0:T(8,128)S(1)}, u32[]{:S(2)}, u32[]{:S(2)}) collective-permute-start(f32[768,256]{1,0:T(8,128)S(1)} %constant_dynamic-slice_fusion.3), channel_id=1, source_target_pairs={{0,4},{4,0},{1,5},{5,1},{2,6},{6,2},{3,7},{7,3},{8,12},{12,8},{9,1... | collective-permute-start | bytes 2359304 | tf_op jit(solution)/shard_map/ppermute | solution.py:76
  109.3 23.4 %copy-start.1 = (bf16[1,2,128,512]{3,2,1,0:T(8,128)(2,1)S(1)}, bf16[1,2,128,512]{3,2,1,0:T(8,128)(2,1)}, u32[]{:S(2)}) copy-start(bf16[1,2,128,512]{3,2,1,0:T(8,128)(2,1)} %param.12) | copy-start | bytes 786436
  109.3 7.7 %collective-permute-start.4 = (f32[192,256]{1,0:T(8,128)S(1)}, f32[192,256]{1,0:T(8,128)S(1)}, u32[]{:S(2)}, u32[]{:S(2)}) collective-permute-start(f32[192,256]{1,0:T(8,128)S(1)} %get-tuple-element.21), channel_id=1, source_target_pairs={{0,1},{1,2},{2,3},{3,0},{4,5},{5,6},{6,7},{7,4},{8,9},{9,10},{10,1... | collective-permute-start | bytes 589832 | tf_op jit(solution)/shard_map/ppermute | solution.py:13
  110.7 11.5 %collective-permute-start.5 = (f32[192,256]{1,0:T(8,128)S(1)}, f32[192,256]{1,0:T(8,128)S(1)}, u32[]{:S(2)}, u32[]{:S(2)}) collective-permute-start(f32[192,256]{1,0:T(8,128)S(1)} %get-tuple-element.23), channel_id=1, source_target_pairs={{0,2},{1,3},{2,0},{3,1},{4,6},{5,7},{6,4},{7,5},{8,10},{9,11},{10,... | collective-permute-start | bytes 589832 | tf_op jit(solution)/shard_map/ppermute | solution.py:13
  113.3 8.9 %collective-permute-start.6 = (f32[192,256]{1,0:T(8,128)S(1)}, f32[192,256]{1,0:T(8,128)S(1)}, u32[]{:S(2)}, u32[]{:S(2)}) collective-permute-start(f32[192,256]{1,0:T(8,128)S(1)} %get-tuple-element.22), channel_id=1, source_target_pairs={{0,3},{1,0},{2,1},{3,2},{4,7},{5,4},{6,5},{7,6},{8,11},{9,8},{10,9... | collective-permute-start | bytes 589832 | tf_op jit(solution)/shard_map/ppermute | solution.py:13
  122.3 5.2 %collective-permute-start.7 = (bf16[192,256]{1,0:T(8,128)(2,1)S(1)}, bf16[192,256]{1,0:T(8,128)(2,1)S(1)}, u32[]{:S(2)}, u32[]{:S(2)}) collective-permute-start(bf16[192,256]{1,0:T(8,128)(2,1)S(1)} %get-tuple-element.6), channel_id=1, source_target_pairs={{0,1},{1,2},{2,3},{3,0},{4,5},{5,6},{6,7},{7,4},{8,9},{9,10},{10,1... | collective-permute-start | bytes 294920 | tf_op jit(solution)/shard_map/ppermute | solution.py:13
  123.4 7.2 %collective-permute-start.8 = (bf16[192,256]{1,0:T(8,128)(2,1)S(1)}, bf16[192,256]{1,0:T(8,128)(2,1)S(1)}, u32[]{:S(2)}, u32[]{:S(2)}) collective-permute-start(bf16[192,256]{1,0:T(8,128)(2,1)S(1)} %get-tuple-element.6), channel_id=1, source_target_pairs={{0,2},{1,3},{2,0},{3,1},{4,6},{5,7},{6,4},{7,5},{8,10},{9,11},{10,... | collective-permute-start | bytes 294920 | tf_op jit(solution)/shard_map/ppermute | solution.py:13
  126.1 4.8 %collective-permute-start.9 = (bf16[192,256]{1,0:T(8,128)(2,1)S(1)}, bf16[192,256]{1,0:T(8,128)(2,1)S(1)}, u32[]{:S(2)}, u32[]{:S(2)}) collective-permute-start(bf16[192,256]{1,0:T(8,128)(2,1)S(1)} %get-tuple-element.6), channel_id=1, source_target_pairs={{0,3},{1,0},{2,1},{3,2},{4,7},{5,4},{6,5},{7,6},{8,11},{9,8},{10,9... | collective-permute-start | bytes 294920 | tf_op jit(solution)/shard_map/ppermute | solution.py:13
  131.0 3.0 %collective-permute-start.10 = (bf16[768,256]{1,0:T(8,128)(2,1)S(1)}, bf16[768,256]{1,0:T(8,128)(2,1)S(1)}, u32[]{:S(2)}, u32[]{:S(2)}) collective-permute-start(bf16[768,256]{1,0:T(8,128)(2,1)S(1)} %constant_dynamic-update-slice_fusion), channel_id=1, source_target_pairs={{0,4},{4,0},{1,5},{5,1},{2,6},{6,2},{3,7},{7,3},{8,12},{12,8},{9,1... | collective-permute-start | bytes 1179656 | tf_op jit(solution)/shard_map/ppermute | solution.py:92
  132.7 1.5 collective-permute-start.11
  200.1 7.7 %collective-permute-start.12 = (bf16[384,512]{1,0:T(8,128)(2,1)S(1)}, bf16[384,512]{1,0:T(8,128)(2,1)S(1)}, u32[]{:S(2)}, u32[]{:S(2)}) collective-permute-start(bf16[384,512]{1,0:T(8,128)(2,1)S(1)} %slice.84), channel_id=1, source_target_pairs={{0,4},{4,0},{1,5},{5,1},{2,6},{6,2},{3,7},{7,3},{8,12},{12,8},{9,1... | collective-permute-start | bytes 1179656 | tf_op jit(solution)/shard_map/ppermute | solution.py:107
  201.6 4.1 %collective-permute-start.13 = (f32[384]{0:T(512)S(1)}, f32[384]{0:T(512)S(1)}, u32[]{:S(2)}, u32[]{:S(2)}) collective-permute-start(f32[384]{0:T(512)S(1)} %get-tuple-element.7), channel_id=1, source_target_pairs={{0,1},{1,2},{2,3},{3,0},{4,5},{5,6},{6,7},{7,4},{8,9},{9,10},{10,1... | collective-permute-start | bytes 4616 | tf_op jit(solution)/shard_map/ppermute | solution.py:13
  202.2 4.0 %collective-permute-start.14 = (f32[384]{0:T(512)S(1)}, f32[384]{0:T(512)S(1)}, u32[]{:S(2)}, u32[]{:S(2)}) collective-permute-start(f32[384]{0:T(512)S(1)} %get-tuple-element.7), channel_id=1, source_target_pairs={{0,2},{1,3},{2,0},{3,1},{4,6},{5,7},{6,4},{7,5},{8,10},{9,11},{10,... | collective-permute-start | bytes 4616 | tf_op jit(solution)/shard_map/ppermute | solution.py:13
  204.9 2.8 %collective-permute-start.15 = (f32[384]{0:T(512)S(1)}, f32[384]{0:T(512)S(1)}, u32[]{:S(2)}, u32[]{:S(2)}) collective-permute-start(f32[384]{0:T(512)S(1)} %get-tuple-element.7), channel_id=1, source_target_pairs={{0,3},{1,0},{2,1},{3,2},{4,7},{5,4},{6,5},{7,6},{8,11},{9,8},{10,9... | collective-permute-start | bytes 4616 | tf_op jit(solution)/shard_map/ppermute | solution.py:13
Sparse Core Ops, SparseCore 0:
  10.4 72.0 all-gather.2
  85.3 130.6 all-gather.4

commit v2 on v1

v2 whole, which is shorter than its diff:
```python
import jax
import jax.numpy as jnp
from jax import lax
from jax.sharding import Mesh, PartitionSpec as P

EPSILON = 1e-06
ADAPTER_SCALE = 0.5
SWAP = [(0, 1), (1, 0)]
CHIP = ("z", "x")


def shift(array, distance, size):
    return lax.ppermute(array, "y", [(i, (i + distance) % size) for i in range(size)])


def dot(a, b):
    return jnp.dot(a, b, preferred_element_type=jnp.float32)


def cut_at(array, index, size, axis):
    return lax.dynamic_slice_in_dim(array, index * jnp.uint32(size), size, axis)


def body(tokens, scale, gate_matrix, up_matrix, down, up_factors, row_judges):
    f32, bf16 = jnp.float32, jnp.bfloat16
    rows, width = tokens.shape
    chips = lax.axis_size("z") * lax.axis_size("x")
    judges = 2 * chips
    cap = 2 * rows // judges
    ny = lax.axis_size("y")
    core = lax.axis_index("c")
    y, half_at = lax.axis_index("y").astype(jnp.uint32), core.astype(jnp.uint32)

    def ring(distance):
        return lax.rem(y + jnp.uint32(distance % ny), jnp.uint32(ny))

    half = width // 2
    span = gate_matrix.shape[1]
    cols = span // 2
    rank_width = down.shape[2] // 2

    def swap(array):
        return lax.ppermute(array, "c", SWAP)

    def by_core(own, other, at):
        return jnp.where(core == at, own, other)

    weights = lax.all_gather(jnp.concatenate([gate_matrix, up_matrix], axis=1), "z", axis=0)

    wide = tokens.astype(f32)
    squares = jnp.sum(wide * wide, axis=1)
    scaled = (wide * scale.astype(f32)).astype(bf16)
    block = gate_matrix.shape[0]
    blocks = width // block
    parity = [
        jnp.concatenate(
            [scaled[:, i * block : (i + 1) * block] for i in range(p, blocks, 2)], axis=1
        )
        for p in range(2)
    ]
    both = jnp.concatenate(
        [by_core(parity[0], parity[1], 0), swap(by_core(parity[0], parity[1], 1))], axis=0
    )

    labels = row_judges[:, 0]
    matches = (labels[:, None] == jnp.arange(judges, dtype=jnp.int32)[None, :]).astype(bf16)
    at = jnp.arange(rows, dtype=jnp.int32)
    before = dot((at[:, None] > at[None, :]).astype(bf16), matches)
    place = jnp.sum(before * matches.astype(f32), axis=1).astype(jnp.int32)
    count = chips * 2 * cap
    own_slot = (labels % 2) * count + (labels // 2) * (2 * cap) + core * cap + place
    slots = jnp.concatenate([own_slot, swap(own_slot)])
    slot_at = jnp.arange(count, dtype=jnp.int32)
    choose = [
        (slot_at[:, None] + b * count == slots[None, :]).astype(bf16) for b in range(2)
    ]

    down_pair = down[0].reshape(blocks // 2, 2, block, 2 * rank_width)
    down_parity = [down_pair[:, p].reshape(half, 2 * rank_width) for p in range(2)]
    down_own = by_core(down_parity[0], down_parity[1], 0)
    down_other = swap(by_core(down_parity[0], down_parity[1], 1))
    up_own = cut_at(up_factors[0], half_at, cols, 2)
    up_other = swap(cut_at(up_factors[0], 1 - half_at, cols, 2))

    def send_out(b):
        return dot(choose[b], both).astype(bf16).reshape(chips, 2 * cap, half)

    def exchange(array):
        return lax.all_to_all(array, CHIP, 0, 0, tiled=True)

    def process(b, arrived):
        partial = dot(arrived.reshape(count, half), by_core(down_own, down_other, b))
        mid = count // 2
        partial = cut_at(partial, half_at, mid, 0) + swap(cut_at(partial, 1 - half_at, mid, 0))
        piece = mid // ny
        total = cut_at(partial, y, piece, 0)
        for d in range(1, ny):
            total = total + shift(cut_at(partial, ring(d), piece, 0), d, ny)
        total = total.astype(bf16)
        code = jnp.zeros((mid, 2 * rank_width), bf16)
        code = lax.dynamic_update_slice_in_dim(code, total, y * jnp.uint32(piece), 0)
        for d in range(1, ny):
            code = lax.dynamic_update_slice_in_dim(
                code, shift(total, d, ny), ring(-d) * jnp.uint32(piece), 0
            )
        other = swap(code)
        codes = jnp.concatenate([by_core(code, other, 0), by_core(code, other, 1)], axis=0)
        factors = by_core(up_own, up_other, b)
        nothing = jnp.zeros_like(factors[0])
        factors = jnp.concatenate(
            [
                jnp.concatenate([factors[0], nothing], axis=1),
                jnp.concatenate([nothing, factors[1]], axis=1),
            ],
            axis=0,
        )
        deltas = dot(codes, factors).astype(bf16)
        return deltas.reshape(chips, 2 * cap, span)

    left, right = shift(both, 1, ny), shift(both, -1, ny)
    first = exchange(send_out(0))
    second, first, left, right, weights = lax.optimization_barrier(
        (send_out(1), first, left, right, weights)
    )
    second = exchange(second)
    weights = lax.all_gather(weights, "x", axis=1, tiled=True)
    weights = weights.reshape(ny, width // 2, 2 * span)
    far = [shift(left[:rows], 1, ny), shift(right[rows:], -1, ny)]
    deltas = process(0, first)
    second, deltas, far = lax.optimization_barrier((second, deltas, far))
    returned = exchange(deltas)
    returned, deltas = lax.optimization_barrier((returned, process(1, second)))
    back = [returned, exchange(deltas)]
    far = jnp.concatenate(far, axis=0)
    by_row = sum(
        lax.dot_general(
            choose[b],
            back[b].reshape(count, span),
            (((0,), (0,)), ((), ())),
            preferred_element_type=f32,
        )
        for b in range(2)
    ).astype(bf16)
    here = by_row[:rows]
    there = swap(by_row[rows:])
    low = by_core(here, there, 0).astype(f32)
    high = by_core(here, there, 1).astype(f32)

    plain = None
    for array, d in ((both, 0), (left, -1), (right, 1), (far, 2)):
        term = dot(array, lax.dynamic_index_in_dim(weights, ring(d), 0, keepdims=False))
        plain = term if plain is None else plain + term
    plain = plain[:rows] + swap(plain[rows:])

    sums = squares
    for d in range(1, ny):
        sums = sums + shift(squares, d, ny)
    factor = lax.rsqrt(sums / (width * ny) + EPSILON)[:, None]

    gate_add = jnp.concatenate([low[:, :cols], high[:, :cols]], axis=1)
    up_add = jnp.concatenate([low[:, cols:], high[:, cols:]], axis=1)
    gate = (plain[:, :span] + ADAPTER_SCALE * gate_add) * factor
    up = (plain[:, span:] + ADAPTER_SCALE * up_add) * factor
    return (jax.nn.silu(gate) * up).astype(bf16)


def solution(mesh):
    cut = Mesh(mesh.devices.reshape(8, 4, 2, 4), ("z", "x", "c", "y"))
    dp = ("z", "x", "c")
    placed = (
        P(dp, "y"),
        P("y"),
        P(dp, "y"),
        P(dp, "y"),
        P(dp, "y", None),
        P(dp, None, None, "y"),
        P(dp, None),
    )
    return jax.shard_map(body, mesh=cut, in_specs=placed, out_specs=P(dp, "y"), check_vma=False)
```

time: 236 us -> 237 us (level)
  blocking collectives: 62.2 us -> 0 us
  starting transfers between devices: 32.3 us -> 69.2 us
  waiting for transfers between devices: 95.1 us -> 109 us
  local copies, waits for them, and re-layouts: 3.54 us -> 8.59 us
  other arithmetic: 7.37 us -> 11 us
    all_to_all x1 -> x4, waiting for transfers between devices: 65.9 us -> 1.91 us  [exchange(): return lax.all_to_all(array, CHIP, 0, 0, tiled=True)]
    all_to_all x1 -> x0, blocking collectives: 62.2 us -> none  [body(): lax.all_to_all(deltas.reshape(chips, 4 * cap, span), CHIP, 0, 0, tiled=True)]
    ppermute x9 -> x19, waiting for transfers between devices: 15 us -> 62.5 us  [shift(): lax.ppermute(array, 'y', [(i, (i + distance) % size) for i in range(size)])]
    all_gather x2, waiting for transfers between devices: 7.89 us -> 40.7 us  [the longest x1 23.9 us: body(): weights = lax.all_gather(weights, 'x', axis=1, tiled=True)]
    all_to_all x1 -> x4, starting transfers between devices: 9.3 us -> 33 us  [exchange(): return lax.all_to_all(array, CHIP, 0, 0, tiled=True)]
    ppermute x9 -> x19, starting transfers between devices: 12.7 us -> 21.7 us  [shift(): lax.ppermute(array, 'y', [(i, (i + distance) % size) for i in range(size)])]
    ppermute x7 -> x10, starting transfers between devices: 10.3 us -> 14.5 us  [swap(): return lax.ppermute(array, 'c', SWAP)]
    unnamed x10 -> x43, local copies, waits for them, and re-layouts: 0.66 us -> 4.48 us
  transfers between devices with their start and end apart: 19 -> 35, of which waited for: 15 -> 20; matrix products, arithmetic and copies ran while one was open for 6% -> 14% of each run, Pallas kernels for 0% -> 0%
where the time goes in v2:
time: 237 us; the launch traced here: 236 us
  waiting for transfers between devices  109 us (46%)
  starting transfers between devices  69.2 us (29%)
  matrix products  23.8 us (10%)
  between operations  13.9 us (6%)
  other arithmetic  11 us (5%)
  local copies, waits for them, and re-layouts  8.59 us (4%)
    ppermute x19, waiting for transfers between devices, shift(): lax.ppermute(array, 'y', [(i, (i + distance) % size) for i in range(size)])  62.5 us
    all_to_all x4, starting transfers between devices, exchange(): return lax.all_to_all(array, CHIP, 0, 0, tiled=True)  33 us
    all_gather x1, waiting for transfers between devices, body(): weights = lax.all_gather(weights, 'x', axis=1, tiled=True)  23.9 us
    ppermute x19, starting transfers between devices, shift(): lax.ppermute(array, 'y', [(i, (i + distance) % size) for i in range(size)])  21.7 us
    dot_general x11, matrix products, dot(): return jnp.dot(a, b, preferred_element_type=jnp.float32)  20.7 us
    all_gather x1, waiting for transfers between devices, body(): lax.all_gather(jnp.concatenate([gate_matrix, up_matrix], axis=1), 'z', ax...  16.7 us
    ppermute x10, starting transfers between devices, swap(): return lax.ppermute(array, 'c', SWAP)  14.5 us
  transfers between devices with their start and end apart: 35, of which 20 were waited for; matrix products, arithmetic and copies ran while one was open for 14% of the time, Pallas kernels for 0%

profile of v2, /device:TPU:1, one launch (start us, length us, event | category | flops | bytes accessed | tf_op | source)
XLA Modules:
  0.0 236.0 jit_solution(17774046162600281096)
XLA Ops:
  7.2 2.0 fusion.1
  10.0 3.3 %collective-permute-start = (bf16[384,1024]{1,0:T(8,128)(2,1)S(1)}, bf16[384,1024]{1,0:T(8,128)(2,1)S(1)}, u32[]{:S(2)}, u32[]{:S(2)}) collective-permute-start(bf16[384,1024]{1,0:T(8,128)(2,1)S(1)} %get-tuple-element.34), channel_id=1, source_target_pairs={{0,4},{4,0},{1,5},{5,1},{2,6},{6,2},{3,7},{7,3},{8,12},{12,8},{9,1... | collective-permute-start | bytes 2359304 | tf_op jit(solution)/shard_map/ppermute | solution.py:43
  16.0 2.6 %fusion.20 = bf16[768,1024]{1,0:T(8,128)(2,1)} fusion(s32[768]{0:T(1024)S(1)} %pad_add_fusion, bf16[384,1024]{1,0:T(8,128)(2,1)S(1)} %collective-permute-done, bf16[384,1024]{1,0:T(8,128)(2,1)S(1)} %get-tuple-element.33), kind=kOutput, calls=%fused_computation.24 | convolution fusion | flops 1212481536 | bytes 3148800 | tf_op jit(solution)/shard_map/dot_general | solution.py:17
  18.6 9.3 %all-to-all-start = ((bf16[32,24,1024]{2,1,0:T(8,128)(2,1)}), bf16[32,24,1024]{2,1,0:T(8,128)(2,1)S(1)}, u32[]{:S(2)}, u32[]{:S(2)}) async-start(bf16[32,24,1024]{2,1,0:T(8,128)(2,1)} %bitcast.54), calls=%async_computation | async-start | bytes 3145728 | tf_op jit(solution)/shard_map/all_to_all | solution.py:89
  28.0 2.8 %collective-permute-start.3 = (bf16[768,1024]{1,0:T(8,128)(2,1)S(1)}, bf16[768,1024]{1,0:T(8,128)(2,1)S(1)}, u32[]{:S(2)}, u32[]{:S(2)}) collective-permute-start(bf16[768,1024]{1,0:T(8,128)(2,1)S(1)} %pad_maximum_fusion), channel_id=1, source_target_pairs={{0,3},{1,0},{2,1},{3,2},{4,7},{5,4},{6,5},{7,6},{8,11},{9,8},{10,9... | collective-permute-start | bytes 4718600 | tf_op jit(solution)/shard_map/ppermute | solution.py:13
  30.9 2.6 %fusion.21 = bf16[768,1024]{1,0:T(8,128)(2,1)} fusion(s32[768]{0:T(1024)S(1)} %pad_add_fusion, s32[768]{0:T(1024)S(1)} %iota_add_fusion, bf16[384,1024]{1,0:T(8,128)(2,1)S(1)} %collective-permute-done, bf16[384,1024]{1,0:T(8,128)(2,1)S(1)} %get-tuple-element.33), kind=kOutput, calls=%fused_computation.25 | convolution fusion | flops 1212481536 | bytes 3151872 | tf_op jit(solution)/shard_map/dot_general | solution.py:17
  33.5 30.5 %collective-permute-done.3 = bf16[768,1024]{1,0:T(8,128)(2,1)S(1)} collective-permute-done((bf16[768,1024]{1,0:T(8,128)(2,1)S(1)}, bf16[768,1024]{1,0:T(8,128)(2,1)S(1)}, u32[]{:S(2)}, u32[]{:S(2)}) %collective-permute-start.3) | collective-permute-done | bytes 1572896 | tf_op jit(solution)/shard_map/ppermute | solution.py:13
  65.1 2.0 collective-permute-done.2
  67.2 16.7 %all-gather.6.cloned.1.call-done = bf16[1024,1024]{1,0:T(8,128)(2,1)} async-done(((bf16[128,1024]{1,0:T(8,128)(2,1)}), bf16[1024,1024]{1,0:T(8,128)(2,1)}) %all-gather.6.cloned.1.call-update) | async-done | bytes 2097168 | tf_op jit(solution)/shard_map/all_gather | solution.py:48
  85.0 1.8 collective-permute-start.4
  86.8 6.8 %all-to-all-start.1 = ((bf16[32,24,1024]{2,1,0:T(8,128)(2,1)}), bf16[32,24,1024]{2,1,0:T(8,128)(2,1)S(1)}, u32[]{:S(2)}, u32[]{:S(2)}) async-start(bf16[32,24,1024]{2,1,0:T(8,128)(2,1)} %bitcast.53), calls=%async_computation.1 | async-start | bytes 3145728 | tf_op jit(solution)/shard_map/all_to_all | solution.py:89
  93.6 2.1 bitcast_select_fusion
  105.7 2.6 %collective-permute-done.7 = f32[96,256]{1,0:T(8,128)S(1)} collective-permute-done((f32[96,256]{1,0:T(8,128)S(1)}, f32[96,256]{1,0:T(8,128)S(1)}, u32[]{:S(2)}, u32[]{:S(2)}) %collective-permute-start.7) | collective-permute-done | bytes 98336 | tf_op jit(solution)/shard_map/ppermute | solution.py:13
  111.5 2.0 collective-permute-start.15
  116.3 15.3 %collective-permute-done.10 = bf16[96,256]{1,0:T(8,128)(2,1)S(1)} collective-permute-done((bf16[96,256]{1,0:T(8,128)(2,1)S(1)}, bf16[96,256]{1,0:T(8,128)(2,1)S(1)}, u32[]{:S(2)}, u32[]{:S(2)}) %collective-permute-start.10) | collective-permute-done | bytes 49184 | tf_op jit(solution)/shard_map/ppermute | solution.py:13
  131.6 3.3 %collective-permute-start.12 = (bf16[384,256]{1,0:T(8,128)(2,1)S(1)}, bf16[384,256]{1,0:T(8,128)(2,1)S(1)}, u32[]{:S(2)}, u32[]{:S(2)}) collective-permute-start(bf16[384,256]{1,0:T(8,128)(2,1)S(1)} %constant_dynamic-update-slice_fusion.4), channel_id=1, source_target_pairs={{0,4},{4,0},{1,5},{5,1},{2,6},{6,2},{3,7},{7,3},{8,12},{12,8},{9,1... | collective-permute-start | bytes 589832 | tf_op jit(solution)/shard_map/ppermute | solution.py:43
  139.3 9.5 %all-to-all-start.2 = ((bf16[32,24,512]{2,1,0:T(8,128)(2,1)}), bf16[32,24,512]{2,1,0:T(8,128)(2,1)S(1)}, u32[]{:S(2)}, u32[]{:S(2)}) async-start(bf16[32,24,512]{2,1,0:T(8,128)(2,1)} %bitcast.57), calls=%async_computation.2 | async-start | bytes 1572864 | tf_op jit(solution)/shard_map/all_to_all | solution.py:89
  149.0 2.7 %collective-permute-start.20 = (f32[96,256]{1,0:T(8,128)S(1)}, f32[96,256]{1,0:T(8,128)S(1)}, u32[]{:S(2)}, u32[]{:S(2)}) collective-permute-start(f32[96,256]{1,0:T(8,128)S(1)} %get-tuple-element.66), channel_id=1, source_target_pairs={{0,3},{1,0},{2,1},{3,2},{4,7},{5,4},{6,5},{7,6},{8,11},{9,8},{10,9... | collective-permute-start | bytes 294920 | tf_op jit(solution)/shard_map/ppermute | solution.py:13
  151.7 2.5 %collective-permute-done.18 = f32[96,256]{1,0:T(8,128)S(1)} collective-permute-done((f32[96,256]{1,0:T(8,128)S(1)}, f32[96,256]{1,0:T(8,128)S(1)}, u32[]{:S(2)}, u32[]{:S(2)}) %collective-permute-start.18) | collective-permute-done | bytes 98336 | tf_op jit(solution)/shard_map/ppermute | solution.py:13
  154.3 2.6 %collective-permute-done.19 = f32[96,256]{1,0:T(8,128)S(1)} collective-permute-done((f32[96,256]{1,0:T(8,128)S(1)}, f32[96,256]{1,0:T(8,128)S(1)}, u32[]{:S(2)}, u32[]{:S(2)}) %collective-permute-start.19) | collective-permute-done | bytes 98336 | tf_op jit(solution)/shard_map/ppermute | solution.py:13
  157.1 3.3 %collective-permute-start.22 = (bf16[96,256]{1,0:T(8,128)(2,1)S(1)}, bf16[96,256]{1,0:T(8,128)(2,1)S(1)}, u32[]{:S(2)}, u32[]{:S(2)}) collective-permute-start(bf16[96,256]{1,0:T(8,128)(2,1)S(1)} %get-tuple-element.28), channel_id=1, source_target_pairs={{0,2},{1,3},{2,0},{3,1},{4,6},{5,7},{6,4},{7,5},{8,10},{9,11},{10,... | collective-permute-start | bytes 147464 | tf_op jit(solution)/shard_map/ppermute | solution.py:13
  163.7 2.4 %collective-permute-start.24 = (bf16[384,256]{1,0:T(8,128)(2,1)S(1)}, bf16[384,256]{1,0:T(8,128)(2,1)S(1)}, u32[]{:S(2)}, u32[]{:S(2)}) collective-permute-start(bf16[384,256]{1,0:T(8,128)(2,1)S(1)} %constant_dynamic-update-slice_fusion), channel_id=1, source_target_pairs={{0,4},{4,0},{1,5},{5,1},{2,6},{6,2},{3,7},{7,3},{8,12},{12,8},{9,1... | collective-permute-start | bytes 589832 | tf_op jit(solution)/shard_map/ppermute | solution.py:43
  168.5 1.9 all-to-all-done.2
  170.4 7.4 %all-to-all-start.3 = ((bf16[32,24,512]{2,1,0:T(8,128)(2,1)}), bf16[32,24,512]{2,1,0:T(8,128)(2,1)}, u32[]{:S(2)}, u32[]{:S(2)}) async-start(bf16[32,24,512]{2,1,0:T(8,128)(2,1)} %bitcast.20), calls=%async_computation.3 | async-start | bytes 1572864 | tf_op jit(solution)/shard_map/all_to_all | solution.py:89
  177.9 23.9 %all-gather.4.cloned.1.call-done = bf16[8,512,1024]{2,1,0:T(8,128)(2,1)} async-done(((bf16[8,128,1024]{2,1,0:T(8,128)(2,1)}), bf16[8,512,1024]{2,1,0:T(8,128)(2,1)}) %all-gather.4.cloned.1.call-update) | async-done | bytes 8388624 | tf_op jit(solution)/shard_map/all_gather | solution.py:126
  201.8 3.5 %fusion.14 = f32[768,1024]{1,0:T(8,128)S(1)} fusion(bf16[4,1024,1024]{2,1,0:T(8,128)(2,1)} %bitcast.58, u32[]{:T(128)S(6)} %rem.56, bf16[384,1024]{1,0:T(8,128)(2,1)S(1)} %copy-done.8, bf16[384,1024]{1,0:T(8,128)(2,1)S(1)} %copy-done.1), kind=kOutput, calls=%fused_computation.18 | convolution fusion | flops 1613758464 | bytes 6815748 | tf_op jit(solution)/shard_map/dot_general | solution.py:17
  206.3 1.8 fusion.10
  208.2 3.3 %fusion.12 = f32[768,1024]{1,0:T(8,128)S(1)} fusion(bf16[768,1024]{1,0:T(8,128)(2,1)} %collective-permute-done.2, bf16[4,1024,1024]{2,1,0:T(8,128)(2,1)S(1)} %bitcast.60, u32[]{:T(128)S(6)} %rem.57), kind=kOutput, calls=%fused_computation.16 | convolution fusion | flops 1610612736 | bytes 6815748 | tf_op jit(solution)/shard_map/dot_general | solution.py:17
  211.5 3.0 %add_add_fusion = f32[768,1024]{1,0:T(8,128)S(1)} fusion(f32[768,1024]{1,0:T(8,128)S(1)} %fusion.10, f32[768,1024]{1,0:T(8,128)S(1)} %fusion.14, f32[768,1024]{1,0:T(8,128)S(1)} %fusion.12, bf16[4,1024,1024]{2,1,0:T(8,128)(2,1)S(1)} %bitcast.61, u32[]{:T(128)S(6)} %rem.59, bf16[384,1024]{1,0:T(8,128)(2,1)S(1)} %copy-done.17, ...), kind=kOutput, calls=%fused_computation.4 | convolution fusion | flops 1616117760 | bytes 16252932 | tf_op jit(solution)/shard_map/dot_general | solution.py:17
  216.3 2.2 fusion.2
  219.5 2.3 collective-permute-start.28
  222.9 2.8 %collective-permute-done.27 = f32[384]{0:T(512)S(1)} collective-permute-done((f32[384]{0:T(512)S(1)}, f32[384]{0:T(512)S(1)}, u32[]{:S(2)}, u32[]{:S(2)}) %collective-permute-start.27) | collective-permute-done | bytes 1568 | tf_op jit(solution)/shard_map/ppermute | solution.py:13
  (139 shorter events, 41.2 us)
Async XLA Ops:
  6.5 77.4 %all-gather.6.cloned.1.call-start = ((), (), s32[]{:S(2)}) async-start(), calls=%async_computation.5 | async-start | bytes 2359296 | tf_op jit(solution)/shard_map/all_gather | solution.py:48
  10.0 6.0 %collective-permute-start = (bf16[384,1024]{1,0:T(8,128)(2,1)S(1)}, bf16[384,1024]{1,0:T(8,128)(2,1)S(1)}, u32[]{:S(2)}, u32[]{:S(2)}) collective-permute-start(bf16[384,1024]{1,0:T(8,128)(2,1)S(1)} %get-tuple-element.34), channel_id=1, source_target_pairs={{0,4},{4,0},{1,5},{5,1},{2,6},{6,2},{3,7},{7,3},{8,12},{12,8},{9,1... | collective-permute-start | bytes 2359304 | tf_op jit(solution)/shard_map/ppermute | solution.py:43
  18.6 65.3 %all-to-all-start = ((bf16[32,24,1024]{2,1,0:T(8,128)(2,1)}), bf16[32,24,1024]{2,1,0:T(8,128)(2,1)S(1)}, u32[]{:S(2)}, u32[]{:S(2)}) async-start(bf16[32,24,1024]{2,1,0:T(8,128)(2,1)} %bitcast.54), calls=%async_computation | async-start | bytes 3145728 | tf_op jit(solution)/shard_map/all_to_all | solution.py:89
  27.9 173.9 %all-gather.4.cloned.1.call-start = ((), (), s32[]{:S(2)}) async-start(), calls=%async_computation.4 | async-start | bytes 10485760 | tf_op jit(solution)/shard_map/all_gather | solution.py:126
  28.0 35.9 %collective-permute-start.3 = (bf16[768,1024]{1,0:T(8,128)(2,1)S(1)}, bf16[768,1024]{1,0:T(8,128)(2,1)S(1)}, u32[]{:S(2)}, u32[]{:S(2)}) collective-permute-start(bf16[768,1024]{1,0:T(8,128)(2,1)S(1)} %pad_maximum_fusion), channel_id=1, source_target_pairs={{0,3},{1,0},{2,1},{3,2},{4,7},{5,4},{6,5},{7,6},{8,11},{9,8},{10,9... | collective-permute-start | bytes 4718600 | tf_op jit(solution)/shard_map/ppermute | solution.py:13
  30.9 36.3 %collective-permute-start.2 = (bf16[768,1024]{1,0:T(8,128)(2,1)S(1)}, bf16[768,1024]{1,0:T(8,128)(2,1)}, u32[]{:S(2)}, u32[]{:S(2)}) collective-permute-start(bf16[768,1024]{1,0:T(8,128)(2,1)S(1)} %pad_maximum_fusion), channel_id=1, source_target_pairs={{0,1},{1,2},{2,3},{3,0},{4,5},{5,6},{6,7},{7,4},{8,9},{9,10},{10,1... | collective-permute-start | bytes 4718600 | tf_op jit(solution)/shard_map/ppermute | solution.py:13
  85.0 8.6 %collective-permute-start.4 = (bf16[1024,256]{1,0:T(8,128)(2,1)}, bf16[1024,256]{1,0:T(8,128)(2,1)}, u32[]{:S(2)}, u32[]{:S(2)}) collective-permute-start(bf16[1024,256]{1,0:T(8,128)(2,1)} %bitcast.10), channel_id=1, source_target_pairs={{0,4},{4,0},{1,5},{5,1},{2,6},{6,2},{3,7},{7,3},{8,12},{12,8},{9,1... | collective-permute-start | bytes 1572872 | tf_op jit(solution)/shard_map/ppermute | solution.py:43
  86.8 51.4 %all-to-all-start.1 = ((bf16[32,24,1024]{2,1,0:T(8,128)(2,1)}), bf16[32,24,1024]{2,1,0:T(8,128)(2,1)S(1)}, u32[]{:S(2)}, u32[]{:S(2)}) async-start(bf16[32,24,1024]{2,1,0:T(8,128)(2,1)} %bitcast.53), calls=%async_computation.1 | async-start | bytes 3145728 | tf_op jit(solution)/shard_map/all_to_all | solution.py:89
  100.2 5.5 %collective-permute-start.6 = (f32[96,256]{1,0:T(8,128)S(1)}, f32[96,256]{1,0:T(8,128)S(1)}, u32[]{:S(2)}, u32[]{:S(2)}) collective-permute-start(f32[96,256]{1,0:T(8,128)S(1)} %get-tuple-element.70), channel_id=1, source_target_pairs={{0,1},{1,2},{2,3},{3,0},{4,5},{5,6},{6,7},{7,4},{8,9},{9,10},{10,1... | collective-permute-start | bytes 294920 | tf_op jit(solution)/shard_map/ppermute | solution.py:13
  101.3 4.4 %collective-permute-start.8 = (f32[96,256]{1,0:T(8,128)S(1)}, f32[96,256]{1,0:T(8,128)S(1)}, u32[]{:S(2)}, u32[]{:S(2)}) collective-permute-start(f32[96,256]{1,0:T(8,128)S(1)} %get-tuple-element.71), channel_id=1, source_target_pairs={{0,3},{1,0},{2,1},{3,2},{4,7},{5,4},{6,5},{7,6},{8,11},{9,8},{10,9... | collective-permute-start | bytes 294920 | tf_op jit(solution)/shard_map/ppermute | solution.py:13
  103.0 5.3 %collective-permute-start.7 = (f32[96,256]{1,0:T(8,128)S(1)}, f32[96,256]{1,0:T(8,128)S(1)}, u32[]{:S(2)}, u32[]{:S(2)}) collective-permute-start(f32[96,256]{1,0:T(8,128)S(1)} %get-tuple-element.72), channel_id=1, source_target_pairs={{0,2},{1,3},{2,0},{3,1},{4,6},{5,7},{6,4},{7,5},{8,10},{9,11},{10,... | collective-permute-start | bytes 294920 | tf_op jit(solution)/shard_map/ppermute | solution.py:13
  103.9 5.2 %collective-permute-start.13 = (bf16[2,128,256]{2,1,0:T(8,128)(2,1)S(1)}, bf16[2,128,256]{2,1,0:T(8,128)(2,1)S(1)}, u32[]{:S(2)}, u32[]{:S(2)}) collective-permute-start(bf16[2,128,256]{2,1,0:T(8,128)(2,1)S(1)} %dynamic-slice_bitcast_fusion), channel_id=1, source_target_pairs={{0,4},{4,0},{1,5},{5,1},{2,6},{6,2},{3,7},{7,3},{8,12},{12,8},{9,1... | collective-permute-start | bytes 393224 | tf_op jit(solution)/shard_map/ppermute | solution.py:43
  108.3 8.0 %collective-permute-start.9 = (bf16[96,256]{1,0:T(8,128)(2,1)S(1)}, bf16[96,256]{1,0:T(8,128)(2,1)S(1)}, u32[]{:S(2)}, u32[]{:S(2)}) collective-permute-start(bf16[96,256]{1,0:T(8,128)(2,1)S(1)} %get-tuple-element.30), channel_id=1, source_target_pairs={{0,1},{1,2},{2,3},{3,0},{4,5},{5,6},{6,7},{7,4},{8,9},{9,10},{10,1... | collective-permute-start | bytes 147464 | tf_op jit(solution)/shard_map/ppermute | solution.py:13
  111.5 25.8 %collective-permute-start.15 = (bf16[384,1024]{1,0:T(8,128)(2,1)S(1)}, bf16[384,1024]{1,0:T(8,128)(2,1)S(1)}, u32[]{:S(2)}, u32[]{:S(2)}) collective-permute-start(bf16[384,1024]{1,0:T(8,128)(2,1)S(1)} %slice.123), channel_id=1, source_target_pairs={{0,3},{1,0},{2,1},{3,2},{4,7},{5,4},{6,5},{7,6},{8,11},{9,8},{10,9... | collective-permute-start | bytes 2359304 | tf_op jit(solution)/shard_map/ppermute | solution.py:13
  113.6 24.6 %collective-permute-start.14 = (bf16[384,1024]{1,0:T(8,128)(2,1)S(1)}, bf16[384,1024]{1,0:T(8,128)(2,1)}, u32[]{:S(2)}, u32[]{:S(2)}) collective-permute-start(bf16[384,1024]{1,0:T(8,128)(2,1)S(1)} %slice.122), channel_id=1, source_target_pairs={{0,1},{1,2},{2,3},{3,0},{4,5},{5,6},{6,7},{7,4},{8,9},{9,10},{10,1... | collective-permute-start | bytes 2359304 | tf_op jit(solution)/shard_map/ppermute | solution.py:13
  113.6 18.0 %collective-permute-start.10 = (bf16[96,256]{1,0:T(8,128)(2,1)S(1)}, bf16[96,256]{1,0:T(8,128)(2,1)S(1)}, u32[]{:S(2)}, u32[]{:S(2)}) collective-permute-start(bf16[96,256]{1,0:T(8,128)(2,1)S(1)} %get-tuple-element.30), channel_id=1, source_target_pairs={{0,2},{1,3},{2,0},{3,1},{4,6},{5,7},{6,4},{7,5},{8,10},{9,11},{10,... | collective-permute-start | bytes 147464 | tf_op jit(solution)/shard_map/ppermute | solution.py:13
  115.2 16.4 %collective-permute-start.11 = (bf16[96,256]{1,0:T(8,128)(2,1)S(1)}, bf16[96,256]{1,0:T(8,128)(2,1)S(1)}, u32[]{:S(2)}, u32[]{:S(2)}) collective-permute-start(bf16[96,256]{1,0:T(8,128)(2,1)S(1)} %get-tuple-element.30), channel_id=1, source_target_pairs={{0,3},{1,0},{2,1},{3,2},{4,7},{5,4},{6,5},{7,6},{8,11},{9,8},{10,9... | collective-permute-start | bytes 147464 | tf_op jit(solution)/shard_map/ppermute | solution.py:13
  131.6 4.4 %collective-permute-start.12 = (bf16[384,256]{1,0:T(8,128)(2,1)S(1)}, bf16[384,256]{1,0:T(8,128)(2,1)S(1)}, u32[]{:S(2)}, u32[]{:S(2)}) collective-permute-start(bf16[384,256]{1,0:T(8,128)(2,1)S(1)} %constant_dynamic-update-slice_fusion.4), channel_id=1, source_target_pairs={{0,4},{4,0},{1,5},{5,1},{2,6},{6,2},{3,7},{7,3},{8,12},{12,8},{9,1... | collective-permute-start | bytes 589832 | tf_op jit(solution)/shard_map/ppermute | solution.py:43
  138.8 10.0 %collective-permute-start.17 = (f32[384,256]{1,0:T(8,128)S(1)}, f32[384,256]{1,0:T(8,128)S(1)}, u32[]{:S(2)}, u32[]{:S(2)}) collective-permute-start(f32[384,256]{1,0:T(8,128)S(1)} %constant_dynamic-slice_fusion.3), channel_id=1, source_target_pairs={{0,4},{4,0},{1,5},{5,1},{2,6},{6,2},{3,7},{7,3},{8,12},{12,8},{9,1... | collective-permute-start | bytes 1179656 | tf_op jit(solution)/shard_map/ppermute | solution.py:43
  139.3 31.1 %all-to-all-start.2 = ((bf16[32,24,512]{2,1,0:T(8,128)(2,1)}), bf16[32,24,512]{2,1,0:T(8,128)(2,1)S(1)}, u32[]{:S(2)}, u32[]{:S(2)}) async-start(bf16[32,24,512]{2,1,0:T(8,128)(2,1)} %bitcast.57), calls=%async_computation.2 | async-start | bytes 1572864 | tf_op jit(solution)/shard_map/all_to_all | solution.py:89
  148.9 5.3 %collective-permute-start.18 = (f32[96,256]{1,0:T(8,128)S(1)}, f32[96,256]{1,0:T(8,128)S(1)}, u32[]{:S(2)}, u32[]{:S(2)}) collective-permute-start(f32[96,256]{1,0:T(8,128)S(1)} %get-tuple-element.65), channel_id=1, source_target_pairs={{0,1},{1,2},{2,3},{3,0},{4,5},{5,6},{6,7},{7,4},{8,9},{9,10},{10,1... | collective-permute-start | bytes 294920 | tf_op jit(solution)/shard_map/ppermute | solution.py:13
  149.0 5.4 %collective-permute-start.20 = (f32[96,256]{1,0:T(8,128)S(1)}, f32[96,256]{1,0:T(8,128)S(1)}, u32[]{:S(2)}, u32[]{:S(2)}) collective-permute-start(f32[96,256]{1,0:T(8,128)S(1)} %get-tuple-element.66), channel_id=1, source_target_pairs={{0,3},{1,0},{2,1},{3,2},{4,7},{5,4},{6,5},{7,6},{8,11},{9,8},{10,9... | collective-permute-start | bytes 294920 | tf_op jit(solution)/shard_map/ppermute | solution.py:13
  151.6 5.3 %collective-permute-start.19 = (f32[96,256]{1,0:T(8,128)S(1)}, f32[96,256]{1,0:T(8,128)S(1)}, u32[]{:S(2)}, u32[]{:S(2)}) collective-permute-start(f32[96,256]{1,0:T(8,128)S(1)} %get-tuple-element.67), channel_id=1, source_target_pairs={{0,2},{1,3},{2,0},{3,1},{4,6},{5,7},{6,4},{7,5},{8,10},{9,11},{10,... | collective-permute-start | bytes 294920 | tf_op jit(solution)/shard_map/ppermute | solution.py:13
  157.0 4.6 %collective-permute-start.21 = (bf16[96,256]{1,0:T(8,128)(2,1)S(1)}, bf16[96,256]{1,0:T(8,128)(2,1)S(1)}, u32[]{:S(2)}, u32[]{:S(2)}) collective-permute-start(bf16[96,256]{1,0:T(8,128)(2,1)S(1)} %get-tuple-element.28), channel_id=1, source_target_pairs={{0,1},{1,2},{2,3},{3,0},{4,5},{5,6},{6,7},{7,4},{8,9},{9,10},{10,1... | collective-permute-start | bytes 147464 | tf_op jit(solution)/shard_map/ppermute | solution.py:13
  157.1 5.6 %collective-permute-start.22 = (bf16[96,256]{1,0:T(8,128)(2,1)S(1)}, bf16[96,256]{1,0:T(8,128)(2,1)S(1)}, u32[]{:S(2)}, u32[]{:S(2)}) collective-permute-start(bf16[96,256]{1,0:T(8,128)(2,1)S(1)} %get-tuple-element.28), channel_id=1, source_target_pairs={{0,2},{1,3},{2,0},{3,1},{4,6},{5,7},{6,4},{7,5},{8,10},{9,11},{10,... | collective-permute-start | bytes 147464 | tf_op jit(solution)/shard_map/ppermute | solution.py:13
  163.7 3.5 %collective-permute-start.24 = (bf16[384,256]{1,0:T(8,128)(2,1)S(1)}, bf16[384,256]{1,0:T(8,128)(2,1)S(1)}, u32[]{:S(2)}, u32[]{:S(2)}) collective-permute-start(bf16[384,256]{1,0:T(8,128)(2,1)S(1)} %constant_dynamic-update-slice_fusion), channel_id=1, source_target_pairs={{0,4},{4,0},{1,5},{5,1},{2,6},{6,2},{3,7},{7,3},{8,12},{12,8},{9,1... | collective-permute-start | bytes 589832 | tf_op jit(solution)/shard_map/ppermute | solution.py:43
  170.4 45.9 %all-to-all-start.3 = ((bf16[32,24,512]{2,1,0:T(8,128)(2,1)}), bf16[32,24,512]{2,1,0:T(8,128)(2,1)}, u32[]{:S(2)}, u32[]{:S(2)}) async-start(bf16[32,24,512]{2,1,0:T(8,128)(2,1)} %bitcast.20), calls=%async_computation.3 | async-start | bytes 1572864 | tf_op jit(solution)/shard_map/all_to_all | solution.py:89
  215.8 10.6 %collective-permute-start.16 = (f32[384,1024]{1,0:T(8,128)}, f32[384,1024]{1,0:T(8,128)}, u32[]{:S(2)}, u32[]{:S(2)}) collective-permute-start(f32[384,1024]{1,0:T(8,128)} %slice.157), channel_id=1, source_target_pairs={{0,4},{4,0},{1,5},{5,1},{2,6},{6,2},{3,7},{7,3},{8,12},{12,8},{9,1... | collective-permute-start | bytes 4718600 | tf_op jit(solution)/shard_map/ppermute | solution.py:43
  219.4 6.7 %collective-permute-start.25 = (bf16[384,512]{1,0:T(8,128)(2,1)S(1)}, bf16[384,512]{1,0:T(8,128)(2,1)S(1)}, u32[]{:S(2)}, u32[]{:S(2)}) collective-permute-start(bf16[384,512]{1,0:T(8,128)(2,1)S(1)} %slice.162), channel_id=1, source_target_pairs={{0,4},{4,0},{1,5},{5,1},{2,6},{6,2},{3,7},{7,3},{8,12},{12,8},{9,1... | collective-permute-start | bytes 1179656 | tf_op jit(solution)/shard_map/ppermute | solution.py:43
  219.5 3.4 %collective-permute-start.28 = (f32[384]{0:T(512)S(1)}, f32[384]{0:T(512)S(1)}, u32[]{:S(2)}, u32[]{:S(2)}) collective-permute-start(f32[384]{0:T(512)S(1)} %get-tuple-element.31), channel_id=1, source_target_pairs={{0,3},{1,0},{2,1},{3,2},{4,7},{5,4},{6,5},{7,6},{8,11},{9,8},{10,9... | collective-permute-start | bytes 4616 | tf_op jit(solution)/shard_map/ppermute | solution.py:13
  221.8 3.9 %collective-permute-start.27 = (f32[384]{0:T(512)S(1)}, f32[384]{0:T(512)S(1)}, u32[]{:S(2)}, u32[]{:S(2)}) collective-permute-start(f32[384]{0:T(512)S(1)} %get-tuple-element.31), channel_id=1, source_target_pairs={{0,2},{1,3},{2,0},{3,1},{4,6},{5,7},{6,4},{7,5},{8,10},{9,11},{10,... | collective-permute-start | bytes 4616 | tf_op jit(solution)/shard_map/ppermute | solution.py:13
  222.5 3.6 %collective-permute-start.26 = (f32[384]{0:T(512)S(1)}, f32[384]{0:T(512)S(1)}, u32[]{:S(2)}, u32[]{:S(2)}) collective-permute-start(f32[384]{0:T(512)S(1)} %get-tuple-element.31), channel_id=1, source_target_pairs={{0,1},{1,2},{2,3},{3,0},{4,5},{5,6},{6,7},{7,4},{8,9},{9,10},{10,1... | collective-permute-start | bytes 4616 | tf_op jit(solution)/shard_map/ppermute | solution.py:13
  (21 other events, 234.7 us)
Sparse Core Ops, SparseCore 0:
  14.2 69.6 all-gather.5
  85.7 116.0 all-gather.3

commit v3 on v2

--- a/solution.py
+++ b/solution.py
@@ -45,22 +45,15 @@
     def by_core(own, other, at):
         return jnp.where(core == at, own, other)
 
-    weights = lax.all_gather(jnp.concatenate([gate_matrix, up_matrix], axis=1), "z", axis=0)
+    weights = lax.all_gather(
+        jnp.concatenate([gate_matrix, up_matrix], axis=1), CHIP + ("c",), axis=0, tiled=True
+    ).reshape(ny, width, 2 * span)
 
     wide = tokens.astype(f32)
     squares = jnp.sum(wide * wide, axis=1)
     scaled = (wide * scale.astype(f32)).astype(bf16)
-    block = gate_matrix.shape[0]
-    blocks = width // block
-    parity = [
-        jnp.concatenate(
-            [scaled[:, i * block : (i + 1) * block] for i in range(p, blocks, 2)], axis=1
-        )
-        for p in range(2)
-    ]
-    both = jnp.concatenate(
-        [by_core(parity[0], parity[1], 0), swap(by_core(parity[0], parity[1], 1))], axis=0
-    )
+    low, high = scaled[:, :half], scaled[:, half:]
+    both = jnp.concatenate([by_core(low, high, 0), swap(by_core(low, high, 1))], axis=0)
 
     labels = row_judges[:, 0]
     matches = (labels[:, None] == jnp.arange(judges, dtype=jnp.int32)[None, :]).astype(bf16)
@@ -75,10 +68,8 @@
         (slot_at[:, None] + b * count == slots[None, :]).astype(bf16) for b in range(2)
     ]
 
-    down_pair = down[0].reshape(blocks // 2, 2, block, 2 * rank_width)
-    down_parity = [down_pair[:, p].reshape(half, 2 * rank_width) for p in range(2)]
-    down_own = by_core(down_parity[0], down_parity[1], 0)
-    down_other = swap(by_core(down_parity[0], down_parity[1], 1))
+    low, high = down[0, :half], down[0, half:]
+    down_own, down_other = by_core(low, high, 0), swap(by_core(low, high, 1))
     up_own = cut_at(up_factors[0], half_at, cols, 2)
     up_other = swap(cut_at(up_factors[0], 1 - half_at, cols, 2))
 
@@ -117,21 +108,27 @@
         deltas = dot(codes, factors).astype(bf16)
         return deltas.reshape(chips, 2 * cap, span)
 
-    left, right = shift(both, 1, ny), shift(both, -1, ny)
+    left, right = shift(scaled, 1, ny), shift(scaled, -1, ny)
+    sums = squares
+    for d in range(1, ny):
+        sums = sums + shift(squares, d, ny)
+    factor = lax.rsqrt(sums / (width * ny) + EPSILON)
     first = exchange(send_out(0))
-    second, first, left, right, weights = lax.optimization_barrier(
-        (send_out(1), first, left, right, weights)
+    second, first, left, right, factor = lax.optimization_barrier(
+        (send_out(1), first, left, right, factor)
     )
     second = exchange(second)
-    weights = lax.all_gather(weights, "x", axis=1, tiled=True)
-    weights = weights.reshape(ny, width // 2, 2 * span)
-    far = [shift(left[:rows], 1, ny), shift(right[rows:], -1, ny)]
+    far = [shift(left[: rows // 2], 1, ny), shift(right[rows // 2 :], -1, ny)]
     deltas = process(0, first)
     second, deltas, far = lax.optimization_barrier((second, deltas, far))
     returned = exchange(deltas)
     returned, deltas = lax.optimization_barrier((returned, process(1, second)))
-    back = [returned, exchange(deltas)]
-    far = jnp.concatenate(far, axis=0)
+    plain = None
+    for array, d in ((scaled, 0), (left, -1), (right, 1), (jnp.concatenate(far, axis=0), 2)):
+        term = dot(array, lax.dynamic_index_in_dim(weights, ring(d), 0, keepdims=False))
+        plain = term if plain is None else plain + term
+    last, plain = lax.optimization_barrier((exchange(deltas), plain))
+    back = [returned, last]
     by_row = sum(
         lax.dot_general(
             choose[b],
@@ -146,17 +143,7 @@
     low = by_core(here, there, 0).astype(f32)
     high = by_core(here, there, 1).astype(f32)
 
-    plain = None
-    for array, d in ((both, 0), (left, -1), (right, 1), (far, 2)):
-        term = dot(array, lax.dynamic_index_in_dim(weights, ring(d), 0, keepdims=False))
-        plain = term if plain is None else plain + term
-    plain = plain[:rows] + swap(plain[rows:])
-
-    sums = squares
-    for d in range(1, ny):
-        sums = sums + shift(squares, d, ny)
-    factor = lax.rsqrt(sums / (width * ny) + EPSILON)[:, None]
-
+    factor = factor[:, None]
     gate_add = jnp.concatenate([low[:, :cols], high[:, :cols]], axis=1)
     up_add = jnp.concatenate([low[:, cols:], high[:, cols:]], axis=1)
     gate = (plain[:, :span] + ADAPTER_SCALE * gate_add) * factor

time: 237 us -> 218 us (0.920)
  waiting for transfers between devices: 109 us -> 83.9 us
  matrix products: 23.8 us -> 30.5 us
  starting transfers between devices: 69.2 us -> 66.4 us
    all_gather x2 -> x1, waiting for transfers between devices: 40.7 us -> 0.02 us  [body(): lax.all_gather(jnp.concatenate([gate_matrix, up_matrix], axis=1), CHIP +...]
    all_to_all x4, waiting for transfers between devices: 1.91 us -> 16.9 us  [exchange(): return lax.all_to_all(array, CHIP, 0, 0, tiled=True)]
    dot_general x11, matrix products: 20.7 us -> 28.6 us  [dot(): return jnp.dot(a, b, preferred_element_type=jnp.float32)]
    all_to_all x4, starting transfers between devices: 33 us -> 28.9 us  [exchange(): return lax.all_to_all(array, CHIP, 0, 0, tiled=True)]
    ppermute x10 -> x9, starting transfers between devices: 14.5 us -> 17.7 us  [swap(): return lax.ppermute(array, 'c', SWAP)]
    ppermute x10 -> x9, waiting for transfers between devices: 4.38 us -> 6.17 us  [swap(): return lax.ppermute(array, 'c', SWAP)]
    unnamed x43 -> x26, local copies, waits for them, and re-layouts: 4.48 us -> 5.01 us
  transfers between devices with their start and end apart: 35 -> 33, of which waited for: 20 -> 22; matrix products, arithmetic and copies ran while one was open for 14% -> 20% of each run, Pallas kernels for 0% -> 0%
where the time goes in v3:
time: 218 us; the launch traced here: 217 us
  waiting for transfers between devices  83.9 us (38%)
  starting transfers between devices  66.4 us (30%)
  matrix products  30.5 us (14%)
  between operations  13.8 us (6%)
  other arithmetic  12.2 us (6%)
  local copies, waits for them, and re-layouts  9.89 us (5%)
    ppermute x19, waiting for transfers between devices, shift(): lax.ppermute(array, 'y', [(i, (i + distance) % size) for i in range(size)])  60.9 us
    all_to_all x4, starting transfers between devices, exchange(): return lax.all_to_all(array, CHIP, 0, 0, tiled=True)  28.9 us
    dot_general x11, matrix products, dot(): return jnp.dot(a, b, preferred_element_type=jnp.float32)  28.6 us
    ppermute x19, starting transfers between devices, shift(): lax.ppermute(array, 'y', [(i, (i + distance) % size) for i in range(size)])  19.9 us
    ppermute x9, starting transfers between devices, swap(): return lax.ppermute(array, 'c', SWAP)  17.7 us
    all_to_all x4, waiting for transfers between devices, exchange(): return lax.all_to_all(array, CHIP, 0, 0, tiled=True)  16.9 us
    ppermute x9, waiting for transfers between devices, swap(): return lax.ppermute(array, 'c', SWAP)  6.17 us
    unnamed x26, local copies, waits for them, and re-layouts  5.01 us
  transfers between devices with their start and end apart: 33, of which 22 were waited for; matrix products, arithmetic and copies ran while one was open for 20% of the time, Pallas kernels for 0%

profile of v3, /device:TPU:1, one launch (start us, length us, event | category | flops | bytes accessed | tf_op | source)
XLA Modules:
  0.0 216.7 jit_solution(5471165554641498693)
XLA Ops:
  9.0 1.9 fusion.13
  11.1 3.3 %collective-permute-start.1 = (bf16[384,1024]{1,0:T(8,128)(2,1)S(1)}, bf16[384,1024]{1,0:T(8,128)(2,1)}, u32[]{:S(2)}, u32[]{:S(2)}) collective-permute-start(bf16[384,1024]{1,0:T(8,128)(2,1)S(1)} %get-tuple-element.38), channel_id=1, source_target_pairs={{0,4},{4,0},{1,5},{5,1},{2,6},{6,2},{3,7},{7,3},{8,12},{12,8},{9,1... | collective-permute-start | bytes 2359304 | tf_op jit(solution)/shard_map/ppermute | solution.py:43
  16.4 3.7 %fusion.20 = bf16[768,1024]{1,0:T(8,128)(2,1)} fusion(s32[768]{0:T(1024)S(1)} %pad_add_fusion, bf16[384,1024]{1,0:T(8,128)(2,1)} %collective-permute-done.1, bf16[384,1024]{1,0:T(8,128)(2,1)S(1)} %get-tuple-element.37), kind=kOutput, calls=%fused_computation.23 | convolution fusion | flops 1212481536 | bytes 3148800 | tf_op jit(solution)/shard_map/dot_general | solution.py:17
  20.1 9.3 %all-to-all-start = ((bf16[32,24,1024]{2,1,0:T(8,128)(2,1)}), bf16[32,24,1024]{2,1,0:T(8,128)(2,1)S(1)}, u32[]{:S(2)}, u32[]{:S(2)}) async-start(bf16[32,24,1024]{2,1,0:T(8,128)(2,1)} %bitcast.52), calls=%async_computation | async-start | bytes 3145728 | tf_op jit(solution)/shard_map/all_to_all | solution.py:80
  34.7 2.0 select_bitcast_fusion
  36.8 29.1 %collective-permute-done.6 = f32[384]{0:T(512)S(1)} collective-permute-done((f32[384]{0:T(512)S(1)}, f32[384]{0:T(512)S(1)}, u32[]{:S(2)}, u32[]{:S(2)}) %collective-permute-start.6) | collective-permute-done | bytes 1568 | tf_op jit(solution)/shard_map/ppermute | solution.py:13
  65.9 1.8 collective-permute-start.7
  67.8 3.8 %fusion.21 = bf16[768,1024]{1,0:T(8,128)(2,1)} fusion(s32[768]{0:T(1024)S(1)} %pad_add_fusion, s32[768]{0:T(1024)S(1)} %iota_add_fusion, bf16[384,1024]{1,0:T(8,128)(2,1)} %collective-permute-done.1, bf16[384,1024]{1,0:T(8,128)(2,1)S(1)} %copy-done.2), kind=kOutput, calls=%fused_computation.24 | convolution fusion | flops 1212481536 | bytes 3151872 | tf_op jit(solution)/shard_map/dot_general | solution.py:17
  72.7 2.9 %all-to-all-done = bf16[32,24,1024]{2,1,0:T(8,128)(2,1)S(1)} async-done(((bf16[32,24,1024]{2,1,0:T(8,128)(2,1)}), bf16[32,24,1024]{2,1,0:T(8,128)(2,1)S(1)}, u32[]{:S(2)}, u32[]{:S(2)}) %all-to-all-start) | async-done | bytes 1572896 | tf_op jit(solution)/shard_map/all_to_all | solution.py:80
  76.7 6.6 %all-to-all-start.1 = ((bf16[32,24,1024]{2,1,0:T(8,128)(2,1)}), bf16[32,24,1024]{2,1,0:T(8,128)(2,1)S(1)}, u32[]{:S(2)}, u32[]{:S(2)}) async-start(bf16[32,24,1024]{2,1,0:T(8,128)(2,1)} %bitcast), calls=%async_computation.1 | async-start | bytes 3145728 | tf_op jit(solution)/shard_map/all_to_all | solution.py:80
  83.4 2.6 %fusion.44 = f32[768,256]{1,0:T(8,128)S(1)} fusion(bf16[768,1024]{1,0:T(8,128)(2,1)} %bitcast.51, bf16[1024,256]{1,0:T(8,128)(2,1)} %collective-permute-done.7, pred[]{:T(512)S(6)} %eq.28, bf16[1,2048,256]{2,1,0:T(8,128)(2,1)} %param.11), kind=kOutput, calls=%fused_computation.60 | convolution fusion | flops 403177472 | bytes 3933184 | tf_op jit(solution)/shard_map/dot_general | solution.py:17
  91.6 2.6 %collective-permute-start.11 = (f32[96,256]{1,0:T(8,128)}, f32[96,256]{1,0:T(8,128)}, u32[]{:S(2)}, u32[]{:S(2)}) collective-permute-start(f32[96,256]{1,0:T(8,128)} %get-tuple-element.55), channel_id=1, source_target_pairs={{0,3},{1,0},{2,1},{3,2},{4,7},{5,4},{6,5},{7,6},{8,11},{9,8},{10,9... | collective-permute-start | bytes 294920 | tf_op jit(solution)/shard_map/ppermute | solution.py:13
  99.7 3.0 %collective-permute-done.9 = f32[96,256]{1,0:T(8,128)} collective-permute-done((f32[96,256]{1,0:T(8,128)}, f32[96,256]{1,0:T(8,128)}, u32[]{:S(2)}, u32[]{:S(2)}) %collective-permute-start.9) | collective-permute-done | bytes 98336 | tf_op jit(solution)/shard_map/ppermute | solution.py:13
  107.4 2.7 %collective-permute-start.18 = (bf16[192,2048]{1,0:T(8,128)(2,1)S(1)}, bf16[192,2048]{1,0:T(8,128)(2,1)}, u32[]{:S(2)}, u32[]{:S(2)}) collective-permute-start(bf16[192,2048]{1,0:T(8,128)(2,1)S(1)} %slice.61), channel_id=1, source_target_pairs={{0,3},{1,0},{2,1},{3,2},{4,7},{5,4},{6,5},{7,6},{8,11},{9,8},{10,9... | collective-permute-start | bytes 2359304 | tf_op jit(solution)/shard_map/ppermute | solution.py:13
  111.6 15.8 %collective-permute-done.13 = bf16[96,256]{1,0:T(8,128)(2,1)S(1)} collective-permute-done((bf16[96,256]{1,0:T(8,128)(2,1)S(1)}, bf16[96,256]{1,0:T(8,128)(2,1)S(1)}, u32[]{:S(2)}, u32[]{:S(2)}) %collective-permute-start.13) | collective-permute-done | bytes 49184 | tf_op jit(solution)/shard_map/ppermute | solution.py:13
  128.0 2.0 collective-permute-start.15
  133.2 5.7 %all-to-all-done.1 = bf16[32,24,1024]{2,1,0:T(8,128)(2,1)S(1)} async-done(((bf16[32,24,1024]{2,1,0:T(8,128)(2,1)}), bf16[32,24,1024]{2,1,0:T(8,128)(2,1)S(1)}, u32[]{:S(2)}, u32[]{:S(2)}) %all-to-all-start.1) | async-done | bytes 1572896 | tf_op jit(solution)/shard_map/all_to_all | solution.py:80
  142.4 2.6 %collective-permute-start.19 = (f32[384,256]{1,0:T(8,128)}, f32[384,256]{1,0:T(8,128)}, u32[]{:S(2)}, u32[]{:S(2)}) collective-permute-start(f32[384,256]{1,0:T(8,128)} %constant_dynamic-slice_fusion.3), channel_id=1, source_target_pairs={{0,4},{4,0},{1,5},{5,1},{2,6},{6,2},{3,7},{7,3},{8,12},{12,8},{9,1... | collective-permute-start | bytes 1179656 | tf_op jit(solution)/shard_map/ppermute | solution.py:43
  145.0 4.9 %all-to-all-start.2 = ((bf16[32,24,512]{2,1,0:T(8,128)(2,1)}), bf16[32,24,512]{2,1,0:T(8,128)(2,1)S(1)}, u32[]{:S(2)}, u32[]{:S(2)}) async-start(bf16[32,24,512]{2,1,0:T(8,128)(2,1)} %bitcast.54), calls=%async_computation.2 | async-start | bytes 1572864 | tf_op jit(solution)/shard_map/all_to_all | solution.py:80
  151.1 2.7 %collective-permute-start.22 = (f32[96,256]{1,0:T(8,128)S(1)}, f32[96,256]{1,0:T(8,128)S(1)}, u32[]{:S(2)}, u32[]{:S(2)}) collective-permute-start(f32[96,256]{1,0:T(8,128)S(1)} %get-tuple-element.50), channel_id=1, source_target_pairs={{0,3},{1,0},{2,1},{3,2},{4,7},{5,4},{6,5},{7,6},{8,11},{9,8},{10,9... | collective-permute-start | bytes 294920 | tf_op jit(solution)/shard_map/ppermute | solution.py:13
  155.4 3.4 %collective-permute-done.21 = f32[96,256]{1,0:T(8,128)S(1)} collective-permute-done((f32[96,256]{1,0:T(8,128)S(1)}, f32[96,256]{1,0:T(8,128)S(1)}, u32[]{:S(2)}, u32[]{:S(2)}) %collective-permute-start.21) | collective-permute-done | bytes 98336 | tf_op jit(solution)/shard_map/ppermute | solution.py:13
  158.9 2.9 %collective-permute-done.20 = f32[96,256]{1,0:T(8,128)S(1)} collective-permute-done((f32[96,256]{1,0:T(8,128)S(1)}, f32[96,256]{1,0:T(8,128)S(1)}, u32[]{:S(2)}, u32[]{:S(2)}) %collective-permute-start.20) | collective-permute-done | bytes 98336 | tf_op jit(solution)/shard_map/ppermute | solution.py:13
  162.6 2.0 collective-permute-start.25
  164.6 1.9 collective-permute-done.23
  167.5 1.9 collective-permute-start.26
  173.0 8.0 %all-to-all-start.3 = ((bf16[32,24,512]{2,1,0:T(8,128)(2,1)}), bf16[32,24,512]{2,1,0:T(8,128)(2,1)S(1)}, u32[]{:S(2)}, u32[]{:S(2)}) async-start(bf16[32,24,512]{2,1,0:T(8,128)(2,1)} %bitcast.13), calls=%async_computation.3 | async-start | bytes 1572864 | tf_op jit(solution)/shard_map/all_to_all | solution.py:80
  181.1 4.6 %fusion.2 = f32[384,1024]{1,0:T(8,128)S(1)} fusion(bf16[384,2048]{1,0:T(8,128)(2,1)} %collective-permute-done.3, bf16[4,2048,1024]{2,1,0:T(8,128)(2,1)} %bitcast.56, u32[]{:T(128)S(6)} %rem.56), kind=kOutput, calls=%fused_computation.2 | convolution fusion | flops 1610612736 | bytes 7340036 | tf_op jit(solution)/shard_map/dot_general | solution.py:17
  185.7 4.7 %fusion.4 = f32[384,1024]{1,0:T(8,128)S(1)} fusion(bf16[384,2048]{1,0:T(8,128)(2,1)S(1)} %copy-done.7, bf16[4,2048,1024]{2,1,0:T(8,128)(2,1)} %bitcast.57, u32[]{:T(128)S(6)} %rem.58), kind=kOutput, calls=%fused_computation.4 | convolution fusion | flops 1610612736 | bytes 7340036 | tf_op jit(solution)/shard_map/dot_general | solution.py:17
  190.5 1.8 fusion.6
  192.3 3.0 %add_add_fusion = f32[384,1024]{1,0:T(8,128)S(1)} fusion(f32[384,1024]{1,0:T(8,128)S(1)} %fusion.2, f32[384,1024]{1,0:T(8,128)S(1)} %fusion.6, f32[384,1024]{1,0:T(8,128)S(1)} %fusion.4, bf16[4,2048,1024]{2,1,0:T(8,128)(2,1)S(1)} %bitcast.59, u32[]{:T(128)S(6)} %rem.57, bf16[192,2048]{1,0:T(8,128)(2,1)} %collective-permute-done.18, ...), kind=kOutput, calls=%fused_computation.30 | convolution fusion | flops 1614938112 | bytes 12058628 | tf_op jit(solution)/shard_map/dot_general | solution.py:17
  195.2 7.1 %all-to-all-done.3 = bf16[32,24,512]{2,1,0:T(8,128)(2,1)S(1)} async-done(((bf16[32,24,512]{2,1,0:T(8,128)(2,1)}), bf16[32,24,512]{2,1,0:T(8,128)(2,1)S(1)}, u32[]{:S(2)}, u32[]{:S(2)}) %all-to-all-start.3) | async-done | bytes 786464 | tf_op jit(solution)/shard_map/all_to_all | solution.py:80
  204.2 2.9 %collective-permute-start.27 = (bf16[384,512]{1,0:T(8,128)(2,1)S(1)}, bf16[384,512]{1,0:T(8,128)(2,1)S(1)}, u32[]{:S(2)}, u32[]{:S(2)}) collective-permute-start(bf16[384,512]{1,0:T(8,128)(2,1)S(1)} %slice.79), channel_id=1, source_target_pairs={{0,4},{4,0},{1,5},{5,1},{2,6},{6,2},{3,7},{7,3},{8,12},{12,8},{9,1... | collective-permute-start | bytes 1179656 | tf_op jit(solution)/shard_map/ppermute | solution.py:43
  (112 shorter events, 49.4 us)
Async XLA Ops:
  6.5 174.5 %all-gather.2.cloned.1.call-start = ((), (), s32[]{:S(2)}) async-start(), calls=%async_computation.4 | async-start | bytes 17039360 | tf_op jit(solution)/shard_map/all_gather | solution.py:48
  11.1 5.4 %collective-permute-start.1 = (bf16[384,1024]{1,0:T(8,128)(2,1)S(1)}, bf16[384,1024]{1,0:T(8,128)(2,1)}, u32[]{:S(2)}, u32[]{:S(2)}) collective-permute-start(bf16[384,1024]{1,0:T(8,128)(2,1)S(1)} %get-tuple-element.38), channel_id=1, source_target_pairs={{0,4},{4,0},{1,5},{5,1},{2,6},{6,2},{3,7},{7,3},{8,12},{12,8},{9,1... | collective-permute-start | bytes 2359304 | tf_op jit(solution)/shard_map/ppermute | solution.py:43
  20.1 55.5 %all-to-all-start = ((bf16[32,24,1024]{2,1,0:T(8,128)(2,1)}), bf16[32,24,1024]{2,1,0:T(8,128)(2,1)S(1)}, u32[]{:S(2)}, u32[]{:S(2)}) async-start(bf16[32,24,1024]{2,1,0:T(8,128)(2,1)} %bitcast.52), calls=%async_computation | async-start | bytes 3145728 | tf_op jit(solution)/shard_map/all_to_all | solution.py:80
  29.4 42.1 %collective-permute-start.2 = (bf16[384,2048]{1,0:T(8,128)(2,1)S(1)}, bf16[384,2048]{1,0:T(8,128)(2,1)S(1)}, u32[]{:S(2)}, u32[]{:S(2)}) collective-permute-start(bf16[384,2048]{1,0:T(8,128)(2,1)S(1)} %get-tuple-element.36), channel_id=1, source_target_pairs={{0,1},{1,2},{2,3},{3,0},{4,5},{5,6},{6,7},{7,4},{8,9},{9,10},{10,1... | collective-permute-start | bytes 4718600 | tf_op jit(solution)/shard_map/ppermute | solution.py:13
  30.8 41.9 %collective-permute-start.3 = (bf16[384,2048]{1,0:T(8,128)(2,1)S(1)}, bf16[384,2048]{1,0:T(8,128)(2,1)}, u32[]{:S(2)}, u32[]{:S(2)}) collective-permute-start(bf16[384,2048]{1,0:T(8,128)(2,1)S(1)} %get-tuple-element.36), channel_id=1, source_target_pairs={{0,3},{1,0},{2,1},{3,2},{4,7},{5,4},{6,5},{7,6},{8,11},{9,8},{10,9... | collective-permute-start | bytes 4718600 | tf_op jit(solution)/shard_map/ppermute | solution.py:13
  32.3 33.6 %collective-permute-start.6 = (f32[384]{0:T(512)S(1)}, f32[384]{0:T(512)S(1)}, u32[]{:S(2)}, u32[]{:S(2)}) collective-permute-start(f32[384]{0:T(512)S(1)} %get-tuple-element.35), channel_id=1, source_target_pairs={{0,3},{1,0},{2,1},{3,2},{4,7},{5,4},{6,5},{7,6},{8,11},{9,8},{10,9... | collective-permute-start | bytes 4616 | tf_op jit(solution)/shard_map/ppermute | solution.py:13
  33.7 34.1 %collective-permute-start.5 = (f32[384]{0:T(512)S(1)}, f32[384]{0:T(512)S(1)}, u32[]{:S(2)}, u32[]{:S(2)}) collective-permute-start(f32[384]{0:T(512)S(1)} %get-tuple-element.35), channel_id=1, source_target_pairs={{0,2},{1,3},{2,0},{3,1},{4,6},{5,7},{6,4},{7,5},{8,10},{9,11},{10,... | collective-permute-start | bytes 4616 | tf_op jit(solution)/shard_map/ppermute | solution.py:13
  34.0 33.7 %collective-permute-start.4 = (f32[384]{0:T(512)S(1)}, f32[384]{0:T(512)S(1)}, u32[]{:S(2)}, u32[]{:S(2)}) collective-permute-start(f32[384]{0:T(512)S(1)} %get-tuple-element.35), channel_id=1, source_target_pairs={{0,1},{1,2},{2,3},{3,0},{4,5},{5,6},{6,7},{7,4},{8,9},{9,10},{10,1... | collective-permute-start | bytes 4616 | tf_op jit(solution)/shard_map/ppermute | solution.py:13
  65.9 17.5 %collective-permute-start.7 = (bf16[1024,256]{1,0:T(8,128)(2,1)}, bf16[1024,256]{1,0:T(8,128)(2,1)}, u32[]{:S(2)}, u32[]{:S(2)}) collective-permute-start(bf16[1024,256]{1,0:T(8,128)(2,1)} %select_bitcast_fusion), channel_id=1, source_target_pairs={{0,4},{4,0},{1,5},{5,1},{2,6},{6,2},{3,7},{7,3},{8,12},{12,8},{9,1... | collective-permute-start | bytes 1572872 | tf_op jit(solution)/shard_map/ppermute | solution.py:43
  76.7 62.2 %all-to-all-start.1 = ((bf16[32,24,1024]{2,1,0:T(8,128)(2,1)}), bf16[32,24,1024]{2,1,0:T(8,128)(2,1)S(1)}, u32[]{:S(2)}, u32[]{:S(2)}) async-start(bf16[32,24,1024]{2,1,0:T(8,128)(2,1)} %bitcast), calls=%async_computation.1 | async-start | bytes 3145728 | tf_op jit(solution)/shard_map/all_to_all | solution.py:80
  86.9 2.8 %collective-permute-start.8 = (f32[384,256]{1,0:T(8,128)S(1)}, f32[384,256]{1,0:T(8,128)}, u32[]{:S(2)}, u32[]{:S(2)}) collective-permute-start(f32[384,256]{1,0:T(8,128)S(1)} %constant_dynamic-slice_fusion.7), channel_id=1, source_target_pairs={{0,4},{4,0},{1,5},{5,1},{2,6},{6,2},{3,7},{7,3},{8,12},{12,8},{9,1... | collective-permute-start | bytes 1179656 | tf_op jit(solution)/shard_map/ppermute | solution.py:43
  91.6 6.7 %collective-permute-start.11 = (f32[96,256]{1,0:T(8,128)}, f32[96,256]{1,0:T(8,128)}, u32[]{:S(2)}, u32[]{:S(2)}) collective-permute-start(f32[96,256]{1,0:T(8,128)} %get-tuple-element.55), channel_id=1, source_target_pairs={{0,3},{1,0},{2,1},{3,2},{4,7},{5,4},{6,5},{7,6},{8,11},{9,8},{10,9... | collective-permute-start | bytes 294920 | tf_op jit(solution)/shard_map/ppermute | solution.py:13
  94.2 5.5 %collective-permute-start.10 = (f32[96,256]{1,0:T(8,128)}, f32[96,256]{1,0:T(8,128)}, u32[]{:S(2)}, u32[]{:S(2)}) collective-permute-start(f32[96,256]{1,0:T(8,128)} %get-tuple-element.56), channel_id=1, source_target_pairs={{0,2},{1,3},{2,0},{3,1},{4,6},{5,7},{6,4},{7,5},{8,10},{9,11},{10,... | collective-permute-start | bytes 294920 | tf_op jit(solution)/shard_map/ppermute | solution.py:13
  94.7 8.0 %collective-permute-start.9 = (f32[96,256]{1,0:T(8,128)}, f32[96,256]{1,0:T(8,128)}, u32[]{:S(2)}, u32[]{:S(2)}) collective-permute-start(f32[96,256]{1,0:T(8,128)} %get-tuple-element.54), channel_id=1, source_target_pairs={{0,1},{1,2},{2,3},{3,0},{4,5},{5,6},{6,7},{7,4},{8,9},{9,10},{10,1... | collective-permute-start | bytes 294920 | tf_op jit(solution)/shard_map/ppermute | solution.py:13
  95.9 7.9 %collective-permute-start.16 = (bf16[2,128,256]{2,1,0:T(8,128)(2,1)}, bf16[2,128,256]{2,1,0:T(8,128)(2,1)}, u32[]{:S(2)}, u32[]{:S(2)}) collective-permute-start(bf16[2,128,256]{2,1,0:T(8,128)(2,1)} %dynamic-slice_bitcast_fusion), channel_id=1, source_target_pairs={{0,4},{4,0},{1,5},{5,1},{2,6},{6,2},{3,7},{7,3},{8,12},{12,8},{9,1... | collective-permute-start | bytes 393224 | tf_op jit(solution)/shard_map/ppermute | solution.py:43
  103.7 7.9 %collective-permute-start.12 = (bf16[96,256]{1,0:T(8,128)(2,1)S(1)}, bf16[96,256]{1,0:T(8,128)(2,1)S(1)}, u32[]{:S(2)}, u32[]{:S(2)}) collective-permute-start(bf16[96,256]{1,0:T(8,128)(2,1)S(1)} %get-tuple-element.34), channel_id=1, source_target_pairs={{0,1},{1,2},{2,3},{3,0},{4,5},{5,6},{6,7},{7,4},{8,9},{9,10},{10,1... | collective-permute-start | bytes 147464 | tf_op jit(solution)/shard_map/ppermute | solution.py:13
  106.1 26.3 %collective-permute-start.17 = (bf16[192,2048]{1,0:T(8,128)(2,1)S(1)}, bf16[192,2048]{1,0:T(8,128)(2,1)S(1)}, u32[]{:S(2)}, u32[]{:S(2)}) collective-permute-start(bf16[192,2048]{1,0:T(8,128)(2,1)S(1)} %slice.60), channel_id=1, source_target_pairs={{0,1},{1,2},{2,3},{3,0},{4,5},{5,6},{6,7},{7,4},{8,9},{9,10},{10,1... | collective-permute-start | bytes 2359304 | tf_op jit(solution)/shard_map/ppermute | solution.py:13
  107.4 25.9 %collective-permute-start.18 = (bf16[192,2048]{1,0:T(8,128)(2,1)S(1)}, bf16[192,2048]{1,0:T(8,128)(2,1)}, u32[]{:S(2)}, u32[]{:S(2)}) collective-permute-start(bf16[192,2048]{1,0:T(8,128)(2,1)S(1)} %slice.61), channel_id=1, source_target_pairs={{0,3},{1,0},{2,1},{3,2},{4,7},{5,4},{6,5},{7,6},{8,11},{9,8},{10,9... | collective-permute-start | bytes 2359304 | tf_op jit(solution)/shard_map/ppermute | solution.py:13
  110.1 17.3 %collective-permute-start.13 = (bf16[96,256]{1,0:T(8,128)(2,1)S(1)}, bf16[96,256]{1,0:T(8,128)(2,1)S(1)}, u32[]{:S(2)}, u32[]{:S(2)}) collective-permute-start(bf16[96,256]{1,0:T(8,128)(2,1)S(1)} %get-tuple-element.34), channel_id=1, source_target_pairs={{0,2},{1,3},{2,0},{3,1},{4,6},{5,7},{6,4},{7,5},{8,10},{9,11},{10,... | collective-permute-start | bytes 147464 | tf_op jit(solution)/shard_map/ppermute | solution.py:13
  111.4 16.6 %collective-permute-start.14 = (bf16[96,256]{1,0:T(8,128)(2,1)S(1)}, bf16[96,256]{1,0:T(8,128)(2,1)S(1)}, u32[]{:S(2)}, u32[]{:S(2)}) collective-permute-start(bf16[96,256]{1,0:T(8,128)(2,1)S(1)} %get-tuple-element.34), channel_id=1, source_target_pairs={{0,3},{1,0},{2,1},{3,2},{4,7},{5,4},{6,5},{7,6},{8,11},{9,8},{10,9... | collective-permute-start | bytes 147464 | tf_op jit(solution)/shard_map/ppermute | solution.py:13
  128.0 3.1 %collective-permute-start.15 = (bf16[384,256]{1,0:T(8,128)(2,1)S(1)}, bf16[384,256]{1,0:T(8,128)(2,1)S(1)}, u32[]{:S(2)}, u32[]{:S(2)}) collective-permute-start(bf16[384,256]{1,0:T(8,128)(2,1)S(1)} %constant_dynamic-update-slice_fusion.4), channel_id=1, source_target_pairs={{0,4},{4,0},{1,5},{5,1},{2,6},{6,2},{3,7},{7,3},{8,12},{12,8},{9,1... | collective-permute-start | bytes 589832 | tf_op jit(solution)/shard_map/ppermute | solution.py:43
  142.4 7.5 %collective-permute-start.19 = (f32[384,256]{1,0:T(8,128)}, f32[384,256]{1,0:T(8,128)}, u32[]{:S(2)}, u32[]{:S(2)}) collective-permute-start(f32[384,256]{1,0:T(8,128)} %constant_dynamic-slice_fusion.3), channel_id=1, source_target_pairs={{0,4},{4,0},{1,5},{5,1},{2,6},{6,2},{3,7},{7,3},{8,12},{12,8},{9,1... | collective-permute-start | bytes 1179656 | tf_op jit(solution)/shard_map/ppermute | solution.py:43
  145.0 28.0 %all-to-all-start.2 = ((bf16[32,24,512]{2,1,0:T(8,128)(2,1)}), bf16[32,24,512]{2,1,0:T(8,128)(2,1)S(1)}, u32[]{:S(2)}, u32[]{:S(2)}) async-start(bf16[32,24,512]{2,1,0:T(8,128)(2,1)} %bitcast.54), calls=%async_computation.2 | async-start | bytes 1572864 | tf_op jit(solution)/shard_map/all_to_all | solution.py:80
  151.1 4.4 %collective-permute-start.22 = (f32[96,256]{1,0:T(8,128)S(1)}, f32[96,256]{1,0:T(8,128)S(1)}, u32[]{:S(2)}, u32[]{:S(2)}) collective-permute-start(f32[96,256]{1,0:T(8,128)S(1)} %get-tuple-element.50), channel_id=1, source_target_pairs={{0,3},{1,0},{2,1},{3,2},{4,7},{5,4},{6,5},{7,6},{8,11},{9,8},{10,9... | collective-permute-start | bytes 294920 | tf_op jit(solution)/shard_map/ppermute | solution.py:13
  153.8 5.1 %collective-permute-start.21 = (f32[96,256]{1,0:T(8,128)S(1)}, f32[96,256]{1,0:T(8,128)S(1)}, u32[]{:S(2)}, u32[]{:S(2)}) collective-permute-start(f32[96,256]{1,0:T(8,128)S(1)} %get-tuple-element.51), channel_id=1, source_target_pairs={{0,2},{1,3},{2,0},{3,1},{4,6},{5,7},{6,4},{7,5},{8,10},{9,11},{10,... | collective-permute-start | bytes 294920 | tf_op jit(solution)/shard_map/ppermute | solution.py:13
  154.3 7.6 %collective-permute-start.20 = (f32[96,256]{1,0:T(8,128)S(1)}, f32[96,256]{1,0:T(8,128)S(1)}, u32[]{:S(2)}, u32[]{:S(2)}) collective-permute-start(f32[96,256]{1,0:T(8,128)S(1)} %get-tuple-element.49), channel_id=1, source_target_pairs={{0,1},{1,2},{2,3},{3,0},{4,5},{5,6},{6,7},{7,4},{8,9},{9,10},{10,1... | collective-permute-start | bytes 294920 | tf_op jit(solution)/shard_map/ppermute | solution.py:13
  161.9 4.6 %collective-permute-start.23 = (bf16[96,256]{1,0:T(8,128)(2,1)S(1)}, bf16[96,256]{1,0:T(8,128)(2,1)S(1)}, u32[]{:S(2)}, u32[]{:S(2)}) collective-permute-start(bf16[96,256]{1,0:T(8,128)(2,1)S(1)} %get-tuple-element.32), channel_id=1, source_target_pairs={{0,1},{1,2},{2,3},{3,0},{4,5},{5,6},{6,7},{7,4},{8,9},{9,10},{10,1... | collective-permute-start | bytes 147464 | tf_op jit(solution)/shard_map/ppermute | solution.py:13
  162.0 5.0 %collective-permute-start.24 = (bf16[96,256]{1,0:T(8,128)(2,1)S(1)}, bf16[96,256]{1,0:T(8,128)(2,1)S(1)}, u32[]{:S(2)}, u32[]{:S(2)}) collective-permute-start(bf16[96,256]{1,0:T(8,128)(2,1)S(1)} %get-tuple-element.32), channel_id=1, source_target_pairs={{0,2},{1,3},{2,0},{3,1},{4,6},{5,7},{6,4},{7,5},{8,10},{9,11},{10,... | collective-permute-start | bytes 147464 | tf_op jit(solution)/shard_map/ppermute | solution.py:13
  162.6 4.9 %collective-permute-start.25 = (bf16[96,256]{1,0:T(8,128)(2,1)S(1)}, bf16[96,256]{1,0:T(8,128)(2,1)S(1)}, u32[]{:S(2)}, u32[]{:S(2)}) collective-permute-start(bf16[96,256]{1,0:T(8,128)(2,1)S(1)} %get-tuple-element.32), channel_id=1, source_target_pairs={{0,3},{1,0},{2,1},{3,2},{4,7},{5,4},{6,5},{7,6},{8,11},{9,8},{10,9... | collective-permute-start | bytes 147464 | tf_op jit(solution)/shard_map/ppermute | solution.py:13
  167.5 3.0 %collective-permute-start.26 = (bf16[384,256]{1,0:T(8,128)(2,1)S(1)}, bf16[384,256]{1,0:T(8,128)(2,1)S(1)}, u32[]{:S(2)}, u32[]{:S(2)}) collective-permute-start(bf16[384,256]{1,0:T(8,128)(2,1)S(1)} %constant_dynamic-update-slice_fusion), channel_id=1, source_target_pairs={{0,4},{4,0},{1,5},{5,1},{2,6},{6,2},{3,7},{7,3},{8,12},{12,8},{9,1... | collective-permute-start | bytes 589832 | tf_op jit(solution)/shard_map/ppermute | solution.py:43
  173.0 29.3 %all-to-all-start.3 = ((bf16[32,24,512]{2,1,0:T(8,128)(2,1)}), bf16[32,24,512]{2,1,0:T(8,128)(2,1)S(1)}, u32[]{:S(2)}, u32[]{:S(2)}) async-start(bf16[32,24,512]{2,1,0:T(8,128)(2,1)} %bitcast.13), calls=%async_computation.3 | async-start | bytes 1572864 | tf_op jit(solution)/shard_map/all_to_all | solution.py:80
  204.2 4.2 %collective-permute-start.27 = (bf16[384,512]{1,0:T(8,128)(2,1)S(1)}, bf16[384,512]{1,0:T(8,128)(2,1)S(1)}, u32[]{:S(2)}, u32[]{:S(2)}) collective-permute-start(bf16[384,512]{1,0:T(8,128)(2,1)S(1)} %slice.79), channel_id=1, source_target_pairs={{0,4},{4,0},{1,5},{5,1},{2,6},{6,2},{3,7},{7,3},{8,12},{12,8},{9,1... | collective-permute-start | bytes 1179656 | tf_op jit(solution)/shard_map/ppermute | solution.py:43
  (14 other events, 87.9 us)
Sparse Core Ops, SparseCore 0:
  10.1 147.0 all-gather.1

commit v4 on v3

--- a/solution.py
+++ b/solution.py
@@ -45,15 +45,13 @@
     def by_core(own, other, at):
         return jnp.where(core == at, own, other)
 
-    weights = lax.all_gather(
-        jnp.concatenate([gate_matrix, up_matrix], axis=1), CHIP + ("c",), axis=0, tiled=True
-    ).reshape(ny, width, 2 * span)
-
-    wide = tokens.astype(f32)
-    squares = jnp.sum(wide * wide, axis=1)
-    scaled = (wide * scale.astype(f32)).astype(bf16)
-    low, high = scaled[:, :half], scaled[:, half:]
-    both = jnp.concatenate([by_core(low, high, 0), swap(by_core(low, high, 1))], axis=0)
+    low, high = tokens[:, :half], tokens[:, half:]
+    own, other = by_core(low, high, 0), swap(by_core(low, high, 1))
+    other, mine = lax.optimization_barrier(
+        (other, jnp.concatenate([gate_matrix, up_matrix], axis=1))
+    )
+    both = jnp.concatenate([own, other], axis=0)
+    weights = lax.all_gather(mine, CHIP + ("c",), axis=0, tiled=True).reshape(ny, width, 2 * span)
 
     labels = row_judges[:, 0]
     matches = (labels[:, None] == jnp.arange(judges, dtype=jnp.int32)[None, :]).astype(bf16)
@@ -68,7 +66,8 @@
         (slot_at[:, None] + b * count == slots[None, :]).astype(bf16) for b in range(2)
     ]
 
-    low, high = down[0, :half], down[0, half:]
+    scaled_down = (down[0].astype(f32) * scale.astype(f32)[:, None]).astype(bf16)
+    low, high = scaled_down[:half], scaled_down[half:]
     down_own, down_other = by_core(low, high, 0), swap(by_core(low, high, 1))
     up_own = cut_at(up_factors[0], half_at, cols, 2)
     up_other = swap(cut_at(up_factors[0], 1 - half_at, cols, 2))
@@ -108,12 +107,15 @@
         deltas = dot(codes, factors).astype(bf16)
         return deltas.reshape(chips, 2 * cap, span)
 
+    first = exchange(send_out(0))
+    wide = tokens.astype(f32)
+    squares = jnp.sum(wide * wide, axis=1)
+    scaled = (wide * scale.astype(f32)).astype(bf16)
     left, right = shift(scaled, 1, ny), shift(scaled, -1, ny)
     sums = squares
     for d in range(1, ny):
         sums = sums + shift(squares, d, ny)
     factor = lax.rsqrt(sums / (width * ny) + EPSILON)
-    first = exchange(send_out(0))
     second, first, left, right, factor = lax.optimization_barrier(
         (send_out(1), first, left, right, factor)
     )

time: 218 us -> 216 us (level)
  waiting for transfers between devices: 83.9 us -> 94.8 us
  other arithmetic: 12.2 us -> 7.71 us
  local copies, waits for them, and re-layouts: 9.89 us -> 6.79 us
  starting transfers between devices: 66.4 us -> 63.9 us
  matrix products: 30.5 us -> 28.2 us
    all_to_all x4, waiting for transfers between devices: 16.9 us -> 25 us  [exchange(): return lax.all_to_all(array, CHIP, 0, 0, tiled=True)]
    all_to_all x4, starting transfers between devices: 28.9 us -> 25.7 us  [exchange(): return lax.all_to_all(array, CHIP, 0, 0, tiled=True)]
    unnamed x26 -> x36, local copies, waits for them, and re-layouts: 5.01 us -> 2.29 us
    dot_general x11, matrix products: 28.6 us -> 26.3 us  [dot(): return jnp.dot(a, b, preferred_element_type=jnp.float32)]
  transfers between devices with their start and end apart: 33 -> 33, of which waited for: 22 -> 21; matrix products, arithmetic and copies ran while one was open for 20% -> 17% of each run, Pallas kernels for 0% -> 0%
where the time goes in v4:
time: 216 us; the launch traced here: 215 us
  waiting for transfers between devices  94.8 us (44%)
  starting transfers between devices  63.9 us (30%)
  matrix products  28.2 us (13%)
  between operations  13.8 us (6%)
  other arithmetic  7.71 us (4%)
  local copies, waits for them, and re-layouts  6.79 us (3%)
    ppermute x19, waiting for transfers between devices, shift(): lax.ppermute(array, 'y', [(i, (i + distance) % size) for i in range(size)])  62.7 us
    dot_general x11, matrix products, dot(): return jnp.dot(a, b, preferred_element_type=jnp.float32)  26.3 us
    all_to_all x4, starting transfers between devices, exchange(): return lax.all_to_all(array, CHIP, 0, 0, tiled=True)  25.7 us
    all_to_all x4, waiting for transfers between devices, exchange(): return lax.all_to_all(array, CHIP, 0, 0, tiled=True)  25 us
    ppermute x19, starting transfers between devices, shift(): lax.ppermute(array, 'y', [(i, (i + distance) % size) for i in range(size)])  20.1 us
    ppermute x9, starting transfers between devices, swap(): return lax.ppermute(array, 'c', SWAP)  18.2 us
    ppermute x9, waiting for transfers between devices, swap(): return lax.ppermute(array, 'c', SWAP)  7.08 us
  transfers between devices with their start and end apart: 33, of which 21 were waited for; matrix products, arithmetic and copies ran while one was open for 17% of the time, Pallas kernels for 0%

profile of v4, /device:TPU:1, one launch (start us, length us, event | category | flops | bytes accessed | tf_op | source)
XLA Modules:
  0.0 215.2 jit_solution(13122127148405333079)
XLA Ops:
  8.1 3.3 %collective-permute-start.1 = (bf16[384,1024]{1,0:T(8,128)(2,1)S(1)}, bf16[384,1024]{1,0:T(8,128)(2,1)S(1)}, u32[]{:S(2)}, u32[]{:S(2)}) collective-permute-start(bf16[384,1024]{1,0:T(8,128)(2,1)S(1)} %get-tuple-element.42), channel_id=1, source_target_pairs={{0,4},{4,0},{1,5},{5,1},{2,6},{6,2},{3,7},{7,3},{8,12},{12,8},{9,1... | collective-permute-start | bytes 2359304 | tf_op jit(solution)/shard_map/ppermute | solution.py:43
  14.9 2.6 %fusion.21 = bf16[768,1024]{1,0:T(8,128)(2,1)} fusion(s32[768]{0:T(1024)S(1)} %pad_add_fusion, bf16[384,1024]{1,0:T(8,128)(2,1)S(1)} %collective-permute-done.1, bf16[384,1024]{1,0:T(8,128)(2,1)S(1)} %get-tuple-element.41), kind=kOutput, calls=%fused_computation.25 | convolution fusion | flops 1212481536 | bytes 3148800 | tf_op jit(solution)/shard_map/dot_general | solution.py:17
  17.6 9.4 %all-to-all-start = ((bf16[32,24,1024]{2,1,0:T(8,128)(2,1)}), bf16[32,24,1024]{2,1,0:T(8,128)(2,1)S(1)}, u32[]{:S(2)}, u32[]{:S(2)}) async-start(bf16[32,24,1024]{2,1,0:T(8,128)(2,1)} %bitcast.48), calls=%async_computation | async-start | bytes 3145728 | tf_op jit(solution)/shard_map/all_to_all | solution.py:79
  29.0 1.5 collective-permute-start.3
  34.2 29.9 %collective-permute-done.6 = f32[384]{0:T(512)S(1)} collective-permute-done((f32[384]{0:T(512)S(1)}, f32[384]{0:T(512)S(1)}, u32[]{:S(2)}, u32[]{:S(2)}) %collective-permute-start.6) | collective-permute-done | bytes 1568 | tf_op jit(solution)/shard_map/ppermute | solution.py:13
  64.1 1.8 collective-permute-start.7
  66.0 2.6 %fusion.22 = bf16[768,1024]{1,0:T(8,128)(2,1)} fusion(s32[768]{0:T(1024)S(1)} %pad_add_fusion, s32[768]{0:T(1024)S(1)} %iota_add_fusion, bf16[384,1024]{1,0:T(8,128)(2,1)S(1)} %copy-done.17, bf16[384,1024]{1,0:T(8,128)(2,1)S(1)} %copy-done.6), kind=kOutput, calls=%fused_computation.26 | convolution fusion | flops 1212481536 | bytes 3151872 | tf_op jit(solution)/shard_map/dot_general | solution.py:17
  68.6 6.1 %all-to-all-done = bf16[32,24,1024]{2,1,0:T(8,128)(2,1)S(1)} async-done(((bf16[32,24,1024]{2,1,0:T(8,128)(2,1)}), bf16[32,24,1024]{2,1,0:T(8,128)(2,1)S(1)}, u32[]{:S(2)}, u32[]{:S(2)}) %all-to-all-start) | async-done | bytes 1572896 | tf_op jit(solution)/shard_map/all_to_all | solution.py:79
  75.9 6.6 %all-to-all-start.1 = ((bf16[32,24,1024]{2,1,0:T(8,128)(2,1)}), bf16[32,24,1024]{2,1,0:T(8,128)(2,1)S(1)}, u32[]{:S(2)}, u32[]{:S(2)}) async-start(bf16[32,24,1024]{2,1,0:T(8,128)(2,1)} %bitcast), calls=%async_computation.1 | async-start | bytes 3145728 | tf_op jit(solution)/shard_map/all_to_all | solution.py:79
  82.6 3.1 %fusion.47 = f32[768,256]{1,0:T(8,128)} fusion(bf16[768,1024]{1,0:T(8,128)(2,1)} %bitcast.47, bf16[1024,256]{1,0:T(8,128)(2,1)} %collective-permute-done.7, pred[]{:T(512)S(6)} %eq.28, bf16[2048,256]{1,0:T(8,128)(2,1)S(1)} %fusion.20), kind=kOutput, calls=%fused_computation.62 | convolution fusion | flops 403177472 | bytes 3932161 | tf_op jit(solution)/shard_map/dot_general | solution.py:17
  91.2 2.7 %collective-permute-start.11 = (f32[96,256]{1,0:T(8,128)}, f32[96,256]{1,0:T(8,128)}, u32[]{:S(2)}, u32[]{:S(2)}) collective-permute-start(f32[96,256]{1,0:T(8,128)} %get-tuple-element.59), channel_id=1, source_target_pairs={{0,3},{1,0},{2,1},{3,2},{4,7},{5,4},{6,5},{7,6},{8,11},{9,8},{10,9... | collective-permute-start | bytes 294920 | tf_op jit(solution)/shard_map/ppermute | solution.py:13
  96.3 1.7 collective-permute-done.11
  99.4 2.9 %collective-permute-done.9 = f32[96,256]{1,0:T(8,128)} collective-permute-done((f32[96,256]{1,0:T(8,128)}, f32[96,256]{1,0:T(8,128)}, u32[]{:S(2)}, u32[]{:S(2)}) %collective-permute-start.9) | collective-permute-done | bytes 98336 | tf_op jit(solution)/shard_map/ppermute | solution.py:13
  106.1 2.8 %collective-permute-start.18 = (bf16[192,2048]{1,0:T(8,128)(2,1)S(1)}, bf16[192,2048]{1,0:T(8,128)(2,1)}, u32[]{:S(2)}, u32[]{:S(2)}) collective-permute-start(bf16[192,2048]{1,0:T(8,128)(2,1)S(1)} %slice.61), channel_id=1, source_target_pairs={{0,3},{1,0},{2,1},{3,2},{4,7},{5,4},{6,5},{7,6},{8,11},{9,8},{10,9... | collective-permute-start | bytes 2359304 | tf_op jit(solution)/shard_map/ppermute | solution.py:13
  110.3 15.8 %collective-permute-done.13 = bf16[96,256]{1,0:T(8,128)(2,1)S(1)} collective-permute-done((bf16[96,256]{1,0:T(8,128)(2,1)S(1)}, bf16[96,256]{1,0:T(8,128)(2,1)S(1)}, u32[]{:S(2)}, u32[]{:S(2)}) %collective-permute-start.13) | collective-permute-done | bytes 49184 | tf_op jit(solution)/shard_map/ppermute | solution.py:13
  126.7 2.0 collective-permute-start.15
  132.4 6.1 %all-to-all-done.1 = bf16[32,24,1024]{2,1,0:T(8,128)(2,1)S(1)} async-done(((bf16[32,24,1024]{2,1,0:T(8,128)(2,1)}), bf16[32,24,1024]{2,1,0:T(8,128)(2,1)S(1)}, u32[]{:S(2)}, u32[]{:S(2)}) %all-to-all-start.1) | async-done | bytes 1572896 | tf_op jit(solution)/shard_map/all_to_all | solution.py:79
  139.1 3.5 %collective-permute-start.19 = (f32[384,256]{1,0:T(8,128)S(1)}, f32[384,256]{1,0:T(8,128)S(1)}, u32[]{:S(2)}, u32[]{:S(2)}) collective-permute-start(f32[384,256]{1,0:T(8,128)S(1)} %constant_dynamic-slice_fusion.3), channel_id=1, source_target_pairs={{0,4},{4,0},{1,5},{5,1},{2,6},{6,2},{3,7},{7,3},{8,12},{12,8},{9,1... | collective-permute-start | bytes 1179656 | tf_op jit(solution)/shard_map/ppermute | solution.py:43
  142.6 4.7 %all-to-all-start.2 = ((bf16[32,24,512]{2,1,0:T(8,128)(2,1)}), bf16[32,24,512]{2,1,0:T(8,128)(2,1)S(1)}, u32[]{:S(2)}, u32[]{:S(2)}) async-start(bf16[32,24,512]{2,1,0:T(8,128)(2,1)} %bitcast.8), calls=%async_computation.2 | async-start | bytes 1572864 | tf_op jit(solution)/shard_map/all_to_all | solution.py:79
  147.4 2.9 %collective-permute-start.22 = (f32[96,256]{1,0:T(8,128)S(1)}, f32[96,256]{1,0:T(8,128)S(1)}, u32[]{:S(2)}, u32[]{:S(2)}) collective-permute-start(f32[96,256]{1,0:T(8,128)S(1)} %get-tuple-element.54), channel_id=1, source_target_pairs={{0,3},{1,0},{2,1},{3,2},{4,7},{5,4},{6,5},{7,6},{8,11},{9,8},{10,9... | collective-permute-start | bytes 294920 | tf_op jit(solution)/shard_map/ppermute | solution.py:13
  151.3 2.8 %collective-permute-done.22 = f32[96,256]{1,0:T(8,128)S(1)} collective-permute-done((f32[96,256]{1,0:T(8,128)S(1)}, f32[96,256]{1,0:T(8,128)S(1)}, u32[]{:S(2)}, u32[]{:S(2)}) %collective-permute-start.22) | collective-permute-done | bytes 98336 | tf_op jit(solution)/shard_map/ppermute | solution.py:13
  155.5 3.1 %collective-permute-done.20 = f32[96,256]{1,0:T(8,128)S(1)} collective-permute-done((f32[96,256]{1,0:T(8,128)S(1)}, f32[96,256]{1,0:T(8,128)S(1)}, u32[]{:S(2)}, u32[]{:S(2)}) %collective-permute-start.20) | collective-permute-done | bytes 98336 | tf_op jit(solution)/shard_map/ppermute | solution.py:13
  159.3 2.1 collective-permute-start.25
  161.4 2.4 %collective-permute-done.23 = bf16[96,256]{1,0:T(8,128)(2,1)S(1)} collective-permute-done((bf16[96,256]{1,0:T(8,128)(2,1)S(1)}, bf16[96,256]{1,0:T(8,128)(2,1)S(1)}, u32[]{:S(2)}, u32[]{:S(2)}) %collective-permute-start.23) | collective-permute-done | bytes 49184 | tf_op jit(solution)/shard_map/ppermute | solution.py:13
  168.2 6.5 %all-to-all-done.2 = bf16[32,24,512]{2,1,0:T(8,128)(2,1)S(1)} async-done(((bf16[32,24,512]{2,1,0:T(8,128)(2,1)}), bf16[32,24,512]{2,1,0:T(8,128)(2,1)S(1)}, u32[]{:S(2)}, u32[]{:S(2)}) %all-to-all-start.2) | async-done | bytes 786464 | tf_op jit(solution)/shard_map/all_to_all | solution.py:79
  174.7 4.9 %all-to-all-start.3 = ((bf16[32,24,512]{2,1,0:T(8,128)(2,1)}), bf16[32,24,512]{2,1,0:T(8,128)(2,1)S(1)}, u32[]{:S(2)}, u32[]{:S(2)}) async-start(bf16[32,24,512]{2,1,0:T(8,128)(2,1)} %bitcast.12), calls=%async_computation.3 | async-start | bytes 1572864 | tf_op jit(solution)/shard_map/all_to_all | solution.py:79
  179.7 4.6 %fusion.2 = f32[384,1024]{1,0:T(8,128)S(1)} fusion(bf16[384,2048]{1,0:T(8,128)(2,1)} %collective-permute-done.3, bf16[4,2048,1024]{2,1,0:T(8,128)(2,1)} %bitcast.51, u32[]{:T(128)S(6)} %rem.56), kind=kOutput, calls=%fused_computation.2 | convolution fusion | flops 1610612736 | bytes 7340036 | tf_op jit(solution)/shard_map/dot_general | solution.py:17
  184.3 5.2 %fusion.4 = f32[384,1024]{1,0:T(8,128)S(1)} fusion(bf16[384,2048]{1,0:T(8,128)(2,1)} %collective-permute-done.2, bf16[4,2048,1024]{2,1,0:T(8,128)(2,1)} %bitcast.52, u32[]{:T(128)S(6)} %rem.58), kind=kOutput, calls=%fused_computation.4 | convolution fusion | flops 1610612736 | bytes 7340036 | tf_op jit(solution)/shard_map/dot_general | solution.py:17
  189.6 1.8 fusion.6
  191.4 3.0 %add_add_fusion = f32[384,1024]{1,0:T(8,128)S(1)} fusion(f32[384,1024]{1,0:T(8,128)S(1)} %fusion.2, f32[384,1024]{1,0:T(8,128)S(1)} %fusion.6, f32[384,1024]{1,0:T(8,128)S(1)} %fusion.4, bf16[4,2048,1024]{2,1,0:T(8,128)(2,1)S(1)} %bitcast.54, u32[]{:T(128)S(6)} %rem.57, bf16[192,2048]{1,0:T(8,128)(2,1)} %collective-permute-done.18, ...), kind=kOutput, calls=%fused_computation.32 | convolution fusion | flops 1614938112 | bytes 12058628 | tf_op jit(solution)/shard_map/dot_general | solution.py:17
  194.4 6.3 %all-to-all-done.3 = bf16[32,24,512]{2,1,0:T(8,128)(2,1)S(1)} async-done(((bf16[32,24,512]{2,1,0:T(8,128)(2,1)}), bf16[32,24,512]{2,1,0:T(8,128)(2,1)S(1)}, u32[]{:S(2)}, u32[]{:S(2)}) %all-to-all-start.3) | async-done | bytes 786464 | tf_op jit(solution)/shard_map/all_to_all | solution.py:79
  202.6 3.0 %collective-permute-start.27 = (bf16[384,512]{1,0:T(8,128)(2,1)S(1)}, bf16[384,512]{1,0:T(8,128)(2,1)S(1)}, u32[]{:S(2)}, u32[]{:S(2)}) collective-permute-start(bf16[384,512]{1,0:T(8,128)(2,1)S(1)} %slice.79), channel_id=1, source_target_pairs={{0,4},{4,0},{1,5},{5,1},{2,6},{6,2},{3,7},{7,3},{8,12},{12,8},{9,1... | collective-permute-start | bytes 1179656 | tf_op jit(solution)/shard_map/ppermute | solution.py:43
  (123 shorter events, 43.5 us)
Async XLA Ops:
  6.5 173.2 %all-gather.2.cloned.1.call-start = ((), (), s32[]{:S(2)}) async-start(), calls=%async_computation.4 | async-start | bytes 17039360 | tf_op jit(solution)/shard_map/all_gather | solution.py:54
  8.1 5.2 %collective-permute-start.1 = (bf16[384,1024]{1,0:T(8,128)(2,1)S(1)}, bf16[384,1024]{1,0:T(8,128)(2,1)S(1)}, u32[]{:S(2)}, u32[]{:S(2)}) collective-permute-start(bf16[384,1024]{1,0:T(8,128)(2,1)S(1)} %get-tuple-element.42), channel_id=1, source_target_pairs={{0,4},{4,0},{1,5},{5,1},{2,6},{6,2},{3,7},{7,3},{8,12},{12,8},{9,1... | collective-permute-start | bytes 2359304 | tf_op jit(solution)/shard_map/ppermute | solution.py:43
  17.6 57.1 %all-to-all-start = ((bf16[32,24,1024]{2,1,0:T(8,128)(2,1)}), bf16[32,24,1024]{2,1,0:T(8,128)(2,1)S(1)}, u32[]{:S(2)}, u32[]{:S(2)}) async-start(bf16[32,24,1024]{2,1,0:T(8,128)(2,1)} %bitcast.48), calls=%async_computation | async-start | bytes 3145728 | tf_op jit(solution)/shard_map/all_to_all | solution.py:79
  27.6 41.0 %collective-permute-start.2 = (bf16[384,2048]{1,0:T(8,128)(2,1)S(1)}, bf16[384,2048]{1,0:T(8,128)(2,1)}, u32[]{:S(2)}, u32[]{:S(2)}) collective-permute-start(bf16[384,2048]{1,0:T(8,128)(2,1)S(1)} %get-tuple-element.40), channel_id=1, source_target_pairs={{0,1},{1,2},{2,3},{3,0},{4,5},{5,6},{6,7},{7,4},{8,9},{9,10},{10,1... | collective-permute-start | bytes 4718600 | tf_op jit(solution)/shard_map/ppermute | solution.py:13
  29.0 39.6 %collective-permute-start.3 = (bf16[384,2048]{1,0:T(8,128)(2,1)S(1)}, bf16[384,2048]{1,0:T(8,128)(2,1)}, u32[]{:S(2)}, u32[]{:S(2)}) collective-permute-start(bf16[384,2048]{1,0:T(8,128)(2,1)S(1)} %get-tuple-element.40), channel_id=1, source_target_pairs={{0,3},{1,0},{2,1},{3,2},{4,7},{5,4},{6,5},{7,6},{8,11},{9,8},{10,9... | collective-permute-start | bytes 4718600 | tf_op jit(solution)/shard_map/ppermute | solution.py:13
  30.5 33.6 %collective-permute-start.6 = (f32[384]{0:T(512)S(1)}, f32[384]{0:T(512)S(1)}, u32[]{:S(2)}, u32[]{:S(2)}) collective-permute-start(f32[384]{0:T(512)S(1)} %get-tuple-element.39), channel_id=1, source_target_pairs={{0,3},{1,0},{2,1},{3,2},{4,7},{5,4},{6,5},{7,6},{8,11},{9,8},{10,9... | collective-permute-start | bytes 4616 | tf_op jit(solution)/shard_map/ppermute | solution.py:13
  31.9 34.1 %collective-permute-start.5 = (f32[384]{0:T(512)S(1)}, f32[384]{0:T(512)S(1)}, u32[]{:S(2)}, u32[]{:S(2)}) collective-permute-start(f32[384]{0:T(512)S(1)} %get-tuple-element.39), channel_id=1, source_target_pairs={{0,2},{1,3},{2,0},{3,1},{4,6},{5,7},{6,4},{7,5},{8,10},{9,11},{10,... | collective-permute-start | bytes 4616 | tf_op jit(solution)/shard_map/ppermute | solution.py:13
  32.2 33.7 %collective-permute-start.4 = (f32[384]{0:T(512)S(1)}, f32[384]{0:T(512)S(1)}, u32[]{:S(2)}, u32[]{:S(2)}) collective-permute-start(f32[384]{0:T(512)S(1)} %get-tuple-element.39), channel_id=1, source_target_pairs={{0,1},{1,2},{2,3},{3,0},{4,5},{5,6},{6,7},{7,4},{8,9},{9,10},{10,1... | collective-permute-start | bytes 4616 | tf_op jit(solution)/shard_map/ppermute | solution.py:13
  64.1 18.4 %collective-permute-start.7 = (bf16[1024,256]{1,0:T(8,128)(2,1)}, bf16[1024,256]{1,0:T(8,128)(2,1)}, u32[]{:S(2)}, u32[]{:S(2)}) collective-permute-start(bf16[1024,256]{1,0:T(8,128)(2,1)} %broadcast_select_fusion.2), channel_id=1, source_target_pairs={{0,4},{4,0},{1,5},{5,1},{2,6},{6,2},{3,7},{7,3},{8,12},{12,8},{9,1... | collective-permute-start | bytes 1572872 | tf_op jit(solution)/shard_map/ppermute | solution.py:43
  75.9 62.6 %all-to-all-start.1 = ((bf16[32,24,1024]{2,1,0:T(8,128)(2,1)}), bf16[32,24,1024]{2,1,0:T(8,128)(2,1)S(1)}, u32[]{:S(2)}, u32[]{:S(2)}) async-start(bf16[32,24,1024]{2,1,0:T(8,128)(2,1)} %bitcast), calls=%async_computation.1 | async-start | bytes 3145728 | tf_op jit(solution)/shard_map/all_to_all | solution.py:79
  86.7 2.7 %collective-permute-start.8 = (f32[384,256]{1,0:T(8,128)S(1)}, f32[384,256]{1,0:T(8,128)S(1)}, u32[]{:S(2)}, u32[]{:S(2)}) collective-permute-start(f32[384,256]{1,0:T(8,128)S(1)} %constant_dynamic-slice_fusion.7), channel_id=1, source_target_pairs={{0,4},{4,0},{1,5},{5,1},{2,6},{6,2},{3,7},{7,3},{8,12},{12,8},{9,1... | collective-permute-start | bytes 1179656 | tf_op jit(solution)/shard_map/ppermute | solution.py:43
  91.2 6.7 %collective-permute-start.11 = (f32[96,256]{1,0:T(8,128)}, f32[96,256]{1,0:T(8,128)}, u32[]{:S(2)}, u32[]{:S(2)}) collective-permute-start(f32[96,256]{1,0:T(8,128)} %get-tuple-element.59), channel_id=1, source_target_pairs={{0,3},{1,0},{2,1},{3,2},{4,7},{5,4},{6,5},{7,6},{8,11},{9,8},{10,9... | collective-permute-start | bytes 294920 | tf_op jit(solution)/shard_map/ppermute | solution.py:13
  93.9 5.5 %collective-permute-start.10 = (f32[96,256]{1,0:T(8,128)}, f32[96,256]{1,0:T(8,128)}, u32[]{:S(2)}, u32[]{:S(2)}) collective-permute-start(f32[96,256]{1,0:T(8,128)} %get-tuple-element.60), channel_id=1, source_target_pairs={{0,2},{1,3},{2,0},{3,1},{4,6},{5,7},{6,4},{7,5},{8,10},{9,11},{10,... | collective-permute-start | bytes 294920 | tf_op jit(solution)/shard_map/ppermute | solution.py:13
  94.3 8.0 %collective-permute-start.9 = (f32[96,256]{1,0:T(8,128)}, f32[96,256]{1,0:T(8,128)}, u32[]{:S(2)}, u32[]{:S(2)}) collective-permute-start(f32[96,256]{1,0:T(8,128)} %get-tuple-element.58), channel_id=1, source_target_pairs={{0,1},{1,2},{2,3},{3,0},{4,5},{5,6},{6,7},{7,4},{8,9},{9,10},{10,1... | collective-permute-start | bytes 294920 | tf_op jit(solution)/shard_map/ppermute | solution.py:13
  95.0 8.5 %collective-permute-start.16 = (bf16[2,128,256]{2,1,0:T(8,128)(2,1)S(1)}, bf16[2,128,256]{2,1,0:T(8,128)(2,1)S(1)}, u32[]{:S(2)}, u32[]{:S(2)}) collective-permute-start(bf16[2,128,256]{2,1,0:T(8,128)(2,1)S(1)} %dynamic-slice_bitcast_fusion), channel_id=1, source_target_pairs={{0,4},{4,0},{1,5},{5,1},{2,6},{6,2},{3,7},{7,3},{8,12},{12,8},{9,1... | collective-permute-start | bytes 393224 | tf_op jit(solution)/shard_map/ppermute | solution.py:43
  103.4 6.9 %collective-permute-start.12 = (bf16[96,256]{1,0:T(8,128)(2,1)S(1)}, bf16[96,256]{1,0:T(8,128)(2,1)S(1)}, u32[]{:S(2)}, u32[]{:S(2)}) collective-permute-start(bf16[96,256]{1,0:T(8,128)(2,1)S(1)} %get-tuple-element.38), channel_id=1, source_target_pairs={{0,1},{1,2},{2,3},{3,0},{4,5},{5,6},{6,7},{7,4},{8,9},{9,10},{10,1... | collective-permute-start | bytes 147464 | tf_op jit(solution)/shard_map/ppermute | solution.py:13
  104.8 26.6 %collective-permute-start.17 = (bf16[192,2048]{1,0:T(8,128)(2,1)S(1)}, bf16[192,2048]{1,0:T(8,128)(2,1)S(1)}, u32[]{:S(2)}, u32[]{:S(2)}) collective-permute-start(bf16[192,2048]{1,0:T(8,128)(2,1)S(1)} %slice.60), channel_id=1, source_target_pairs={{0,1},{1,2},{2,3},{3,0},{4,5},{5,6},{6,7},{7,4},{8,9},{9,10},{10,1... | collective-permute-start | bytes 2359304 | tf_op jit(solution)/shard_map/ppermute | solution.py:13
  106.1 26.3 %collective-permute-start.18 = (bf16[192,2048]{1,0:T(8,128)(2,1)S(1)}, bf16[192,2048]{1,0:T(8,128)(2,1)}, u32[]{:S(2)}, u32[]{:S(2)}) collective-permute-start(bf16[192,2048]{1,0:T(8,128)(2,1)S(1)} %slice.61), channel_id=1, source_target_pairs={{0,3},{1,0},{2,1},{3,2},{4,7},{5,4},{6,5},{7,6},{8,11},{9,8},{10,9... | collective-permute-start | bytes 2359304 | tf_op jit(solution)/shard_map/ppermute | solution.py:13
  108.9 17.2 %collective-permute-start.13 = (bf16[96,256]{1,0:T(8,128)(2,1)S(1)}, bf16[96,256]{1,0:T(8,128)(2,1)S(1)}, u32[]{:S(2)}, u32[]{:S(2)}) collective-permute-start(bf16[96,256]{1,0:T(8,128)(2,1)S(1)} %get-tuple-element.38), channel_id=1, source_target_pairs={{0,2},{1,3},{2,0},{3,1},{4,6},{5,7},{6,4},{7,5},{8,10},{9,11},{10,... | collective-permute-start | bytes 147464 | tf_op jit(solution)/shard_map/ppermute | solution.py:13
  110.1 16.6 %collective-permute-start.14 = (bf16[96,256]{1,0:T(8,128)(2,1)S(1)}, bf16[96,256]{1,0:T(8,128)(2,1)S(1)}, u32[]{:S(2)}, u32[]{:S(2)}) collective-permute-start(bf16[96,256]{1,0:T(8,128)(2,1)S(1)} %get-tuple-element.38), channel_id=1, source_target_pairs={{0,3},{1,0},{2,1},{3,2},{4,7},{5,4},{6,5},{7,6},{8,11},{9,8},{10,9... | collective-permute-start | bytes 147464 | tf_op jit(solution)/shard_map/ppermute | solution.py:13
  126.7 3.4 %collective-permute-start.15 = (bf16[384,256]{1,0:T(8,128)(2,1)S(1)}, bf16[384,256]{1,0:T(8,128)(2,1)S(1)}, u32[]{:S(2)}, u32[]{:S(2)}) collective-permute-start(bf16[384,256]{1,0:T(8,128)(2,1)S(1)} %constant_dynamic-update-slice_fusion.4), channel_id=1, source_target_pairs={{0,4},{4,0},{1,5},{5,1},{2,6},{6,2},{3,7},{7,3},{8,12},{12,8},{9,1... | collective-permute-start | bytes 589832 | tf_op jit(solution)/shard_map/ppermute | solution.py:43
  139.1 8.2 %collective-permute-start.19 = (f32[384,256]{1,0:T(8,128)S(1)}, f32[384,256]{1,0:T(8,128)S(1)}, u32[]{:S(2)}, u32[]{:S(2)}) collective-permute-start(f32[384,256]{1,0:T(8,128)S(1)} %constant_dynamic-slice_fusion.3), channel_id=1, source_target_pairs={{0,4},{4,0},{1,5},{5,1},{2,6},{6,2},{3,7},{7,3},{8,12},{12,8},{9,1... | collective-permute-start | bytes 1179656 | tf_op jit(solution)/shard_map/ppermute | solution.py:43
  142.6 32.1 %all-to-all-start.2 = ((bf16[32,24,512]{2,1,0:T(8,128)(2,1)}), bf16[32,24,512]{2,1,0:T(8,128)(2,1)S(1)}, u32[]{:S(2)}, u32[]{:S(2)}) async-start(bf16[32,24,512]{2,1,0:T(8,128)(2,1)} %bitcast.8), calls=%async_computation.2 | async-start | bytes 1572864 | tf_op jit(solution)/shard_map/all_to_all | solution.py:79
  147.4 6.7 %collective-permute-start.22 = (f32[96,256]{1,0:T(8,128)S(1)}, f32[96,256]{1,0:T(8,128)S(1)}, u32[]{:S(2)}, u32[]{:S(2)}) collective-permute-start(f32[96,256]{1,0:T(8,128)S(1)} %get-tuple-element.54), channel_id=1, source_target_pairs={{0,3},{1,0},{2,1},{3,2},{4,7},{5,4},{6,5},{7,6},{8,11},{9,8},{10,9... | collective-permute-start | bytes 294920 | tf_op jit(solution)/shard_map/ppermute | solution.py:13
  150.2 5.3 %collective-permute-start.21 = (f32[96,256]{1,0:T(8,128)S(1)}, f32[96,256]{1,0:T(8,128)S(1)}, u32[]{:S(2)}, u32[]{:S(2)}) collective-permute-start(f32[96,256]{1,0:T(8,128)S(1)} %get-tuple-element.55), channel_id=1, source_target_pairs={{0,2},{1,3},{2,0},{3,1},{4,6},{5,7},{6,4},{7,5},{8,10},{9,11},{10,... | collective-permute-start | bytes 294920 | tf_op jit(solution)/shard_map/ppermute | solution.py:13
  150.6 8.0 %collective-permute-start.20 = (f32[96,256]{1,0:T(8,128)S(1)}, f32[96,256]{1,0:T(8,128)S(1)}, u32[]{:S(2)}, u32[]{:S(2)}) collective-permute-start(f32[96,256]{1,0:T(8,128)S(1)} %get-tuple-element.53), channel_id=1, source_target_pairs={{0,1},{1,2},{2,3},{3,0},{4,5},{5,6},{6,7},{7,4},{8,9},{9,10},{10,1... | collective-permute-start | bytes 294920 | tf_op jit(solution)/shard_map/ppermute | solution.py:13
  158.7 5.2 %collective-permute-start.23 = (bf16[96,256]{1,0:T(8,128)(2,1)S(1)}, bf16[96,256]{1,0:T(8,128)(2,1)S(1)}, u32[]{:S(2)}, u32[]{:S(2)}) collective-permute-start(bf16[96,256]{1,0:T(8,128)(2,1)S(1)} %get-tuple-element.36), channel_id=1, source_target_pairs={{0,1},{1,2},{2,3},{3,0},{4,5},{5,6},{6,7},{7,4},{8,9},{9,10},{10,1... | collective-permute-start | bytes 147464 | tf_op jit(solution)/shard_map/ppermute | solution.py:13
  158.8 5.1 %collective-permute-start.24 = (bf16[96,256]{1,0:T(8,128)(2,1)S(1)}, bf16[96,256]{1,0:T(8,128)(2,1)S(1)}, u32[]{:S(2)}, u32[]{:S(2)}) collective-permute-start(bf16[96,256]{1,0:T(8,128)(2,1)S(1)} %get-tuple-element.36), channel_id=1, source_target_pairs={{0,2},{1,3},{2,0},{3,1},{4,6},{5,7},{6,4},{7,5},{8,10},{9,11},{10,... | collective-permute-start | bytes 147464 | tf_op jit(solution)/shard_map/ppermute | solution.py:13
  159.3 5.1 %collective-permute-start.25 = (bf16[96,256]{1,0:T(8,128)(2,1)S(1)}, bf16[96,256]{1,0:T(8,128)(2,1)S(1)}, u32[]{:S(2)}, u32[]{:S(2)}) collective-permute-start(bf16[96,256]{1,0:T(8,128)(2,1)S(1)} %get-tuple-element.36), channel_id=1, source_target_pairs={{0,3},{1,0},{2,1},{3,2},{4,7},{5,4},{6,5},{7,6},{8,11},{9,8},{10,9... | collective-permute-start | bytes 147464 | tf_op jit(solution)/shard_map/ppermute | solution.py:13
  164.4 2.5 %collective-permute-start.26 = (bf16[384,256]{1,0:T(8,128)(2,1)S(1)}, bf16[384,256]{1,0:T(8,128)(2,1)S(1)}, u32[]{:S(2)}, u32[]{:S(2)}) collective-permute-start(bf16[384,256]{1,0:T(8,128)(2,1)S(1)} %constant_dynamic-update-slice_fusion), channel_id=1, source_target_pairs={{0,4},{4,0},{1,5},{5,1},{2,6},{6,2},{3,7},{7,3},{8,12},{12,8},{9,1... | collective-permute-start | bytes 589832 | tf_op jit(solution)/shard_map/ppermute | solution.py:43
  174.7 26.0 %all-to-all-start.3 = ((bf16[32,24,512]{2,1,0:T(8,128)(2,1)}), bf16[32,24,512]{2,1,0:T(8,128)(2,1)S(1)}, u32[]{:S(2)}, u32[]{:S(2)}) async-start(bf16[32,24,512]{2,1,0:T(8,128)(2,1)} %bitcast.12), calls=%async_computation.3 | async-start | bytes 1572864 | tf_op jit(solution)/shard_map/all_to_all | solution.py:79
  202.6 4.3 %collective-permute-start.27 = (bf16[384,512]{1,0:T(8,128)(2,1)S(1)}, bf16[384,512]{1,0:T(8,128)(2,1)S(1)}, u32[]{:S(2)}, u32[]{:S(2)}) collective-permute-start(bf16[384,512]{1,0:T(8,128)(2,1)S(1)} %slice.79), channel_id=1, source_target_pairs={{0,4},{4,0},{1,5},{5,1},{2,6},{6,2},{3,7},{7,3},{8,12},{12,8},{9,1... | collective-permute-start | bytes 1179656 | tf_op jit(solution)/shard_map/ppermute | solution.py:43
  (19 other events, 173.1 us)
Sparse Core Ops, SparseCore 0:
  13.5 156.6 all-gather.1

commit v5 on v4

--- a/solution.py
+++ b/solution.py
@@ -58,13 +58,16 @@
     at = jnp.arange(rows, dtype=jnp.int32)
     before = dot((at[:, None] > at[None, :]).astype(bf16), matches)
     place = jnp.sum(before * matches.astype(f32), axis=1).astype(jnp.int32)
-    count = chips * 2 * cap
-    own_slot = (labels % 2) * count + (labels // 2) * (2 * cap) + core * cap + place
+    count = judges * 2 * cap
+    own_slot = labels * (2 * cap) + core * cap + place
     slots = jnp.concatenate([own_slot, swap(own_slot)])
     slot_at = jnp.arange(count, dtype=jnp.int32)
-    choose = [
-        (slot_at[:, None] + b * count == slots[None, :]).astype(bf16) for b in range(2)
-    ]
+    choose = (slot_at[:, None] == slots[None, :]).astype(bf16)
+    mine_at = ((slot_at // (2 * cap)) % 2 == core)[:, None]
+
+    def pick(both_judges):
+        w = both_judges.shape[1] // 2
+        return jnp.where(mine_at, both_judges[:, :w], both_judges[:, w:])
 
     scaled_down = (down[0].astype(f32) * scale.astype(f32)[:, None]).astype(bf16)
     low, high = scaled_down[:half], scaled_down[half:]
@@ -72,14 +75,22 @@
     up_own = cut_at(up_factors[0], half_at, cols, 2)
     up_other = swap(cut_at(up_factors[0], 1 - half_at, cols, 2))
 
-    def send_out(b):
-        return dot(choose[b], both).astype(bf16).reshape(chips, 2 * cap, half)
+    nothing = jnp.zeros((rank_width, cols), bf16)
+    up_blocks = jnp.concatenate(
+        [
+            jnp.concatenate(pair, axis=1)
+            for u in (up_own, up_other)
+            for pair in ((u[0], nothing), (nothing, u[1]))
+        ],
+        axis=0,
+    )
 
     def exchange(array):
         return lax.all_to_all(array, CHIP, 0, 0, tiled=True)
 
-    def process(b, arrived):
-        partial = dot(arrived.reshape(count, half), by_core(down_own, down_other, b))
+    def process(arrived, up_blocks):
+        factors = jnp.concatenate([down_own, down_other], axis=1)
+        partial = pick(dot(arrived.reshape(count, half), factors))
         mid = count // 2
         partial = cut_at(partial, half_at, mid, 0) + swap(cut_at(partial, 1 - half_at, mid, 0))
         piece = mid // ny
@@ -95,19 +106,14 @@
             )
         other = swap(code)
         codes = jnp.concatenate([by_core(code, other, 0), by_core(code, other, 1)], axis=0)
-        factors = by_core(up_own, up_other, b)
-        nothing = jnp.zeros_like(factors[0])
-        factors = jnp.concatenate(
-            [
-                jnp.concatenate([factors[0], nothing], axis=1),
-                jnp.concatenate([nothing, factors[1]], axis=1),
-            ],
-            axis=0,
+        apart = jnp.concatenate(
+            [jnp.where(mine_at, codes, 0), jnp.where(mine_at, 0, codes)], axis=1
         )
-        deltas = dot(codes, factors).astype(bf16)
-        return deltas.reshape(chips, 2 * cap, span)
+        deltas = dot(apart, up_blocks).astype(bf16)
+        return deltas.reshape(chips, 4 * cap, span)
 
-    first = exchange(send_out(0))
+    outgoing = dot(choose, both).astype(bf16).reshape(chips, 4 * cap, half)
+    arrived = exchange(outgoing)
     wide = tokens.astype(f32)
     squares = jnp.sum(wide * wide, axis=1)
     scaled = (wide * scale.astype(f32)).astype(bf16)
@@ -116,29 +122,22 @@
     for d in range(1, ny):
         sums = sums + shift(squares, d, ny)
     factor = lax.rsqrt(sums / (width * ny) + EPSILON)
-    second, first, left, right, factor = lax.optimization_barrier(
-        (send_out(1), first, left, right, factor)
+    far = [shift(left[: rows // 2], 1, ny), shift(right[rows // 2 :], -1, ny)]
+    arrived, left, right, far, factor, up_blocks = lax.optimization_barrier(
+        (arrived, left, right, far, factor, up_blocks)
     )
-    second = exchange(second)
-    far = [shift(left[: rows // 2], 1, ny), shift(right[rows // 2 :], -1, ny)]
-    deltas = process(0, first)
-    second, deltas, far = lax.optimization_barrier((second, deltas, far))
-    returned = exchange(deltas)
-    returned, deltas = lax.optimization_barrier((returned, process(1, second)))
+    deltas = process(arrived, up_blocks)
+    deltas, scaled = lax.optimization_barrier((deltas, scaled))
     plain = None
     for array, d in ((scaled, 0), (left, -1), (right, 1), (jnp.concatenate(far, axis=0), 2)):
         term = dot(array, lax.dynamic_index_in_dim(weights, ring(d), 0, keepdims=False))
         plain = term if plain is None else plain + term
-    last, plain = lax.optimization_barrier((exchange(deltas), plain))
-    back = [returned, last]
-    by_row = sum(
-        lax.dot_general(
-            choose[b],
-            back[b].reshape(count, span),
-            (((0,), (0,)), ((), ())),
-            preferred_element_type=f32,
-        )
-        for b in range(2)
+    returned, plain = lax.optimization_barrier((exchange(deltas), plain))
+    by_row = lax.dot_general(
+        choose,
+        returned.reshape(count, span),
+        (((0,), (0,)), ((), ())),
+        preferred_element_type=f32,
     ).astype(bf16)
     here = by_row[:rows]
     there = swap(by_row[rows:])

time: 216 us -> 214 us (level)
  waiting for transfers between devices: 94.8 us -> 116 us
  starting transfers between devices: 63.9 us -> 45.6 us
  local copies, waits for them, and re-layouts: 6.79 us -> 3.44 us
    all_to_all x4 -> x2, waiting for transfers between devices: 25 us -> 57.4 us  [exchange(): return lax.all_to_all(array, CHIP, 0, 0, tiled=True)]
    ppermute x19 -> x13, waiting for transfers between devices: 62.7 us -> 52 us  [shift(): lax.ppermute(array, 'y', [(i, (i + distance) % size) for i in range(size)])]
    all_to_all x4 -> x2, starting transfers between devices: 25.7 us -> 15.4 us  [exchange(): return lax.all_to_all(array, CHIP, 0, 0, tiled=True)]
    ppermute x9 -> x7, starting transfers between devices: 18.2 us -> 11.7 us  [swap(): return lax.ppermute(array, 'c', SWAP)]
    ppermute x19 -> x13, starting transfers between devices: 20.1 us -> 18.6 us  [shift(): lax.ppermute(array, 'y', [(i, (i + distance) % size) for i in range(size)])]
    dot_general x11 -> x8, matrix products: 26.3 us -> 25 us  [dot(): return jnp.dot(a, b, preferred_element_type=jnp.float32)]
    ppermute x9 -> x7, waiting for transfers between devices: 7.08 us -> 6.86 us  [swap(): return lax.ppermute(array, 'c', SWAP)]
  transfers between devices with their start and end apart: 33 -> 23, of which waited for: 21 -> 15; matrix products, arithmetic and copies ran while one was open for 17% -> 15% of each run, Pallas kernels for 0% -> 0%
where the time goes in v5:
time: 214 us
  waiting for transfers between devices  116 us (54%)
  starting transfers between devices  45.6 us (21%)
  matrix products  26.4 us (12%)
  between operations  13.7 us (6%)
  other arithmetic  8.08 us (4%)
  local copies, waits for them, and re-layouts  3.44 us (2%)
    all_to_all x2, waiting for transfers between devices, exchange(): return lax.all_to_all(array, CHIP, 0, 0, tiled=True)  57.4 us
    ppermute x13, waiting for transfers between devices, shift(): lax.ppermute(array, 'y', [(i, (i + distance) % size) for i in range(size)])  52 us
    dot_general x8, matrix products, dot(): return jnp.dot(a, b, preferred_element_type=jnp.float32)  25 us
    ppermute x13, starting transfers between devices, shift(): lax.ppermute(array, 'y', [(i, (i + distance) % size) for i in range(size)])  18.6 us
    all_to_all x2, starting transfers between devices, exchange(): return lax.all_to_all(array, CHIP, 0, 0, tiled=True)  15.4 us
    ppermute x7, starting transfers between devices, swap(): return lax.ppermute(array, 'c', SWAP)  11.7 us
    ppermute x7, waiting for transfers between devices, swap(): return lax.ppermute(array, 'c', SWAP)  6.86 us
  transfers between devices with their start and end apart: 23, of which 15 were waited for; matrix products, arithmetic and copies ran while one was open for 15% of the time, Pallas kernels for 0%

profile of v5, /device:TPU:1, one launch (start us, length us, event | category | flops | bytes accessed | tf_op | source)
XLA Modules:
  0.0 213.6 jit_solution(454849485164968599)
XLA Ops:
  6.5 1.5 broadcast_select_fusion.3
  8.1 3.3 %collective-permute-start.1 = (bf16[384,1024]{1,0:T(8,128)(2,1)S(1)}, bf16[384,1024]{1,0:T(8,128)(2,1)S(1)}, u32[]{:S(2)}, u32[]{:S(2)}) collective-permute-start(bf16[384,1024]{1,0:T(8,128)(2,1)S(1)} %get-tuple-element.36), channel_id=1, source_target_pairs={{0,4},{4,0},{1,5},{5,1},{2,6},{6,2},{3,7},{7,3},{8,12},{12,8},{9,1... | collective-permute-start | bytes 2359304 | tf_op jit(solution)/shard_map/ppermute | solution.py:43
  14.9 4.0 %fusion.14 = bf16[1536,1024]{1,0:T(8,128)(2,1)} fusion(s32[768]{0:T(1024)S(1)} %pad_add_fusion, bf16[384,1024]{1,0:T(8,128)(2,1)S(1)} %collective-permute-done.1, bf16[384,1024]{1,0:T(8,128)(2,1)S(1)} %get-tuple-element.35), kind=kOutput, calls=%fused_computation.17 | convolution fusion | flops 2421817344 | bytes 4721664 | tf_op jit(solution)/shard_map/dot_general | solution.py:17
  18.9 9.5 %all-to-all-start = ((bf16[32,48,1024]{2,1,0:T(8,128)(2,1)}), bf16[32,48,1024]{2,1,0:T(8,128)(2,1)}, u32[]{:S(2)}, u32[]{:S(2)}) async-start(bf16[32,48,1024]{2,1,0:T(8,128)(2,1)} %bitcast.38), calls=%async_computation | async-start | bytes 6291456 | tf_op jit(solution)/shard_map/all_to_all | solution.py:89
  29.0 1.4 collective-permute-start.2
  30.4 1.5 collective-permute-start.3
  31.9 2.6 %collective-permute-start.7 = (f32[384]{0:T(512)S(1)}, f32[384]{0:T(512)}, u32[]{:S(2)}, u32[]{:S(2)}) collective-permute-start(f32[384]{0:T(512)S(1)} %get-tuple-element.33), channel_id=1, source_target_pairs={{0,2},{1,3},{2,0},{3,1},{4,6},{5,7},{6,4},{7,5},{8,10},{9,11},{10,... | collective-permute-start | bytes 4616 | tf_op jit(solution)/shard_map/ppermute | solution.py:13
  35.6 1.6 fusion.19
  37.3 28.6 %collective-permute-done.2 = bf16[384,2048]{1,0:T(8,128)(2,1)} collective-permute-done((bf16[384,2048]{1,0:T(8,128)(2,1)S(1)}, bf16[384,2048]{1,0:T(8,128)(2,1)}, u32[]{:S(2)}, u32[]{:S(2)}) %collective-permute-start.2) | collective-permute-done | bytes 1572896 | tf_op jit(solution)/shard_map/ppermute | solution.py:13
  68.4 2.7 %collective-permute-start.5 = (bf16[192,2048]{1,0:T(8,128)(2,1)S(1)}, bf16[192,2048]{1,0:T(8,128)(2,1)}, u32[]{:S(2)}, u32[]{:S(2)}) collective-permute-start(bf16[192,2048]{1,0:T(8,128)(2,1)S(1)} %slice.83), channel_id=1, source_target_pairs={{0,3},{1,0},{2,1},{3,2},{4,7},{5,4},{6,5},{7,6},{8,11},{9,8},{10,9... | collective-permute-start | bytes 2359304 | tf_op jit(solution)/shard_map/ppermute | solution.py:13
  71.2 2.1 collective-permute-start.9
  75.1 10.9 %collective-permute-done.4 = bf16[192,2048]{1,0:T(8,128)(2,1)} collective-permute-done((bf16[192,2048]{1,0:T(8,128)(2,1)S(1)}, bf16[192,2048]{1,0:T(8,128)(2,1)}, u32[]{:S(2)}, u32[]{:S(2)}) %collective-permute-start.4) | collective-permute-done | bytes 786464 | tf_op jit(solution)/shard_map/ppermute | solution.py:13
  86.3 34.7 %all-to-all-done = bf16[32,48,1024]{2,1,0:T(8,128)(2,1)} async-done(((bf16[32,48,1024]{2,1,0:T(8,128)(2,1)}), bf16[32,48,1024]{2,1,0:T(8,128)(2,1)}, u32[]{:S(2)}, u32[]{:S(2)}) %all-to-all-start) | async-done | bytes 3145760 | tf_op jit(solution)/shard_map/all_to_all | solution.py:89
  121.0 3.7 %fusion.31 = f32[1536,512]{1,0:T(8,128)S(1)} fusion(bf16[1536,1024]{1,0:T(8,128)(2,1)} %bitcast.6, bf16[1024,256]{1,0:T(8,128)(2,1)S(1)} %collective-permute-done.10, bf16[1024,256]{1,0:T(8,128)(2,1)S(1)} %get-tuple-element.39), kind=kOutput, calls=%fused_computation.45 | convolution fusion | flops 1612709888 | bytes 7340032 | tf_op jit(solution)/shard_map/dot_general | solution.py:17
  125.0 1.9 collective-permute-start.11
  127.0 2.1 %collective-permute-done.11 = f32[768,256]{1,0:T(8,128)S(1)} collective-permute-done((f32[768,256]{1,0:T(8,128)S(1)}, f32[768,256]{1,0:T(8,128)S(1)}, u32[]{:S(2)}, u32[]{:S(2)}) %collective-permute-start.11) | collective-permute-done | bytes 786464 | tf_op jit(solution)/shard_map/ppermute | solution.py:43
  130.6 2.4 %collective-permute-start.13 = (f32[192,256]{1,0:T(8,128)S(1)}, f32[192,256]{1,0:T(8,128)S(1)}, u32[]{:S(2)}, u32[]{:S(2)}) collective-permute-start(f32[192,256]{1,0:T(8,128)S(1)} %get-tuple-element.51), channel_id=1, source_target_pairs={{0,2},{1,3},{2,0},{3,1},{4,6},{5,7},{6,4},{7,5},{8,10},{9,11},{10,... | collective-permute-start | bytes 589832 | tf_op jit(solution)/shard_map/ppermute | solution.py:13
  134.2 2.9 %collective-permute-done.12 = f32[192,256]{1,0:T(8,128)S(1)} collective-permute-done((f32[192,256]{1,0:T(8,128)S(1)}, f32[192,256]{1,0:T(8,128)S(1)}, u32[]{:S(2)}, u32[]{:S(2)}) %collective-permute-start.12) | collective-permute-done | bytes 196640 | tf_op jit(solution)/shard_map/ppermute | solution.py:13
  137.0 5.0 %collective-permute-done.13 = f32[192,256]{1,0:T(8,128)S(1)} collective-permute-done((f32[192,256]{1,0:T(8,128)S(1)}, f32[192,256]{1,0:T(8,128)S(1)}, u32[]{:S(2)}, u32[]{:S(2)}) %collective-permute-start.13) | collective-permute-done | bytes 196640 | tf_op jit(solution)/shard_map/ppermute | solution.py:13
  143.2 2.8 %collective-permute-start.16 = (bf16[192,256]{1,0:T(8,128)(2,1)S(1)}, bf16[192,256]{1,0:T(8,128)(2,1)S(1)}, u32[]{:S(2)}, u32[]{:S(2)}) collective-permute-start(bf16[192,256]{1,0:T(8,128)(2,1)S(1)} %get-tuple-element.32), channel_id=1, source_target_pairs={{0,2},{1,3},{2,0},{3,1},{4,6},{5,7},{6,4},{7,5},{8,10},{9,11},{10,... | collective-permute-start | bytes 294920 | tf_op jit(solution)/shard_map/ppermute | solution.py:13
  147.3 3.4 %collective-permute-done.16 = bf16[192,256]{1,0:T(8,128)(2,1)S(1)} collective-permute-done((bf16[192,256]{1,0:T(8,128)(2,1)S(1)}, bf16[192,256]{1,0:T(8,128)(2,1)S(1)}, u32[]{:S(2)}, u32[]{:S(2)}) %collective-permute-start.16) | collective-permute-done | bytes 98336 | tf_op jit(solution)/shard_map/ppermute | solution.py:13
  152.1 1.3 collective-permute-done.18
  154.6 2.2 %convolution_convert_fusion = bf16[1536,512]{1,0:T(8,128)(2,1)} fusion(bf16[512,512]{1,0:T(8,128)(2,1)S(1)} %copy-done.3, bf16[1536,256]{1,0:T(8,128)(2,1)S(1)} %get-tuple-element.42, bf16[1536,256]{1,0:T(8,128)(2,1)S(1)} %get-tuple-element.41), kind=kOutput, calls=%fused_computation.20 | convolution fusion | flops 809238528 | bytes 3670016 | tf_op jit(solution)/shard_map/dot_general | solution.py:17
  156.7 5.8 %all-to-all-start.1 = ((bf16[32,48,512]{2,1,0:T(8,128)(2,1)}), bf16[32,48,512]{2,1,0:T(8,128)(2,1)S(1)}, u32[]{:S(2)}, u32[]{:S(2)}) async-start(bf16[32,48,512]{2,1,0:T(8,128)(2,1)} %bitcast.8), calls=%async_computation.1 | async-start | bytes 3145728 | tf_op jit(solution)/shard_map/all_to_all | solution.py:89
  162.6 4.6 %fusion.4 = f32[384,1024]{1,0:T(8,128)S(1)} fusion(bf16[384,2048]{1,0:T(8,128)(2,1)} %collective-permute-done.3, bf16[4,2048,1024]{2,1,0:T(8,128)(2,1)} %bitcast.40, u32[]{:T(128)S(6)} %rem.58), kind=kOutput, calls=%fused_computation.5 | convolution fusion | flops 1610612736 | bytes 7340036 | tf_op jit(solution)/shard_map/dot_general | solution.py:17
  167.3 5.2 %fusion.6 = f32[384,1024]{1,0:T(8,128)S(1)} fusion(bf16[384,2048]{1,0:T(8,128)(2,1)} %collective-permute-done.2, bf16[4,2048,1024]{2,1,0:T(8,128)(2,1)} %bitcast.41, u32[]{:T(128)S(6)} %rem.60), kind=kOutput, calls=%fused_computation.7 | convolution fusion | flops 1610612736 | bytes 7340036 | tf_op jit(solution)/shard_map/dot_general | solution.py:17
  172.5 1.8 fusion.8
  174.3 3.2 %add_add_fusion = f32[384,1024]{1,0:T(8,128)S(1)} fusion(f32[384,1024]{1,0:T(8,128)S(1)} %fusion.4, f32[384,1024]{1,0:T(8,128)S(1)} %fusion.8, f32[384,1024]{1,0:T(8,128)S(1)} %fusion.6, bf16[4,2048,1024]{2,1,0:T(8,128)(2,1)S(1)} %bitcast.43, u32[]{:T(128)S(6)} %rem.59, bf16[192,2048]{1,0:T(8,128)(2,1)} %collective-permute-done.5, ...), kind=kOutput, calls=%fused_computation.39 | convolution fusion | flops 1614938112 | bytes 12058628 | tf_op jit(solution)/shard_map/dot_general | solution.py:17
  177.5 22.7 %all-to-all-done.1 = bf16[32,48,512]{2,1,0:T(8,128)(2,1)S(1)} async-done(((bf16[32,48,512]{2,1,0:T(8,128)(2,1)}), bf16[32,48,512]{2,1,0:T(8,128)(2,1)S(1)}, u32[]{:S(2)}, u32[]{:S(2)}) %all-to-all-start.1) | async-done | bytes 1572896 | tf_op jit(solution)/shard_map/all_to_all | solution.py:89
  200.2 1.4 fusion.29
  201.7 2.3 %collective-permute-start.19 = (bf16[384,512]{1,0:T(8,128)(2,1)S(1)}, bf16[384,512]{1,0:T(8,128)(2,1)S(1)}, u32[]{:S(2)}, u32[]{:S(2)}) collective-permute-start(bf16[384,512]{1,0:T(8,128)(2,1)S(1)} %slice.91), channel_id=1, source_target_pairs={{0,4},{4,0},{1,5},{5,1},{2,6},{6,2},{3,7},{7,3},{8,12},{12,8},{9,1... | collective-permute-start | bytes 1179656 | tf_op jit(solution)/shard_map/ppermute | solution.py:43
  204.0 1.3 collective-permute-done.19
  (78 shorter events, 19.1 us)
Async XLA Ops:
  6.5 156.1 %all-gather.2.cloned.1.call-start = ((), (), s32[]{:S(2)}) async-start(), calls=%async_computation.2 | async-start | bytes 17039360 | tf_op jit(solution)/shard_map/all_gather | solution.py:54
  6.5 4.9 %copy-start.7 = (bf16[128,512]{1,0:T(8,128)(2,1)S(1)}, bf16[128,512]{1,0:T(8,128)(2,1)}, u32[]{:S(2)}) copy-start(bf16[128,512]{1,0:T(8,128)(2,1)} %param.9) | copy-start | bytes 393220
  6.5 6.8 %copy-start.9 = (s32[384,1]{0,1:T(1,128)S(1)}, s32[384,1]{0,1:T(1,128)}, u32[]{:S(2)}) copy-start(s32[384,1]{0,1:T(1,128)} %param.13) | copy-start | bytes 4612
  8.1 5.2 %collective-permute-start.1 = (bf16[384,1024]{1,0:T(8,128)(2,1)S(1)}, bf16[384,1024]{1,0:T(8,128)(2,1)S(1)}, u32[]{:S(2)}, u32[]{:S(2)}) collective-permute-start(bf16[384,1024]{1,0:T(8,128)(2,1)S(1)} %get-tuple-element.36), channel_id=1, source_target_pairs={{0,4},{4,0},{1,5},{5,1},{2,6},{6,2},{3,7},{7,3},{8,12},{12,8},{9,1... | collective-permute-start | bytes 2359304 | tf_op jit(solution)/shard_map/ppermute | solution.py:43
  13.6 1.3 collective-permute-start
  18.9 9.6 %copy-start.8 = (bf16[2048]{0:T(1024)(128)(2,1)S(1)}, bf16[2048]{0:T(1024)(128)(2,1)}, u32[]{:S(2)}) copy-start(bf16[2048]{0:T(1024)(128)(2,1)} %param.8) | copy-start | bytes 12292
  18.9 9.6 %copy-start = (bf16[384,2048]{1,0:T(8,128)(2,1)S(1)}, bf16[384,2048]{1,0:T(8,128)(2,1)}, u32[]{:S(2)}) copy-start(bf16[384,2048]{1,0:T(8,128)(2,1)} %param.7) | copy-start | bytes 4718596
  18.9 102.0 %all-to-all-start = ((bf16[32,48,1024]{2,1,0:T(8,128)(2,1)}), bf16[32,48,1024]{2,1,0:T(8,128)(2,1)}, u32[]{:S(2)}, u32[]{:S(2)}) async-start(bf16[32,48,1024]{2,1,0:T(8,128)(2,1)} %bitcast.38), calls=%async_computation | async-start | bytes 6291456 | tf_op jit(solution)/shard_map/all_to_all | solution.py:89
  28.5 7.1 %copy-start.4 = (bf16[1,2,128,512]{3,2,1,0:T(8,128)(2,1)S(1)}, bf16[1,2,128,512]{3,2,1,0:T(8,128)(2,1)}, u32[]{:S(2)}) copy-start(bf16[1,2,128,512]{3,2,1,0:T(8,128)(2,1)} %param.12) | copy-start | bytes 786436
  29.0 8.2 %copy-start.1 = (bf16[384,2048]{1,0:T(8,128)(2,1)}, bf16[384,2048]{1,0:T(8,128)(2,1)S(1)}, u32[]{:S(2)}) copy-start(bf16[384,2048]{1,0:T(8,128)(2,1)S(1)} %get-tuple-element.22) | copy-start | bytes 4718596
  29.0 36.9 %collective-permute-start.2 = (bf16[384,2048]{1,0:T(8,128)(2,1)S(1)}, bf16[384,2048]{1,0:T(8,128)(2,1)}, u32[]{:S(2)}, u32[]{:S(2)}) collective-permute-start(bf16[384,2048]{1,0:T(8,128)(2,1)S(1)} %get-tuple-element.22), channel_id=1, source_target_pairs={{0,1},{1,2},{2,3},{3,0},{4,5},{5,6},{6,7},{7,4},{8,9},{9,10},{10,1... | collective-permute-start | bytes 4718600 | tf_op jit(solution)/shard_map/ppermute | solution.py:13
  30.4 36.8 %collective-permute-start.3 = (bf16[384,2048]{1,0:T(8,128)(2,1)S(1)}, bf16[384,2048]{1,0:T(8,128)(2,1)}, u32[]{:S(2)}, u32[]{:S(2)}) collective-permute-start(bf16[384,2048]{1,0:T(8,128)(2,1)S(1)} %get-tuple-element.22), channel_id=1, source_target_pairs={{0,3},{1,0},{2,1},{3,2},{4,7},{5,4},{6,5},{7,6},{8,11},{9,8},{10,9... | collective-permute-start | bytes 4718600 | tf_op jit(solution)/shard_map/ppermute | solution.py:13
  31.9 39.2 %collective-permute-start.6 = (f32[384]{0:T(512)S(1)}, f32[384]{0:T(512)}, u32[]{:S(2)}, u32[]{:S(2)}) collective-permute-start(f32[384]{0:T(512)S(1)} %get-tuple-element.33), channel_id=1, source_target_pairs={{0,1},{1,2},{2,3},{3,0},{4,5},{5,6},{6,7},{7,4},{8,9},{9,10},{10,1... | collective-permute-start | bytes 4616 | tf_op jit(solution)/shard_map/ppermute | solution.py:13
  31.9 41.3 %collective-permute-start.7 = (f32[384]{0:T(512)S(1)}, f32[384]{0:T(512)}, u32[]{:S(2)}, u32[]{:S(2)}) collective-permute-start(f32[384]{0:T(512)S(1)} %get-tuple-element.33), channel_id=1, source_target_pairs={{0,2},{1,3},{2,0},{3,1},{4,6},{5,7},{6,4},{7,5},{8,10},{9,11},{10,... | collective-permute-start | bytes 4616 | tf_op jit(solution)/shard_map/ppermute | solution.py:13
  34.5 39.1 %collective-permute-start.8 = (f32[384]{0:T(512)S(1)}, f32[384]{0:T(512)}, u32[]{:S(2)}, u32[]{:S(2)}) collective-permute-start(f32[384]{0:T(512)S(1)} %get-tuple-element.33), channel_id=1, source_target_pairs={{0,3},{1,0},{2,1},{3,2},{4,7},{5,4},{6,5},{7,6},{8,11},{9,8},{10,9... | collective-permute-start | bytes 4616 | tf_op jit(solution)/shard_map/ppermute | solution.py:13
  37.3 33.9 %copy-start.5 = (bf16[1,2,128,512]{3,2,1,0:T(8,128)(2,1)S(1)}, bf16[1,2,128,512]{3,2,1,0:T(8,128)(2,1)}, u32[]{:S(2)}) copy-start(bf16[1,2,128,512]{3,2,1,0:T(8,128)(2,1)} %param.12) | copy-start | bytes 786436
  67.1 19.0 %collective-permute-start.4 = (bf16[192,2048]{1,0:T(8,128)(2,1)S(1)}, bf16[192,2048]{1,0:T(8,128)(2,1)}, u32[]{:S(2)}, u32[]{:S(2)}) collective-permute-start(bf16[192,2048]{1,0:T(8,128)(2,1)S(1)} %slice.82), channel_id=1, source_target_pairs={{0,1},{1,2},{2,3},{3,0},{4,5},{5,6},{6,7},{7,4},{8,9},{9,10},{10,1... | collective-permute-start | bytes 2359304 | tf_op jit(solution)/shard_map/ppermute | solution.py:13
  68.4 17.8 %collective-permute-start.5 = (bf16[192,2048]{1,0:T(8,128)(2,1)S(1)}, bf16[192,2048]{1,0:T(8,128)(2,1)}, u32[]{:S(2)}, u32[]{:S(2)}) collective-permute-start(bf16[192,2048]{1,0:T(8,128)(2,1)S(1)} %slice.83), channel_id=1, source_target_pairs={{0,3},{1,0},{2,1},{3,2},{4,7},{5,4},{6,5},{7,6},{8,11},{9,8},{10,9... | collective-permute-start | bytes 2359304 | tf_op jit(solution)/shard_map/ppermute | solution.py:13
  71.2 3.1 %collective-permute-start.9 = (bf16[2,128,256]{2,1,0:T(8,128)(2,1)S(1)}, bf16[2,128,256]{2,1,0:T(8,128)(2,1)S(1)}, u32[]{:S(2)}, u32[]{:S(2)}) collective-permute-start(bf16[2,128,256]{2,1,0:T(8,128)(2,1)S(1)} %dynamic-slice_bitcast_fusion), channel_id=1, source_target_pairs={{0,4},{4,0},{1,5},{5,1},{2,6},{6,2},{3,7},{7,3},{8,12},{12,8},{9,1... | collective-permute-start | bytes 393224 | tf_op jit(solution)/shard_map/ppermute | solution.py:43
  73.3 47.7 %collective-permute-start.10 = (bf16[1024,256]{1,0:T(8,128)(2,1)S(1)}, bf16[1024,256]{1,0:T(8,128)(2,1)S(1)}, u32[]{:S(2)}, u32[]{:S(2)}) collective-permute-start(bf16[1024,256]{1,0:T(8,128)(2,1)S(1)} %get-tuple-element.40), channel_id=1, source_target_pairs={{0,4},{4,0},{1,5},{5,1},{2,6},{6,2},{3,7},{7,3},{8,12},{12,8},{9,1... | collective-permute-start | bytes 1572872 | tf_op jit(solution)/shard_map/ppermute | solution.py:43
  125.0 4.1 %collective-permute-start.11 = (f32[768,256]{1,0:T(8,128)S(1)}, f32[768,256]{1,0:T(8,128)S(1)}, u32[]{:S(2)}, u32[]{:S(2)}) collective-permute-start(f32[768,256]{1,0:T(8,128)S(1)} %constant_dynamic-slice_fusion.3), channel_id=1, source_target_pairs={{0,4},{4,0},{1,5},{5,1},{2,6},{6,2},{3,7},{7,3},{8,12},{12,8},{9,1... | collective-permute-start | bytes 2359304 | tf_op jit(solution)/shard_map/ppermute | solution.py:43
  129.3 7.8 %collective-permute-start.12 = (f32[192,256]{1,0:T(8,128)S(1)}, f32[192,256]{1,0:T(8,128)S(1)}, u32[]{:S(2)}, u32[]{:S(2)}) collective-permute-start(f32[192,256]{1,0:T(8,128)S(1)} %get-tuple-element.49), channel_id=1, source_target_pairs={{0,1},{1,2},{2,3},{3,0},{4,5},{5,6},{6,7},{7,4},{8,9},{9,10},{10,1... | collective-permute-start | bytes 589832 | tf_op jit(solution)/shard_map/ppermute | solution.py:13
  130.6 11.4 %collective-permute-start.13 = (f32[192,256]{1,0:T(8,128)S(1)}, f32[192,256]{1,0:T(8,128)S(1)}, u32[]{:S(2)}, u32[]{:S(2)}) collective-permute-start(f32[192,256]{1,0:T(8,128)S(1)} %get-tuple-element.51), channel_id=1, source_target_pairs={{0,2},{1,3},{2,0},{3,1},{4,6},{5,7},{6,4},{7,5},{8,10},{9,11},{10,... | collective-permute-start | bytes 589832 | tf_op jit(solution)/shard_map/ppermute | solution.py:13
  133.0 9.0 %collective-permute-start.14 = (f32[192,256]{1,0:T(8,128)S(1)}, f32[192,256]{1,0:T(8,128)S(1)}, u32[]{:S(2)}, u32[]{:S(2)}) collective-permute-start(f32[192,256]{1,0:T(8,128)S(1)} %get-tuple-element.50), channel_id=1, source_target_pairs={{0,3},{1,0},{2,1},{3,2},{4,7},{5,4},{6,5},{7,6},{8,11},{9,8},{10,9... | collective-permute-start | bytes 589832 | tf_op jit(solution)/shard_map/ppermute | solution.py:13
  142.1 5.2 %collective-permute-start.15 = (bf16[192,256]{1,0:T(8,128)(2,1)S(1)}, bf16[192,256]{1,0:T(8,128)(2,1)S(1)}, u32[]{:S(2)}, u32[]{:S(2)}) collective-permute-start(bf16[192,256]{1,0:T(8,128)(2,1)S(1)} %get-tuple-element.32), channel_id=1, source_target_pairs={{0,1},{1,2},{2,3},{3,0},{4,5},{5,6},{6,7},{7,4},{8,9},{9,10},{10,1... | collective-permute-start | bytes 294920 | tf_op jit(solution)/shard_map/ppermute | solution.py:13
  143.2 7.4 %collective-permute-start.16 = (bf16[192,256]{1,0:T(8,128)(2,1)S(1)}, bf16[192,256]{1,0:T(8,128)(2,1)S(1)}, u32[]{:S(2)}, u32[]{:S(2)}) collective-permute-start(bf16[192,256]{1,0:T(8,128)(2,1)S(1)} %get-tuple-element.32), channel_id=1, source_target_pairs={{0,2},{1,3},{2,0},{3,1},{4,6},{5,7},{6,4},{7,5},{8,10},{9,11},{10,... | collective-permute-start | bytes 294920 | tf_op jit(solution)/shard_map/ppermute | solution.py:13
  146.0 4.8 %collective-permute-start.17 = (bf16[192,256]{1,0:T(8,128)(2,1)S(1)}, bf16[192,256]{1,0:T(8,128)(2,1)S(1)}, u32[]{:S(2)}, u32[]{:S(2)}) collective-permute-start(bf16[192,256]{1,0:T(8,128)(2,1)S(1)} %get-tuple-element.32), channel_id=1, source_target_pairs={{0,3},{1,0},{2,1},{3,2},{4,7},{5,4},{6,5},{7,6},{8,11},{9,8},{10,9... | collective-permute-start | bytes 294920 | tf_op jit(solution)/shard_map/ppermute | solution.py:13
  150.9 2.6 %collective-permute-start.18 = (bf16[768,256]{1,0:T(8,128)(2,1)S(1)}, bf16[768,256]{1,0:T(8,128)(2,1)S(1)}, u32[]{:S(2)}, u32[]{:S(2)}) collective-permute-start(bf16[768,256]{1,0:T(8,128)(2,1)S(1)} %constant_dynamic-update-slice_fusion), channel_id=1, source_target_pairs={{0,4},{4,0},{1,5},{5,1},{2,6},{6,2},{3,7},{7,3},{8,12},{12,8},{9,1... | collective-permute-start | bytes 1179656 | tf_op jit(solution)/shard_map/ppermute | solution.py:43
  156.7 43.5 %all-to-all-start.1 = ((bf16[32,48,512]{2,1,0:T(8,128)(2,1)}), bf16[32,48,512]{2,1,0:T(8,128)(2,1)S(1)}, u32[]{:S(2)}, u32[]{:S(2)}) async-start(bf16[32,48,512]{2,1,0:T(8,128)(2,1)} %bitcast.8), calls=%async_computation.1 | async-start | bytes 3145728 | tf_op jit(solution)/shard_map/all_to_all | solution.py:89
  162.6 9.9 %copy-start.10 = (bf16[8192,1024]{1,0:T(8,128)(2,1)S(1)}, bf16[8192,1024]{1,0:T(8,128)(2,1)}, u32[]{:S(2)}) copy-start(bf16[8192,1024]{1,0:T(8,128)(2,1)} %all-gather.2.cloned.1.call-done) | copy-start | bytes 50331652
  167.2 5.3 %copy-start.2 = (bf16[384,2048]{1,0:T(8,128)(2,1)S(1)}, bf16[384,2048]{1,0:T(8,128)(2,1)}, u32[]{:S(2)}) copy-start(bf16[384,2048]{1,0:T(8,128)(2,1)} %copy-done.1) | copy-start | bytes 4718596
  201.7 3.7 %collective-permute-start.19 = (bf16[384,512]{1,0:T(8,128)(2,1)S(1)}, bf16[384,512]{1,0:T(8,128)(2,1)S(1)}, u32[]{:S(2)}, u32[]{:S(2)}) collective-permute-start(bf16[384,512]{1,0:T(8,128)(2,1)S(1)} %slice.91), channel_id=1, source_target_pairs={{0,4},{4,0},{1,5},{5,1},{2,6},{6,2},{3,7},{7,3},{8,12},{12,8},{9,1... | collective-permute-start | bytes 1179656 | tf_op jit(solution)/shard_map/ppermute | solution.py:43
  (2 other events, 5.9 us)
Sparse Core Ops, SparseCore 0:
  13.4 137.1 all-gather.1

commit v6 on v5

--- a/solution.py
+++ b/solution.py
@@ -96,7 +96,8 @@
         piece = mid // ny
         total = cut_at(partial, y, piece, 0)
         for d in range(1, ny):
-            total = total + shift(cut_at(partial, ring(d), piece, 0), d, ny)
+            sent = cut_at(partial, ring(d), piece, 0).astype(bf16)
+            total = total + shift(sent, d, ny).astype(f32)
         total = total.astype(bf16)
         code = jnp.zeros((mid, 2 * rank_width), bf16)
         code = lax.dynamic_update_slice_in_dim(code, total, y * jnp.uint32(piece), 0)

time: 214 us -> 210 us (0.981)
  waiting for transfers between devices: 116 us -> 111 us
    ppermute x13, waiting for transfers between devices: 52 us -> 46.4 us  [shift(): lax.ppermute(array, 'y', [(i, (i + distance) % size) for i in range(size)])]
  transfers between devices with their start and end apart: 23 -> 23, of which waited for: 15 -> 15; matrix products, arithmetic and copies ran while one was open for 15% -> 16% of each run, Pallas kernels for 0% -> 0%
where the time goes in v6:
time: 210 us; the launch traced here: 209 us
  waiting for transfers between devices  111 us (53%)
  starting transfers between devices  46.5 us (22%)
  matrix products  26.4 us (13%)
  between operations  13.7 us (7%)
  other arithmetic  8.09 us (4%)
  local copies, waits for them, and re-layouts  3.44 us (2%)
    all_to_all x2, waiting for transfers between devices, exchange(): return lax.all_to_all(array, CHIP, 0, 0, tiled=True)  57.4 us
    ppermute x13, waiting for transfers between devices, shift(): lax.ppermute(array, 'y', [(i, (i + distance) % size) for i in range(size)])  46.4 us
    dot_general x8, matrix products, dot(): return jnp.dot(a, b, preferred_element_type=jnp.float32)  25 us
    ppermute x13, starting transfers between devices, shift(): lax.ppermute(array, 'y', [(i, (i + distance) % size) for i in range(size)])  18.6 us
    all_to_all x2, starting transfers between devices, exchange(): return lax.all_to_all(array, CHIP, 0, 0, tiled=True)  15.2 us
    ppermute x7, starting transfers between devices, swap(): return lax.ppermute(array, 'c', SWAP)  12.6 us
    ppermute x7, waiting for transfers between devices, swap(): return lax.ppermute(array, 'c', SWAP)  7.32 us
  transfers between devices with their start and end apart: 23, of which 15 were waited for; matrix products, arithmetic and copies ran while one was open for 16% of the time, Pallas kernels for 0%

profile of v6, /device:TPU:1, one launch (start us, length us, event | category | flops | bytes accessed | tf_op | source)
XLA Modules:
  0.0 209.2 jit_solution(16677516603582537341)
XLA Ops:
  6.5 1.5 broadcast_select_fusion.3
  8.1 3.3 %collective-permute-start.1 = (bf16[384,1024]{1,0:T(8,128)(2,1)S(1)}, bf16[384,1024]{1,0:T(8,128)(2,1)S(1)}, u32[]{:S(2)}, u32[]{:S(2)}) collective-permute-start(bf16[384,1024]{1,0:T(8,128)(2,1)S(1)} %get-tuple-element.36), channel_id=1, source_target_pairs={{0,4},{4,0},{1,5},{5,1},{2,6},{6,2},{3,7},{7,3},{8,12},{12,8},{9,1... | collective-permute-start | bytes 2359304 | tf_op jit(solution)/shard_map/ppermute | solution.py:43
  14.9 4.0 %fusion.14 = bf16[1536,1024]{1,0:T(8,128)(2,1)} fusion(s32[768]{0:T(1024)S(1)} %pad_add_fusion, bf16[384,1024]{1,0:T(8,128)(2,1)S(1)} %collective-permute-done.1, bf16[384,1024]{1,0:T(8,128)(2,1)S(1)} %get-tuple-element.35), kind=kOutput, calls=%fused_computation.17 | convolution fusion | flops 2421817344 | bytes 4721664 | tf_op jit(solution)/shard_map/dot_general | solution.py:17
  18.9 9.5 %all-to-all-start = ((bf16[32,48,1024]{2,1,0:T(8,128)(2,1)}), bf16[32,48,1024]{2,1,0:T(8,128)(2,1)}, u32[]{:S(2)}, u32[]{:S(2)}) async-start(bf16[32,48,1024]{2,1,0:T(8,128)(2,1)} %bitcast.38), calls=%async_computation | async-start | bytes 6291456 | tf_op jit(solution)/shard_map/all_to_all | solution.py:89
  29.0 1.4 collective-permute-start.2
  30.4 1.5 collective-permute-start.3
  31.9 2.6 %collective-permute-start.7 = (f32[384]{0:T(512)S(1)}, f32[384]{0:T(512)}, u32[]{:S(2)}, u32[]{:S(2)}) collective-permute-start(f32[384]{0:T(512)S(1)} %get-tuple-element.33), channel_id=1, source_target_pairs={{0,2},{1,3},{2,0},{3,1},{4,6},{5,7},{6,4},{7,5},{8,10},{9,11},{10,... | collective-permute-start | bytes 4616 | tf_op jit(solution)/shard_map/ppermute | solution.py:13
  35.6 1.6 fusion.19
  37.3 28.6 %collective-permute-done.2 = bf16[384,2048]{1,0:T(8,128)(2,1)} collective-permute-done((bf16[384,2048]{1,0:T(8,128)(2,1)S(1)}, bf16[384,2048]{1,0:T(8,128)(2,1)}, u32[]{:S(2)}, u32[]{:S(2)}) %collective-permute-start.2) | collective-permute-done | bytes 1572896 | tf_op jit(solution)/shard_map/ppermute | solution.py:13
  68.4 2.7 %collective-permute-start.5 = (bf16[192,2048]{1,0:T(8,128)(2,1)S(1)}, bf16[192,2048]{1,0:T(8,128)(2,1)}, u32[]{:S(2)}, u32[]{:S(2)}) collective-permute-start(bf16[192,2048]{1,0:T(8,128)(2,1)S(1)} %slice.83), channel_id=1, source_target_pairs={{0,3},{1,0},{2,1},{3,2},{4,7},{5,4},{6,5},{7,6},{8,11},{9,8},{10,9... | collective-permute-start | bytes 2359304 | tf_op jit(solution)/shard_map/ppermute | solution.py:13
  71.2 2.1 collective-permute-start.9
  75.1 10.9 %collective-permute-done.4 = bf16[192,2048]{1,0:T(8,128)(2,1)} collective-permute-done((bf16[192,2048]{1,0:T(8,128)(2,1)S(1)}, bf16[192,2048]{1,0:T(8,128)(2,1)}, u32[]{:S(2)}, u32[]{:S(2)}) %collective-permute-start.4) | collective-permute-done | bytes 786464 | tf_op jit(solution)/shard_map/ppermute | solution.py:13
  86.3 34.7 %all-to-all-done = bf16[32,48,1024]{2,1,0:T(8,128)(2,1)} async-done(((bf16[32,48,1024]{2,1,0:T(8,128)(2,1)}), bf16[32,48,1024]{2,1,0:T(8,128)(2,1)}, u32[]{:S(2)}, u32[]{:S(2)}) %all-to-all-start) | async-done | bytes 3145760 | tf_op jit(solution)/shard_map/all_to_all | solution.py:89
  121.0 3.7 %fusion.31 = f32[1536,512]{1,0:T(8,128)S(1)} fusion(bf16[1536,1024]{1,0:T(8,128)(2,1)} %bitcast.6, bf16[1024,256]{1,0:T(8,128)(2,1)S(1)} %collective-permute-done.10, bf16[1024,256]{1,0:T(8,128)(2,1)S(1)} %get-tuple-element.39), kind=kOutput, calls=%fused_computation.45 | convolution fusion | flops 1612709888 | bytes 7340032 | tf_op jit(solution)/shard_map/dot_general | solution.py:17
  125.0 1.9 collective-permute-start.11
  127.0 2.1 %collective-permute-done.11 = f32[768,256]{1,0:T(8,128)S(1)} collective-permute-done((f32[768,256]{1,0:T(8,128)S(1)}, f32[768,256]{1,0:T(8,128)S(1)}, u32[]{:S(2)}, u32[]{:S(2)}) %collective-permute-start.11) | collective-permute-done | bytes 786464 | tf_op jit(solution)/shard_map/ppermute | solution.py:43
  130.6 2.4 %collective-permute-start.13 = (bf16[192,256]{1,0:T(8,128)(2,1)S(1)}, bf16[192,256]{1,0:T(8,128)(2,1)S(1)}, u32[]{:S(2)}, u32[]{:S(2)}) collective-permute-start(bf16[192,256]{1,0:T(8,128)(2,1)S(1)} %get-tuple-element.51), channel_id=1, source_target_pairs={{0,2},{1,3},{2,0},{3,1},{4,6},{5,7},{6,4},{7,5},{8,10},{9,11},{10,... | collective-permute-start | bytes 294920 | tf_op jit(solution)/shard_map/ppermute | solution.py:13
  134.9 2.9 %collective-permute-done.13 = bf16[192,256]{1,0:T(8,128)(2,1)S(1)} collective-permute-done((bf16[192,256]{1,0:T(8,128)(2,1)S(1)}, bf16[192,256]{1,0:T(8,128)(2,1)S(1)}, u32[]{:S(2)}, u32[]{:S(2)}) %collective-permute-start.13) | collective-permute-done | bytes 98336 | tf_op jit(solution)/shard_map/ppermute | solution.py:13
  138.7 2.2 %collective-permute-start.16 = (bf16[192,256]{1,0:T(8,128)(2,1)S(1)}, bf16[192,256]{1,0:T(8,128)(2,1)S(1)}, u32[]{:S(2)}, u32[]{:S(2)}) collective-permute-start(bf16[192,256]{1,0:T(8,128)(2,1)S(1)} %get-tuple-element.32), channel_id=1, source_target_pairs={{0,2},{1,3},{2,0},{3,1},{4,6},{5,7},{6,4},{7,5},{8,10},{9,11},{10,... | collective-permute-start | bytes 294920 | tf_op jit(solution)/shard_map/ppermute | solution.py:13
  140.9 1.3 collective-permute-start.17
  145.2 2.2 %collective-permute-start.18 = (bf16[768,256]{1,0:T(8,128)(2,1)S(1)}, bf16[768,256]{1,0:T(8,128)(2,1)S(1)}, u32[]{:S(2)}, u32[]{:S(2)}) collective-permute-start(bf16[768,256]{1,0:T(8,128)(2,1)S(1)} %constant_dynamic-update-slice_fusion), channel_id=1, source_target_pairs={{0,4},{4,0},{1,5},{5,1},{2,6},{6,2},{3,7},{7,3},{8,12},{12,8},{9,1... | collective-permute-start | bytes 1179656 | tf_op jit(solution)/shard_map/ppermute | solution.py:43
  147.5 1.8 collective-permute-done.18
  150.4 2.2 %convolution_convert_fusion = bf16[1536,512]{1,0:T(8,128)(2,1)} fusion(bf16[512,512]{1,0:T(8,128)(2,1)S(1)} %copy-done.3, bf16[1536,256]{1,0:T(8,128)(2,1)S(1)} %get-tuple-element.42, bf16[1536,256]{1,0:T(8,128)(2,1)S(1)} %get-tuple-element.41), kind=kOutput, calls=%fused_computation.20 | convolution fusion | flops 809238528 | bytes 3670016 | tf_op jit(solution)/shard_map/dot_general | solution.py:17
  152.6 5.7 %all-to-all-start.1 = ((bf16[32,48,512]{2,1,0:T(8,128)(2,1)}), bf16[32,48,512]{2,1,0:T(8,128)(2,1)S(1)}, u32[]{:S(2)}, u32[]{:S(2)}) async-start(bf16[32,48,512]{2,1,0:T(8,128)(2,1)} %bitcast.8), calls=%async_computation.1 | async-start | bytes 3145728 | tf_op jit(solution)/shard_map/all_to_all | solution.py:89
  158.3 4.6 %fusion.4 = f32[384,1024]{1,0:T(8,128)S(1)} fusion(bf16[384,2048]{1,0:T(8,128)(2,1)} %collective-permute-done.3, bf16[4,2048,1024]{2,1,0:T(8,128)(2,1)} %bitcast.40, u32[]{:T(128)S(6)} %rem.58), kind=kOutput, calls=%fused_computation.5 | convolution fusion | flops 1610612736 | bytes 7340036 | tf_op jit(solution)/shard_map/dot_general | solution.py:17
  162.9 5.2 %fusion.6 = f32[384,1024]{1,0:T(8,128)S(1)} fusion(bf16[384,2048]{1,0:T(8,128)(2,1)} %collective-permute-done.2, bf16[4,2048,1024]{2,1,0:T(8,128)(2,1)} %bitcast.41, u32[]{:T(128)S(6)} %rem.60), kind=kOutput, calls=%fused_computation.7 | convolution fusion | flops 1610612736 | bytes 7340036 | tf_op jit(solution)/shard_map/dot_general | solution.py:17
  168.2 1.8 fusion.8
  170.0 3.2 %add_add_fusion = f32[384,1024]{1,0:T(8,128)S(1)} fusion(f32[384,1024]{1,0:T(8,128)S(1)} %fusion.4, f32[384,1024]{1,0:T(8,128)S(1)} %fusion.8, f32[384,1024]{1,0:T(8,128)S(1)} %fusion.6, bf16[4,2048,1024]{2,1,0:T(8,128)(2,1)S(1)} %bitcast.43, u32[]{:T(128)S(6)} %rem.59, bf16[192,2048]{1,0:T(8,128)(2,1)} %collective-permute-done.5, ...), kind=kOutput, calls=%fused_computation.39 | convolution fusion | flops 1614938112 | bytes 12058628 | tf_op jit(solution)/shard_map/dot_general | solution.py:17
  173.2 22.7 %all-to-all-done.1 = bf16[32,48,512]{2,1,0:T(8,128)(2,1)S(1)} async-done(((bf16[32,48,512]{2,1,0:T(8,128)(2,1)}), bf16[32,48,512]{2,1,0:T(8,128)(2,1)S(1)}, u32[]{:S(2)}, u32[]{:S(2)}) %all-to-all-start.1) | async-done | bytes 1572896 | tf_op jit(solution)/shard_map/all_to_all | solution.py:89
  195.9 1.4 fusion.29
  197.4 2.3 %collective-permute-start.19 = (bf16[384,512]{1,0:T(8,128)(2,1)S(1)}, bf16[384,512]{1,0:T(8,128)(2,1)S(1)}, u32[]{:S(2)}, u32[]{:S(2)}) collective-permute-start(bf16[384,512]{1,0:T(8,128)(2,1)S(1)} %slice.91), channel_id=1, source_target_pairs={{0,4},{4,0},{1,5},{5,1},{2,6},{6,2},{3,7},{7,3},{8,12},{12,8},{9,1... | collective-permute-start | bytes 1179656 | tf_op jit(solution)/shard_map/ppermute | solution.py:43
  199.7 1.3 collective-permute-done.19
  (78 shorter events, 19.8 us)
Async XLA Ops:
  6.5 151.8 %all-gather.2.cloned.1.call-start = ((), (), s32[]{:S(2)}) async-start(), calls=%async_computation.2 | async-start | bytes 17039360 | tf_op jit(solution)/shard_map/all_gather | solution.py:54
  6.5 4.9 %copy-start.7 = (bf16[128,512]{1,0:T(8,128)(2,1)S(1)}, bf16[128,512]{1,0:T(8,128)(2,1)}, u32[]{:S(2)}) copy-start(bf16[128,512]{1,0:T(8,128)(2,1)} %param.9) | copy-start | bytes 393220
  6.5 6.8 %copy-start.9 = (s32[384,1]{0,1:T(1,128)S(1)}, s32[384,1]{0,1:T(1,128)}, u32[]{:S(2)}) copy-start(s32[384,1]{0,1:T(1,128)} %param.13) | copy-start | bytes 4612
  8.1 5.2 %collective-permute-start.1 = (bf16[384,1024]{1,0:T(8,128)(2,1)S(1)}, bf16[384,1024]{1,0:T(8,128)(2,1)S(1)}, u32[]{:S(2)}, u32[]{:S(2)}) collective-permute-start(bf16[384,1024]{1,0:T(8,128)(2,1)S(1)} %get-tuple-element.36), channel_id=1, source_target_pairs={{0,4},{4,0},{1,5},{5,1},{2,6},{6,2},{3,7},{7,3},{8,12},{12,8},{9,1... | collective-permute-start | bytes 2359304 | tf_op jit(solution)/shard_map/ppermute | solution.py:43
  13.6 1.3 collective-permute-start
  18.9 9.6 %copy-start.8 = (bf16[2048]{0:T(1024)(128)(2,1)S(1)}, bf16[2048]{0:T(1024)(128)(2,1)}, u32[]{:S(2)}) copy-start(bf16[2048]{0:T(1024)(128)(2,1)} %param.8) | copy-start | bytes 12292
  18.9 9.6 %copy-start = (bf16[384,2048]{1,0:T(8,128)(2,1)S(1)}, bf16[384,2048]{1,0:T(8,128)(2,1)}, u32[]{:S(2)}) copy-start(bf16[384,2048]{1,0:T(8,128)(2,1)} %param.7) | copy-start | bytes 4718596
  18.9 102.0 %all-to-all-start = ((bf16[32,48,1024]{2,1,0:T(8,128)(2,1)}), bf16[32,48,1024]{2,1,0:T(8,128)(2,1)}, u32[]{:S(2)}, u32[]{:S(2)}) async-start(bf16[32,48,1024]{2,1,0:T(8,128)(2,1)} %bitcast.38), calls=%async_computation | async-start | bytes 6291456 | tf_op jit(solution)/shard_map/all_to_all | solution.py:89
  28.5 7.1 %copy-start.4 = (bf16[1,2,128,512]{3,2,1,0:T(8,128)(2,1)S(1)}, bf16[1,2,128,512]{3,2,1,0:T(8,128)(2,1)}, u32[]{:S(2)}) copy-start(bf16[1,2,128,512]{3,2,1,0:T(8,128)(2,1)} %param.12) | copy-start | bytes 786436
  29.0 8.2 %copy-start.1 = (bf16[384,2048]{1,0:T(8,128)(2,1)}, bf16[384,2048]{1,0:T(8,128)(2,1)S(1)}, u32[]{:S(2)}) copy-start(bf16[384,2048]{1,0:T(8,128)(2,1)S(1)} %get-tuple-element.22) | copy-start | bytes 4718596
  29.0 36.9 %collective-permute-start.2 = (bf16[384,2048]{1,0:T(8,128)(2,1)S(1)}, bf16[384,2048]{1,0:T(8,128)(2,1)}, u32[]{:S(2)}, u32[]{:S(2)}) collective-permute-start(bf16[384,2048]{1,0:T(8,128)(2,1)S(1)} %get-tuple-element.22), channel_id=1, source_target_pairs={{0,1},{1,2},{2,3},{3,0},{4,5},{5,6},{6,7},{7,4},{8,9},{9,10},{10,1... | collective-permute-start | bytes 4718600 | tf_op jit(solution)/shard_map/ppermute | solution.py:13
  30.4 36.8 %collective-permute-start.3 = (bf16[384,2048]{1,0:T(8,128)(2,1)S(1)}, bf16[384,2048]{1,0:T(8,128)(2,1)}, u32[]{:S(2)}, u32[]{:S(2)}) collective-permute-start(bf16[384,2048]{1,0:T(8,128)(2,1)S(1)} %get-tuple-element.22), channel_id=1, source_target_pairs={{0,3},{1,0},{2,1},{3,2},{4,7},{5,4},{6,5},{7,6},{8,11},{9,8},{10,9... | collective-permute-start | bytes 4718600 | tf_op jit(solution)/shard_map/ppermute | solution.py:13
  31.9 39.2 %collective-permute-start.6 = (f32[384]{0:T(512)S(1)}, f32[384]{0:T(512)}, u32[]{:S(2)}, u32[]{:S(2)}) collective-permute-start(f32[384]{0:T(512)S(1)} %get-tuple-element.33), channel_id=1, source_target_pairs={{0,1},{1,2},{2,3},{3,0},{4,5},{5,6},{6,7},{7,4},{8,9},{9,10},{10,1... | collective-permute-start | bytes 4616 | tf_op jit(solution)/shard_map/ppermute | solution.py:13
  31.9 41.3 %collective-permute-start.7 = (f32[384]{0:T(512)S(1)}, f32[384]{0:T(512)}, u32[]{:S(2)}, u32[]{:S(2)}) collective-permute-start(f32[384]{0:T(512)S(1)} %get-tuple-element.33), channel_id=1, source_target_pairs={{0,2},{1,3},{2,0},{3,1},{4,6},{5,7},{6,4},{7,5},{8,10},{9,11},{10,... | collective-permute-start | bytes 4616 | tf_op jit(solution)/shard_map/ppermute | solution.py:13
  34.5 39.1 %collective-permute-start.8 = (f32[384]{0:T(512)S(1)}, f32[384]{0:T(512)}, u32[]{:S(2)}, u32[]{:S(2)}) collective-permute-start(f32[384]{0:T(512)S(1)} %get-tuple-element.33), channel_id=1, source_target_pairs={{0,3},{1,0},{2,1},{3,2},{4,7},{5,4},{6,5},{7,6},{8,11},{9,8},{10,9... | collective-permute-start | bytes 4616 | tf_op jit(solution)/shard_map/ppermute | solution.py:13
  37.3 33.9 %copy-start.5 = (bf16[1,2,128,512]{3,2,1,0:T(8,128)(2,1)S(1)}, bf16[1,2,128,512]{3,2,1,0:T(8,128)(2,1)}, u32[]{:S(2)}) copy-start(bf16[1,2,128,512]{3,2,1,0:T(8,128)(2,1)} %param.12) | copy-start | bytes 786436
  67.1 19.0 %collective-permute-start.4 = (bf16[192,2048]{1,0:T(8,128)(2,1)S(1)}, bf16[192,2048]{1,0:T(8,128)(2,1)}, u32[]{:S(2)}, u32[]{:S(2)}) collective-permute-start(bf16[192,2048]{1,0:T(8,128)(2,1)S(1)} %slice.82), channel_id=1, source_target_pairs={{0,1},{1,2},{2,3},{3,0},{4,5},{5,6},{6,7},{7,4},{8,9},{9,10},{10,1... | collective-permute-start | bytes 2359304 | tf_op jit(solution)/shard_map/ppermute | solution.py:13
  68.4 17.8 %collective-permute-start.5 = (bf16[192,2048]{1,0:T(8,128)(2,1)S(1)}, bf16[192,2048]{1,0:T(8,128)(2,1)}, u32[]{:S(2)}, u32[]{:S(2)}) collective-permute-start(bf16[192,2048]{1,0:T(8,128)(2,1)S(1)} %slice.83), channel_id=1, source_target_pairs={{0,3},{1,0},{2,1},{3,2},{4,7},{5,4},{6,5},{7,6},{8,11},{9,8},{10,9... | collective-permute-start | bytes 2359304 | tf_op jit(solution)/shard_map/ppermute | solution.py:13
  71.2 3.1 %collective-permute-start.9 = (bf16[2,128,256]{2,1,0:T(8,128)(2,1)S(1)}, bf16[2,128,256]{2,1,0:T(8,128)(2,1)S(1)}, u32[]{:S(2)}, u32[]{:S(2)}) collective-permute-start(bf16[2,128,256]{2,1,0:T(8,128)(2,1)S(1)} %dynamic-slice_bitcast_fusion), channel_id=1, source_target_pairs={{0,4},{4,0},{1,5},{5,1},{2,6},{6,2},{3,7},{7,3},{8,12},{12,8},{9,1... | collective-permute-start | bytes 393224 | tf_op jit(solution)/shard_map/ppermute | solution.py:43
  73.3 47.7 %collective-permute-start.10 = (bf16[1024,256]{1,0:T(8,128)(2,1)S(1)}, bf16[1024,256]{1,0:T(8,128)(2,1)S(1)}, u32[]{:S(2)}, u32[]{:S(2)}) collective-permute-start(bf16[1024,256]{1,0:T(8,128)(2,1)S(1)} %get-tuple-element.40), channel_id=1, source_target_pairs={{0,4},{4,0},{1,5},{5,1},{2,6},{6,2},{3,7},{7,3},{8,12},{12,8},{9,1... | collective-permute-start | bytes 1572872 | tf_op jit(solution)/shard_map/ppermute | solution.py:43
  125.0 4.1 %collective-permute-start.11 = (f32[768,256]{1,0:T(8,128)S(1)}, f32[768,256]{1,0:T(8,128)S(1)}, u32[]{:S(2)}, u32[]{:S(2)}) collective-permute-start(f32[768,256]{1,0:T(8,128)S(1)} %constant_dynamic-slice_fusion), channel_id=1, source_target_pairs={{0,4},{4,0},{1,5},{5,1},{2,6},{6,2},{3,7},{7,3},{8,12},{12,8},{9,1... | collective-permute-start | bytes 2359304 | tf_op jit(solution)/shard_map/ppermute | solution.py:43
  129.3 5.6 %collective-permute-start.12 = (bf16[192,256]{1,0:T(8,128)(2,1)S(1)}, bf16[192,256]{1,0:T(8,128)(2,1)S(1)}, u32[]{:S(2)}, u32[]{:S(2)}) collective-permute-start(bf16[192,256]{1,0:T(8,128)(2,1)S(1)} %get-tuple-element.49), channel_id=1, source_target_pairs={{0,1},{1,2},{2,3},{3,0},{4,5},{5,6},{6,7},{7,4},{8,9},{9,10},{10,1... | collective-permute-start | bytes 294920 | tf_op jit(solution)/shard_map/ppermute | solution.py:13
  130.6 7.2 %collective-permute-start.13 = (bf16[192,256]{1,0:T(8,128)(2,1)S(1)}, bf16[192,256]{1,0:T(8,128)(2,1)S(1)}, u32[]{:S(2)}, u32[]{:S(2)}) collective-permute-start(bf16[192,256]{1,0:T(8,128)(2,1)S(1)} %get-tuple-element.51), channel_id=1, source_target_pairs={{0,2},{1,3},{2,0},{3,1},{4,6},{5,7},{6,4},{7,5},{8,10},{9,11},{10,... | collective-permute-start | bytes 294920 | tf_op jit(solution)/shard_map/ppermute | solution.py:13
  133.0 4.8 %collective-permute-start.14 = (bf16[192,256]{1,0:T(8,128)(2,1)S(1)}, bf16[192,256]{1,0:T(8,128)(2,1)S(1)}, u32[]{:S(2)}, u32[]{:S(2)}) collective-permute-start(bf16[192,256]{1,0:T(8,128)(2,1)S(1)} %get-tuple-element.50), channel_id=1, source_target_pairs={{0,3},{1,0},{2,1},{3,2},{4,7},{5,4},{6,5},{7,6},{8,11},{9,8},{10,9... | collective-permute-start | bytes 294920 | tf_op jit(solution)/shard_map/ppermute | solution.py:13
  137.9 5.2 %collective-permute-start.15 = (bf16[192,256]{1,0:T(8,128)(2,1)S(1)}, bf16[192,256]{1,0:T(8,128)(2,1)S(1)}, u32[]{:S(2)}, u32[]{:S(2)}) collective-permute-start(bf16[192,256]{1,0:T(8,128)(2,1)S(1)} %get-tuple-element.32), channel_id=1, source_target_pairs={{0,1},{1,2},{2,3},{3,0},{4,5},{5,6},{6,7},{7,4},{8,9},{9,10},{10,1... | collective-permute-start | bytes 294920 | tf_op jit(solution)/shard_map/ppermute | solution.py:13
  138.7 5.6 %collective-permute-start.16 = (bf16[192,256]{1,0:T(8,128)(2,1)S(1)}, bf16[192,256]{1,0:T(8,128)(2,1)S(1)}, u32[]{:S(2)}, u32[]{:S(2)}) collective-permute-start(bf16[192,256]{1,0:T(8,128)(2,1)S(1)} %get-tuple-element.32), channel_id=1, source_target_pairs={{0,2},{1,3},{2,0},{3,1},{4,6},{5,7},{6,4},{7,5},{8,10},{9,11},{10,... | collective-permute-start | bytes 294920 | tf_op jit(solution)/shard_map/ppermute | solution.py:13
  140.9 4.3 %collective-permute-start.17 = (bf16[192,256]{1,0:T(8,128)(2,1)S(1)}, bf16[192,256]{1,0:T(8,128)(2,1)S(1)}, u32[]{:S(2)}, u32[]{:S(2)}) collective-permute-start(bf16[192,256]{1,0:T(8,128)(2,1)S(1)} %get-tuple-element.32), channel_id=1, source_target_pairs={{0,3},{1,0},{2,1},{3,2},{4,7},{5,4},{6,5},{7,6},{8,11},{9,8},{10,9... | collective-permute-start | bytes 294920 | tf_op jit(solution)/shard_map/ppermute | solution.py:13
  145.2 4.0 %collective-permute-start.18 = (bf16[768,256]{1,0:T(8,128)(2,1)S(1)}, bf16[768,256]{1,0:T(8,128)(2,1)S(1)}, u32[]{:S(2)}, u32[]{:S(2)}) collective-permute-start(bf16[768,256]{1,0:T(8,128)(2,1)S(1)} %constant_dynamic-update-slice_fusion), channel_id=1, source_target_pairs={{0,4},{4,0},{1,5},{5,1},{2,6},{6,2},{3,7},{7,3},{8,12},{12,8},{9,1... | collective-permute-start | bytes 1179656 | tf_op jit(solution)/shard_map/ppermute | solution.py:43
  152.6 43.3 %all-to-all-start.1 = ((bf16[32,48,512]{2,1,0:T(8,128)(2,1)}), bf16[32,48,512]{2,1,0:T(8,128)(2,1)S(1)}, u32[]{:S(2)}, u32[]{:S(2)}) async-start(bf16[32,48,512]{2,1,0:T(8,128)(2,1)} %bitcast.8), calls=%async_computation.1 | async-start | bytes 3145728 | tf_op jit(solution)/shard_map/all_to_all | solution.py:89
  158.3 9.9 %copy-start.10 = (bf16[8192,1024]{1,0:T(8,128)(2,1)S(1)}, bf16[8192,1024]{1,0:T(8,128)(2,1)}, u32[]{:S(2)}) copy-start(bf16[8192,1024]{1,0:T(8,128)(2,1)} %all-gather.2.cloned.1.call-done) | copy-start | bytes 50331652
  162.9 5.3 %copy-start.2 = (bf16[384,2048]{1,0:T(8,128)(2,1)S(1)}, bf16[384,2048]{1,0:T(8,128)(2,1)}, u32[]{:S(2)}) copy-start(bf16[384,2048]{1,0:T(8,128)(2,1)} %copy-done.1) | copy-start | bytes 4718596
  197.4 3.7 %collective-permute-start.19 = (bf16[384,512]{1,0:T(8,128)(2,1)S(1)}, bf16[384,512]{1,0:T(8,128)(2,1)S(1)}, u32[]{:S(2)}, u32[]{:S(2)}) collective-permute-start(bf16[384,512]{1,0:T(8,128)(2,1)S(1)} %slice.91), channel_id=1, source_target_pairs={{0,4},{4,0},{1,5},{5,1},{2,6},{6,2},{3,7},{7,3},{8,12},{12,8},{9,1... | collective-permute-start | bytes 1179656 | tf_op jit(solution)/shard_map/ppermute | solution.py:43
  (2 other events, 5.9 us)
Sparse Core Ops, SparseCore 0:
  13.4 137.1 all-gather.1

commit v7 on v6

--- a/solution.py
+++ b/solution.py
@@ -94,14 +94,15 @@
         mid = count // 2
         partial = cut_at(partial, half_at, mid, 0) + swap(cut_at(partial, 1 - half_at, mid, 0))
         piece = mid // ny
+        far_first = sorted(range(1, ny), key=lambda d: -min(d, ny - d))
         total = cut_at(partial, y, piece, 0)
-        for d in range(1, ny):
+        for d in far_first:
             sent = cut_at(partial, ring(d), piece, 0).astype(bf16)
             total = total + shift(sent, d, ny).astype(f32)
         total = total.astype(bf16)
         code = jnp.zeros((mid, 2 * rank_width), bf16)
         code = lax.dynamic_update_slice_in_dim(code, total, y * jnp.uint32(piece), 0)
-        for d in range(1, ny):
+        for d in far_first:
             code = lax.dynamic_update_slice_in_dim(
                 code, shift(total, d, ny), ring(-d) * jnp.uint32(piece), 0
             )

time: 210 us -> 210 us (level)
  transfers between devices with their start and end apart: 23 -> 23, of which waited for: 15 -> 14; matrix products, arithmetic and copies ran while one was open for 16% -> 16% of each run, Pallas kernels for 0% -> 0%
where the time goes in v7:
time: 210 us; the launch traced here: 209 us
  waiting for transfers between devices  111 us (53%)
  starting transfers between devices  46.8 us (22%)
  matrix products  26.4 us (13%)
  between operations  13.8 us (7%)
  other arithmetic  8.09 us (4%)
  local copies, waits for them, and re-layouts  3.44 us (2%)
    all_to_all x2, waiting for transfers between devices, exchange(): return lax.all_to_all(array, CHIP, 0, 0, tiled=True)  57.4 us
    ppermute x13, waiting for transfers between devices, shift(): lax.ppermute(array, 'y', [(i, (i + distance) % size) for i in range(size)])  46 us
    dot_general x8, matrix products, dot(): return jnp.dot(a, b, preferred_element_type=jnp.float32)  25 us
    ppermute x13, starting transfers between devices, shift(): lax.ppermute(array, 'y', [(i, (i + distance) % size) for i in range(size)])  19.4 us
    all_to_all x2, starting transfers between devices, exchange(): return lax.all_to_all(array, CHIP, 0, 0, tiled=True)  15.2 us
    ppermute x7, starting transfers between devices, swap(): return lax.ppermute(array, 'c', SWAP)  12.1 us
    ppermute x7, waiting for transfers between devices, swap(): return lax.ppermute(array, 'c', SWAP)  7.38 us
  transfers between devices with their start and end apart: 23, of which 14 were waited for; matrix products, arithmetic and copies ran while one was open for 16% of the time, Pallas kernels for 0%

profile of v7, /device:TPU:1, one launch (start us, length us, event | category | flops | bytes accessed | tf_op | source)
XLA Modules:
  0.0 209.2 jit_solution(8900945244506116782)
XLA Ops:
  6.5 1.5 broadcast_select_fusion.3
  8.1 3.3 %collective-permute-start.1 = (bf16[384,1024]{1,0:T(8,128)(2,1)S(1)}, bf16[384,1024]{1,0:T(8,128)(2,1)S(1)}, u32[]{:S(2)}, u32[]{:S(2)}) collective-permute-start(bf16[384,1024]{1,0:T(8,128)(2,1)S(1)} %get-tuple-element.36), channel_id=1, source_target_pairs={{0,4},{4,0},{1,5},{5,1},{2,6},{6,2},{3,7},{7,3},{8,12},{12,8},{9,1... | collective-permute-start | bytes 2359304 | tf_op jit(solution)/shard_map/ppermute | solution.py:43
  14.9 4.0 %fusion.14 = bf16[1536,1024]{1,0:T(8,128)(2,1)} fusion(s32[768]{0:T(1024)S(1)} %pad_add_fusion, bf16[384,1024]{1,0:T(8,128)(2,1)S(1)} %collective-permute-done.1, bf16[384,1024]{1,0:T(8,128)(2,1)S(1)} %get-tuple-element.35), kind=kOutput, calls=%fused_computation.17 | convolution fusion | flops 2421817344 | bytes 4721664 | tf_op jit(solution)/shard_map/dot_general | solution.py:17
  18.9 9.5 %all-to-all-start = ((bf16[32,48,1024]{2,1,0:T(8,128)(2,1)}), bf16[32,48,1024]{2,1,0:T(8,128)(2,1)}, u32[]{:S(2)}, u32[]{:S(2)}) async-start(bf16[32,48,1024]{2,1,0:T(8,128)(2,1)} %bitcast.38), calls=%async_computation | async-start | bytes 6291456 | tf_op jit(solution)/shard_map/all_to_all | solution.py:89
  30.4 1.5 collective-permute-start.3
  31.9 2.6 %collective-permute-start.7 = (f32[384]{0:T(512)S(1)}, f32[384]{0:T(512)}, u32[]{:S(2)}, u32[]{:S(2)}) collective-permute-start(f32[384]{0:T(512)S(1)} %get-tuple-element.33), channel_id=1, source_target_pairs={{0,2},{1,3},{2,0},{3,1},{4,6},{5,7},{6,4},{7,5},{8,10},{9,11},{10,... | collective-permute-start | bytes 4616 | tf_op jit(solution)/shard_map/ppermute | solution.py:13
  35.6 1.6 fusion.19
  37.3 28.6 %collective-permute-done.2 = bf16[384,2048]{1,0:T(8,128)(2,1)} collective-permute-done((bf16[384,2048]{1,0:T(8,128)(2,1)S(1)}, bf16[384,2048]{1,0:T(8,128)(2,1)}, u32[]{:S(2)}, u32[]{:S(2)}) %collective-permute-start.2) | collective-permute-done | bytes 1572896 | tf_op jit(solution)/shard_map/ppermute | solution.py:13
  68.4 2.7 %collective-permute-start.5 = (bf16[192,2048]{1,0:T(8,128)(2,1)S(1)}, bf16[192,2048]{1,0:T(8,128)(2,1)}, u32[]{:S(2)}, u32[]{:S(2)}) collective-permute-start(bf16[192,2048]{1,0:T(8,128)(2,1)S(1)} %slice.83), channel_id=1, source_target_pairs={{0,3},{1,0},{2,1},{3,2},{4,7},{5,4},{6,5},{7,6},{8,11},{9,8},{10,9... | collective-permute-start | bytes 2359304 | tf_op jit(solution)/shard_map/ppermute | solution.py:13
  71.2 2.1 collective-permute-start.9
  75.1 10.9 %collective-permute-done.4 = bf16[192,2048]{1,0:T(8,128)(2,1)} collective-permute-done((bf16[192,2048]{1,0:T(8,128)(2,1)S(1)}, bf16[192,2048]{1,0:T(8,128)(2,1)}, u32[]{:S(2)}, u32[]{:S(2)}) %collective-permute-start.4) | collective-permute-done | bytes 786464 | tf_op jit(solution)/shard_map/ppermute | solution.py:13
  86.3 34.7 %all-to-all-done = bf16[32,48,1024]{2,1,0:T(8,128)(2,1)} async-done(((bf16[32,48,1024]{2,1,0:T(8,128)(2,1)}), bf16[32,48,1024]{2,1,0:T(8,128)(2,1)}, u32[]{:S(2)}, u32[]{:S(2)}) %all-to-all-start) | async-done | bytes 3145760 | tf_op jit(solution)/shard_map/all_to_all | solution.py:89
  121.0 3.7 %fusion.31 = f32[1536,512]{1,0:T(8,128)S(1)} fusion(bf16[1536,1024]{1,0:T(8,128)(2,1)} %bitcast.6, bf16[1024,256]{1,0:T(8,128)(2,1)S(1)} %collective-permute-done.10, bf16[1024,256]{1,0:T(8,128)(2,1)S(1)} %get-tuple-element.39), kind=kOutput, calls=%fused_computation.45 | convolution fusion | flops 1612709888 | bytes 7340032 | tf_op jit(solution)/shard_map/dot_general | solution.py:17
  125.0 1.9 collective-permute-start.11
  127.0 2.1 %collective-permute-done.11 = f32[768,256]{1,0:T(8,128)S(1)} collective-permute-done((f32[768,256]{1,0:T(8,128)S(1)}, f32[768,256]{1,0:T(8,128)S(1)}, u32[]{:S(2)}, u32[]{:S(2)}) %collective-permute-start.11) | collective-permute-done | bytes 786464 | tf_op jit(solution)/shard_map/ppermute | solution.py:43
  129.3 2.8 %collective-permute-start.12 = (bf16[192,256]{1,0:T(8,128)(2,1)S(1)}, bf16[192,256]{1,0:T(8,128)(2,1)S(1)}, u32[]{:S(2)}, u32[]{:S(2)}) collective-permute-start(bf16[192,256]{1,0:T(8,128)(2,1)S(1)} %get-tuple-element.49), channel_id=1, source_target_pairs={{0,2},{1,3},{2,0},{3,1},{4,6},{5,7},{6,4},{7,5},{8,10},{9,11},{10,... | collective-permute-start | bytes 294920 | tf_op jit(solution)/shard_map/ppermute | solution.py:13
  132.4 2.4 %collective-permute-start.14 = (bf16[192,256]{1,0:T(8,128)(2,1)S(1)}, bf16[192,256]{1,0:T(8,128)(2,1)S(1)}, u32[]{:S(2)}, u32[]{:S(2)}) collective-permute-start(bf16[192,256]{1,0:T(8,128)(2,1)S(1)} %get-tuple-element.50), channel_id=1, source_target_pairs={{0,3},{1,0},{2,1},{3,2},{4,7},{5,4},{6,5},{7,6},{8,11},{9,8},{10,9... | collective-permute-start | bytes 294920 | tf_op jit(solution)/shard_map/ppermute | solution.py:13
  135.1 2.2 %collective-permute-done.13 = bf16[192,256]{1,0:T(8,128)(2,1)S(1)} collective-permute-done((bf16[192,256]{1,0:T(8,128)(2,1)S(1)}, bf16[192,256]{1,0:T(8,128)(2,1)S(1)}, u32[]{:S(2)}, u32[]{:S(2)}) %collective-permute-start.13) | collective-permute-done | bytes 98336 | tf_op jit(solution)/shard_map/ppermute | solution.py:13
  137.4 1.8 collective-permute-start.15
  139.2 1.5 collective-permute-start.16
  142.5 3.1 %collective-permute-done.16 = bf16[192,256]{1,0:T(8,128)(2,1)S(1)} collective-permute-done((bf16[192,256]{1,0:T(8,128)(2,1)S(1)}, bf16[192,256]{1,0:T(8,128)(2,1)S(1)}, u32[]{:S(2)}, u32[]{:S(2)}) %collective-permute-start.16) | collective-permute-done | bytes 98336 | tf_op jit(solution)/shard_map/ppermute | solution.py:13
  145.7 1.7 collective-permute-start.18
  147.4 1.9 collective-permute-done.18
  150.4 2.2 %convolution_convert_fusion = bf16[1536,512]{1,0:T(8,128)(2,1)} fusion(bf16[512,512]{1,0:T(8,128)(2,1)S(1)} %copy-done.3, bf16[1536,256]{1,0:T(8,128)(2,1)S(1)} %get-tuple-element.42, bf16[1536,256]{1,0:T(8,128)(2,1)S(1)} %get-tuple-element.41), kind=kOutput, calls=%fused_computation.20 | convolution fusion | flops 809238528 | bytes 3670016 | tf_op jit(solution)/shard_map/dot_general | solution.py:17
  152.6 5.7 %all-to-all-start.1 = ((bf16[32,48,512]{2,1,0:T(8,128)(2,1)}), bf16[32,48,512]{2,1,0:T(8,128)(2,1)S(1)}, u32[]{:S(2)}, u32[]{:S(2)}) async-start(bf16[32,48,512]{2,1,0:T(8,128)(2,1)} %bitcast.8), calls=%async_computation.1 | async-start | bytes 3145728 | tf_op jit(solution)/shard_map/all_to_all | solution.py:89
  158.3 4.6 %fusion.4 = f32[384,1024]{1,0:T(8,128)S(1)} fusion(bf16[384,2048]{1,0:T(8,128)(2,1)} %collective-permute-done.3, bf16[4,2048,1024]{2,1,0:T(8,128)(2,1)} %bitcast.40, u32[]{:T(128)S(6)} %rem.59), kind=kOutput, calls=%fused_computation.5 | convolution fusion | flops 1610612736 | bytes 7340036 | tf_op jit(solution)/shard_map/dot_general | solution.py:17
  162.9 5.2 %fusion.6 = f32[384,1024]{1,0:T(8,128)S(1)} fusion(bf16[384,2048]{1,0:T(8,128)(2,1)} %collective-permute-done.2, bf16[4,2048,1024]{2,1,0:T(8,128)(2,1)} %bitcast.41, u32[]{:T(128)S(6)} %rem.60), kind=kOutput, calls=%fused_computation.7 | convolution fusion | flops 1610612736 | bytes 7340036 | tf_op jit(solution)/shard_map/dot_general | solution.py:17
  168.2 1.8 fusion.8
  170.0 3.2 %add_add_fusion = f32[384,1024]{1,0:T(8,128)S(1)} fusion(f32[384,1024]{1,0:T(8,128)S(1)} %fusion.4, f32[384,1024]{1,0:T(8,128)S(1)} %fusion.8, f32[384,1024]{1,0:T(8,128)S(1)} %fusion.6, bf16[4,2048,1024]{2,1,0:T(8,128)(2,1)S(1)} %bitcast.43, u32[]{:T(128)S(6)} %rem.58, bf16[192,2048]{1,0:T(8,128)(2,1)} %collective-permute-done.5, ...), kind=kOutput, calls=%fused_computation.39 | convolution fusion | flops 1614938112 | bytes 12058628 | tf_op jit(solution)/shard_map/dot_general | solution.py:17
  173.2 22.7 %all-to-all-done.1 = bf16[32,48,512]{2,1,0:T(8,128)(2,1)S(1)} async-done(((bf16[32,48,512]{2,1,0:T(8,128)(2,1)}), bf16[32,48,512]{2,1,0:T(8,128)(2,1)S(1)}, u32[]{:S(2)}, u32[]{:S(2)}) %all-to-all-start.1) | async-done | bytes 1572896 | tf_op jit(solution)/shard_map/all_to_all | solution.py:89
  195.9 1.4 fusion.29
  197.4 2.3 %collective-permute-start.19 = (bf16[384,512]{1,0:T(8,128)(2,1)S(1)}, bf16[384,512]{1,0:T(8,128)(2,1)S(1)}, u32[]{:S(2)}, u32[]{:S(2)}) collective-permute-start(bf16[384,512]{1,0:T(8,128)(2,1)S(1)} %slice.91), channel_id=1, source_target_pairs={{0,4},{4,0},{1,5},{5,1},{2,6},{6,2},{3,7},{7,3},{8,12},{12,8},{9,1... | collective-permute-start | bytes 1179656 | tf_op jit(solution)/shard_map/ppermute | solution.py:43
  (78 shorter events, 18.0 us)
Async XLA Ops:
  6.5 151.8 %all-gather.2.cloned.1.call-start = ((), (), s32[]{:S(2)}) async-start(), calls=%async_computation.2 | async-start | bytes 17039360 | tf_op jit(solution)/shard_map/all_gather | solution.py:54
  6.5 4.9 %copy-start.7 = (bf16[128,512]{1,0:T(8,128)(2,1)S(1)}, bf16[128,512]{1,0:T(8,128)(2,1)}, u32[]{:S(2)}) copy-start(bf16[128,512]{1,0:T(8,128)(2,1)} %param.9) | copy-start | bytes 393220
  6.5 6.8 %copy-start.9 = (s32[384,1]{0,1:T(1,128)S(1)}, s32[384,1]{0,1:T(1,128)}, u32[]{:S(2)}) copy-start(s32[384,1]{0,1:T(1,128)} %param.13) | copy-start | bytes 4612
  8.1 5.2 %collective-permute-start.1 = (bf16[384,1024]{1,0:T(8,128)(2,1)S(1)}, bf16[384,1024]{1,0:T(8,128)(2,1)S(1)}, u32[]{:S(2)}, u32[]{:S(2)}) collective-permute-start(bf16[384,1024]{1,0:T(8,128)(2,1)S(1)} %get-tuple-element.36), channel_id=1, source_target_pairs={{0,4},{4,0},{1,5},{5,1},{2,6},{6,2},{3,7},{7,3},{8,12},{12,8},{9,1... | collective-permute-start | bytes 2359304 | tf_op jit(solution)/shard_map/ppermute | solution.py:43
  13.6 1.3 collective-permute-start
  18.9 9.6 %copy-start.8 = (bf16[2048]{0:T(1024)(128)(2,1)S(1)}, bf16[2048]{0:T(1024)(128)(2,1)}, u32[]{:S(2)}) copy-start(bf16[2048]{0:T(1024)(128)(2,1)} %param.8) | copy-start | bytes 12292
  18.9 9.6 %copy-start = (bf16[384,2048]{1,0:T(8,128)(2,1)S(1)}, bf16[384,2048]{1,0:T(8,128)(2,1)}, u32[]{:S(2)}) copy-start(bf16[384,2048]{1,0:T(8,128)(2,1)} %param.7) | copy-start | bytes 4718596
  18.9 102.0 %all-to-all-start = ((bf16[32,48,1024]{2,1,0:T(8,128)(2,1)}), bf16[32,48,1024]{2,1,0:T(8,128)(2,1)}, u32[]{:S(2)}, u32[]{:S(2)}) async-start(bf16[32,48,1024]{2,1,0:T(8,128)(2,1)} %bitcast.38), calls=%async_computation | async-start | bytes 6291456 | tf_op jit(solution)/shard_map/all_to_all | solution.py:89
  28.5 7.1 %copy-start.4 = (bf16[1,2,128,512]{3,2,1,0:T(8,128)(2,1)S(1)}, bf16[1,2,128,512]{3,2,1,0:T(8,128)(2,1)}, u32[]{:S(2)}) copy-start(bf16[1,2,128,512]{3,2,1,0:T(8,128)(2,1)} %param.12) | copy-start | bytes 786436
  29.0 8.2 %copy-start.1 = (bf16[384,2048]{1,0:T(8,128)(2,1)}, bf16[384,2048]{1,0:T(8,128)(2,1)S(1)}, u32[]{:S(2)}) copy-start(bf16[384,2048]{1,0:T(8,128)(2,1)S(1)} %get-tuple-element.22) | copy-start | bytes 4718596
  29.0 36.9 %collective-permute-start.2 = (bf16[384,2048]{1,0:T(8,128)(2,1)S(1)}, bf16[384,2048]{1,0:T(8,128)(2,1)}, u32[]{:S(2)}, u32[]{:S(2)}) collective-permute-start(bf16[384,2048]{1,0:T(8,128)(2,1)S(1)} %get-tuple-element.22), channel_id=1, source_target_pairs={{0,1},{1,2},{2,3},{3,0},{4,5},{5,6},{6,7},{7,4},{8,9},{9,10},{10,1... | collective-permute-start | bytes 4718600 | tf_op jit(solution)/shard_map/ppermute | solution.py:13
  30.4 36.8 %collective-permute-start.3 = (bf16[384,2048]{1,0:T(8,128)(2,1)S(1)}, bf16[384,2048]{1,0:T(8,128)(2,1)}, u32[]{:S(2)}, u32[]{:S(2)}) collective-permute-start(bf16[384,2048]{1,0:T(8,128)(2,1)S(1)} %get-tuple-element.22), channel_id=1, source_target_pairs={{0,3},{1,0},{2,1},{3,2},{4,7},{5,4},{6,5},{7,6},{8,11},{9,8},{10,9... | collective-permute-start | bytes 4718600 | tf_op jit(solution)/shard_map/ppermute | solution.py:13
  31.9 39.2 %collective-permute-start.6 = (f32[384]{0:T(512)S(1)}, f32[384]{0:T(512)}, u32[]{:S(2)}, u32[]{:S(2)}) collective-permute-start(f32[384]{0:T(512)S(1)} %get-tuple-element.33), channel_id=1, source_target_pairs={{0,1},{1,2},{2,3},{3,0},{4,5},{5,6},{6,7},{7,4},{8,9},{9,10},{10,1... | collective-permute-start | bytes 4616 | tf_op jit(solution)/shard_map/ppermute | solution.py:13
  31.9 41.3 %collective-permute-start.7 = (f32[384]{0:T(512)S(1)}, f32[384]{0:T(512)}, u32[]{:S(2)}, u32[]{:S(2)}) collective-permute-start(f32[384]{0:T(512)S(1)} %get-tuple-element.33), channel_id=1, source_target_pairs={{0,2},{1,3},{2,0},{3,1},{4,6},{5,7},{6,4},{7,5},{8,10},{9,11},{10,... | collective-permute-start | bytes 4616 | tf_op jit(solution)/shard_map/ppermute | solution.py:13
  34.5 39.1 %collective-permute-start.8 = (f32[384]{0:T(512)S(1)}, f32[384]{0:T(512)}, u32[]{:S(2)}, u32[]{:S(2)}) collective-permute-start(f32[384]{0:T(512)S(1)} %get-tuple-element.33), channel_id=1, source_target_pairs={{0,3},{1,0},{2,1},{3,2},{4,7},{5,4},{6,5},{7,6},{8,11},{9,8},{10,9... | collective-permute-start | bytes 4616 | tf_op jit(solution)/shard_map/ppermute | solution.py:13
  37.3 33.9 %copy-start.5 = (bf16[1,2,128,512]{3,2,1,0:T(8,128)(2,1)S(1)}, bf16[1,2,128,512]{3,2,1,0:T(8,128)(2,1)}, u32[]{:S(2)}) copy-start(bf16[1,2,128,512]{3,2,1,0:T(8,128)(2,1)} %param.12) | copy-start | bytes 786436
  67.1 19.0 %collective-permute-start.4 = (bf16[192,2048]{1,0:T(8,128)(2,1)S(1)}, bf16[192,2048]{1,0:T(8,128)(2,1)}, u32[]{:S(2)}, u32[]{:S(2)}) collective-permute-start(bf16[192,2048]{1,0:T(8,128)(2,1)S(1)} %slice.82), channel_id=1, source_target_pairs={{0,1},{1,2},{2,3},{3,0},{4,5},{5,6},{6,7},{7,4},{8,9},{9,10},{10,1... | collective-permute-start | bytes 2359304 | tf_op jit(solution)/shard_map/ppermute | solution.py:13
  68.4 17.8 %collective-permute-start.5 = (bf16[192,2048]{1,0:T(8,128)(2,1)S(1)}, bf16[192,2048]{1,0:T(8,128)(2,1)}, u32[]{:S(2)}, u32[]{:S(2)}) collective-permute-start(bf16[192,2048]{1,0:T(8,128)(2,1)S(1)} %slice.83), channel_id=1, source_target_pairs={{0,3},{1,0},{2,1},{3,2},{4,7},{5,4},{6,5},{7,6},{8,11},{9,8},{10,9... | collective-permute-start | bytes 2359304 | tf_op jit(solution)/shard_map/ppermute | solution.py:13
  71.2 3.1 %collective-permute-start.9 = (bf16[2,128,256]{2,1,0:T(8,128)(2,1)S(1)}, bf16[2,128,256]{2,1,0:T(8,128)(2,1)S(1)}, u32[]{:S(2)}, u32[]{:S(2)}) collective-permute-start(bf16[2,128,256]{2,1,0:T(8,128)(2,1)S(1)} %dynamic-slice_bitcast_fusion), channel_id=1, source_target_pairs={{0,4},{4,0},{1,5},{5,1},{2,6},{6,2},{3,7},{7,3},{8,12},{12,8},{9,1... | collective-permute-start | bytes 393224 | tf_op jit(solution)/shard_map/ppermute | solution.py:43
  73.3 47.7 %collective-permute-start.10 = (bf16[1024,256]{1,0:T(8,128)(2,1)S(1)}, bf16[1024,256]{1,0:T(8,128)(2,1)S(1)}, u32[]{:S(2)}, u32[]{:S(2)}) collective-permute-start(bf16[1024,256]{1,0:T(8,128)(2,1)S(1)} %get-tuple-element.40), channel_id=1, source_target_pairs={{0,4},{4,0},{1,5},{5,1},{2,6},{6,2},{3,7},{7,3},{8,12},{12,8},{9,1... | collective-permute-start | bytes 1572872 | tf_op jit(solution)/shard_map/ppermute | solution.py:43
  125.0 4.1 %collective-permute-start.11 = (f32[768,256]{1,0:T(8,128)S(1)}, f32[768,256]{1,0:T(8,128)S(1)}, u32[]{:S(2)}, u32[]{:S(2)}) collective-permute-start(f32[768,256]{1,0:T(8,128)S(1)} %constant_dynamic-slice_fusion), channel_id=1, source_target_pairs={{0,4},{4,0},{1,5},{5,1},{2,6},{6,2},{3,7},{7,3},{8,12},{12,8},{9,1... | collective-permute-start | bytes 2359304 | tf_op jit(solution)/shard_map/ppermute | solution.py:43
  129.3 5.8 %collective-permute-start.12 = (bf16[192,256]{1,0:T(8,128)(2,1)S(1)}, bf16[192,256]{1,0:T(8,128)(2,1)S(1)}, u32[]{:S(2)}, u32[]{:S(2)}) collective-permute-start(bf16[192,256]{1,0:T(8,128)(2,1)S(1)} %get-tuple-element.49), channel_id=1, source_target_pairs={{0,2},{1,3},{2,0},{3,1},{4,6},{5,7},{6,4},{7,5},{8,10},{9,11},{10,... | collective-permute-start | bytes 294920 | tf_op jit(solution)/shard_map/ppermute | solution.py:13
  132.1 5.2 %collective-permute-start.13 = (bf16[192,256]{1,0:T(8,128)(2,1)S(1)}, bf16[192,256]{1,0:T(8,128)(2,1)S(1)}, u32[]{:S(2)}, u32[]{:S(2)}) collective-permute-start(bf16[192,256]{1,0:T(8,128)(2,1)S(1)} %get-tuple-element.51), channel_id=1, source_target_pairs={{0,1},{1,2},{2,3},{3,0},{4,5},{5,6},{6,7},{7,4},{8,9},{9,10},{10,1... | collective-permute-start | bytes 294920 | tf_op jit(solution)/shard_map/ppermute | solution.py:13
  132.4 4.9 %collective-permute-start.14 = (bf16[192,256]{1,0:T(8,128)(2,1)S(1)}, bf16[192,256]{1,0:T(8,128)(2,1)S(1)}, u32[]{:S(2)}, u32[]{:S(2)}) collective-permute-start(bf16[192,256]{1,0:T(8,128)(2,1)S(1)} %get-tuple-element.50), channel_id=1, source_target_pairs={{0,3},{1,0},{2,1},{3,2},{4,7},{5,4},{6,5},{7,6},{8,11},{9,8},{10,9... | collective-permute-start | bytes 294920 | tf_op jit(solution)/shard_map/ppermute | solution.py:13
  137.4 5.1 %collective-permute-start.15 = (bf16[192,256]{1,0:T(8,128)(2,1)S(1)}, bf16[192,256]{1,0:T(8,128)(2,1)S(1)}, u32[]{:S(2)}, u32[]{:S(2)}) collective-permute-start(bf16[192,256]{1,0:T(8,128)(2,1)S(1)} %get-tuple-element.32), channel_id=1, source_target_pairs={{0,2},{1,3},{2,0},{3,1},{4,6},{5,7},{6,4},{7,5},{8,10},{9,11},{10,... | collective-permute-start | bytes 294920 | tf_op jit(solution)/shard_map/ppermute | solution.py:13
  139.2 6.4 %collective-permute-start.16 = (bf16[192,256]{1,0:T(8,128)(2,1)S(1)}, bf16[192,256]{1,0:T(8,128)(2,1)S(1)}, u32[]{:S(2)}, u32[]{:S(2)}) collective-permute-start(bf16[192,256]{1,0:T(8,128)(2,1)S(1)} %get-tuple-element.32), channel_id=1, source_target_pairs={{0,1},{1,2},{2,3},{3,0},{4,5},{5,6},{6,7},{7,4},{8,9},{9,10},{10,1... | collective-permute-start | bytes 294920 | tf_op jit(solution)/shard_map/ppermute | solution.py:13
  140.7 5.0 %collective-permute-start.17 = (bf16[192,256]{1,0:T(8,128)(2,1)S(1)}, bf16[192,256]{1,0:T(8,128)(2,1)S(1)}, u32[]{:S(2)}, u32[]{:S(2)}) collective-permute-start(bf16[192,256]{1,0:T(8,128)(2,1)S(1)} %get-tuple-element.32), channel_id=1, source_target_pairs={{0,3},{1,0},{2,1},{3,2},{4,7},{5,4},{6,5},{7,6},{8,11},{9,8},{10,9... | collective-permute-start | bytes 294920 | tf_op jit(solution)/shard_map/ppermute | solution.py:13
  145.7 3.6 %collective-permute-start.18 = (bf16[768,256]{1,0:T(8,128)(2,1)S(1)}, bf16[768,256]{1,0:T(8,128)(2,1)S(1)}, u32[]{:S(2)}, u32[]{:S(2)}) collective-permute-start(bf16[768,256]{1,0:T(8,128)(2,1)S(1)} %constant_dynamic-update-slice_fusion), channel_id=1, source_target_pairs={{0,4},{4,0},{1,5},{5,1},{2,6},{6,2},{3,7},{7,3},{8,12},{12,8},{9,1... | collective-permute-start | bytes 1179656 | tf_op jit(solution)/shard_map/ppermute | solution.py:43
  152.6 43.3 %all-to-all-start.1 = ((bf16[32,48,512]{2,1,0:T(8,128)(2,1)}), bf16[32,48,512]{2,1,0:T(8,128)(2,1)S(1)}, u32[]{:S(2)}, u32[]{:S(2)}) async-start(bf16[32,48,512]{2,1,0:T(8,128)(2,1)} %bitcast.8), calls=%async_computation.1 | async-start | bytes 3145728 | tf_op jit(solution)/shard_map/all_to_all | solution.py:89
  158.3 9.9 %copy-start.10 = (bf16[8192,1024]{1,0:T(8,128)(2,1)S(1)}, bf16[8192,1024]{1,0:T(8,128)(2,1)}, u32[]{:S(2)}) copy-start(bf16[8192,1024]{1,0:T(8,128)(2,1)} %all-gather.2.cloned.1.call-done) | copy-start | bytes 50331652
  162.9 5.3 %copy-start.2 = (bf16[384,2048]{1,0:T(8,128)(2,1)S(1)}, bf16[384,2048]{1,0:T(8,128)(2,1)}, u32[]{:S(2)}) copy-start(bf16[384,2048]{1,0:T(8,128)(2,1)} %copy-done.1) | copy-start | bytes 4718596
  197.4 3.7 %collective-permute-start.19 = (bf16[384,512]{1,0:T(8,128)(2,1)S(1)}, bf16[384,512]{1,0:T(8,128)(2,1)S(1)}, u32[]{:S(2)}, u32[]{:S(2)}) collective-permute-start(bf16[384,512]{1,0:T(8,128)(2,1)S(1)} %slice.91), channel_id=1, source_target_pairs={{0,4},{4,0},{1,5},{5,1},{2,6},{6,2},{3,7},{7,3},{8,12},{12,8},{9,1... | collective-permute-start | bytes 1179656 | tf_op jit(solution)/shard_map/ppermute | solution.py:43
  (2 other events, 5.9 us)
Sparse Core Ops, SparseCore 0:
  13.4 137.1 all-gather.1

commit v8 on v7

--- a/solution.py
+++ b/solution.py
@@ -54,13 +54,16 @@
     weights = lax.all_gather(mine, CHIP + ("c",), axis=0, tiled=True).reshape(ny, width, 2 * span)
 
     labels = row_judges[:, 0]
-    matches = (labels[:, None] == jnp.arange(judges, dtype=jnp.int32)[None, :]).astype(bf16)
     at = jnp.arange(rows, dtype=jnp.int32)
-    before = dot((at[:, None] > at[None, :]).astype(bf16), matches)
-    place = jnp.sum(before * matches.astype(f32), axis=1).astype(jnp.int32)
+    earlier = (at[:, None] > at[None, :]).astype(bf16)
     count = judges * 2 * cap
-    own_slot = labels * (2 * cap) + core * cap + place
-    slots = jnp.concatenate([own_slot, swap(own_slot)])
+
+    def slots_of(labels, core):
+        matches = (labels[:, None] == jnp.arange(judges, dtype=jnp.int32)[None, :]).astype(bf16)
+        place = jnp.sum(dot(earlier, matches) * matches.astype(f32), axis=1)
+        return labels * (2 * cap) + core * cap + place.astype(jnp.int32)
+
+    slots = jnp.concatenate([slots_of(labels, core), slots_of(swap(labels), 1 - core)])
     slot_at = jnp.arange(count, dtype=jnp.int32)
     choose = (slot_at[:, None] == slots[None, :]).astype(bf16)
     mine_at = ((slot_at // (2 * cap)) % 2 == core)[:, None]

time: 210 us -> 210 us (level)
    dot_general x8 -> x9, matrix products: 25 us -> 25.3 us  [dot(): return jnp.dot(a, b, preferred_element_type=jnp.float32)]
where the time goes in v8:
time: 210 us; the launch traced here: 209 us
  waiting for transfers between devices  110 us (52%)
  starting transfers between devices  46.9 us (22%)
  matrix products  26.7 us (13%)
  between operations  13.8 us (7%)
  other arithmetic  8.11 us (4%)
  local copies, waits for them, and re-layouts  3.43 us (2%)
    all_to_all x2, waiting for transfers between devices, exchange(): return lax.all_to_all(array, CHIP, 0, 0, tiled=True)  57.4 us
    ppermute x13, waiting for transfers between devices, shift(): lax.ppermute(array, 'y', [(i, (i + distance) % size) for i in range(size)])  45.9 us
    dot_general x9, matrix products, dot(): return jnp.dot(a, b, preferred_element_type=jnp.float32)  25.3 us
    ppermute x13, starting transfers between devices, shift(): lax.ppermute(array, 'y', [(i, (i + distance) % size) for i in range(size)])  19.4 us
    all_to_all x2, starting transfers between devices, exchange(): return lax.all_to_all(array, CHIP, 0, 0, tiled=True)  15.2 us
    ppermute x7, starting transfers between devices, swap(): return lax.ppermute(array, 'c', SWAP)  12.3 us
    ppermute x7, waiting for transfers between devices, swap(): return lax.ppermute(array, 'c', SWAP)  7 us
  transfers between devices with their start and end apart: 23, of which 14 were waited for; matrix products, arithmetic and copies ran while one was open for 16% of the time, Pallas kernels for 0%

profile of v8, /device:TPU:1, one launch (start us, length us, event | category | flops | bytes accessed | tf_op | source)
XLA Modules:
  0.0 209.3 jit_solution(17781525362679551209)
XLA Ops:
  6.5 1.5 broadcast_select_fusion.3
  8.1 3.3 %collective-permute-start.1 = (bf16[384,1024]{1,0:T(8,128)(2,1)S(1)}, bf16[384,1024]{1,0:T(8,128)(2,1)S(1)}, u32[]{:S(2)}, u32[]{:S(2)}) collective-permute-start(bf16[384,1024]{1,0:T(8,128)(2,1)S(1)} %get-tuple-element.36), channel_id=1, source_target_pairs={{0,4},{4,0},{1,5},{5,1},{2,6},{6,2},{3,7},{7,3},{8,12},{12,8},{9,1... | collective-permute-start | bytes 2359304 | tf_op jit(solution)/shard_map/ppermute | solution.py:43
  14.9 4.0 %fusion.14 = bf16[1536,1024]{1,0:T(8,128)(2,1)} fusion(s32[768]{0:T(1024)S(1)} %pad_add_fusion, bf16[384,1024]{1,0:T(8,128)(2,1)S(1)} %collective-permute-done.1, bf16[384,1024]{1,0:T(8,128)(2,1)S(1)} %get-tuple-element.35), kind=kOutput, calls=%fused_computation.17 | convolution fusion | flops 2421817344 | bytes 4721664 | tf_op jit(solution)/shard_map/dot_general | solution.py:17
  18.9 9.5 %all-to-all-start = ((bf16[32,48,1024]{2,1,0:T(8,128)(2,1)}), bf16[32,48,1024]{2,1,0:T(8,128)(2,1)}, u32[]{:S(2)}, u32[]{:S(2)}) async-start(bf16[32,48,1024]{2,1,0:T(8,128)(2,1)} %bitcast.38), calls=%async_computation | async-start | bytes 6291456 | tf_op jit(solution)/shard_map/all_to_all | solution.py:92
  30.4 1.5 collective-permute-start.3
  32.0 2.6 %collective-permute-start.7 = (f32[384]{0:T(512)S(1)}, f32[384]{0:T(512)}, u32[]{:S(2)}, u32[]{:S(2)}) collective-permute-start(f32[384]{0:T(512)S(1)} %get-tuple-element.33), channel_id=1, source_target_pairs={{0,2},{1,3},{2,0},{3,1},{4,6},{5,7},{6,4},{7,5},{8,10},{9,11},{10,... | collective-permute-start | bytes 4616 | tf_op jit(solution)/shard_map/ppermute | solution.py:13
  35.6 1.6 fusion.19
  37.3 28.6 %collective-permute-done.2 = bf16[384,2048]{1,0:T(8,128)(2,1)} collective-permute-done((bf16[384,2048]{1,0:T(8,128)(2,1)S(1)}, bf16[384,2048]{1,0:T(8,128)(2,1)}, u32[]{:S(2)}, u32[]{:S(2)}) %collective-permute-start.2) | collective-permute-done | bytes 1572896 | tf_op jit(solution)/shard_map/ppermute | solution.py:13
  68.4 2.7 %collective-permute-start.5 = (bf16[192,2048]{1,0:T(8,128)(2,1)S(1)}, bf16[192,2048]{1,0:T(8,128)(2,1)}, u32[]{:S(2)}, u32[]{:S(2)}) collective-permute-start(bf16[192,2048]{1,0:T(8,128)(2,1)S(1)} %slice.83), channel_id=1, source_target_pairs={{0,3},{1,0},{2,1},{3,2},{4,7},{5,4},{6,5},{7,6},{8,11},{9,8},{10,9... | collective-permute-start | bytes 2359304 | tf_op jit(solution)/shard_map/ppermute | solution.py:13
  71.2 2.1 collective-permute-start.9
  75.1 11.0 %collective-permute-done.4 = bf16[192,2048]{1,0:T(8,128)(2,1)} collective-permute-done((bf16[192,2048]{1,0:T(8,128)(2,1)S(1)}, bf16[192,2048]{1,0:T(8,128)(2,1)}, u32[]{:S(2)}, u32[]{:S(2)}) %collective-permute-start.4) | collective-permute-done | bytes 786464 | tf_op jit(solution)/shard_map/ppermute | solution.py:13
  86.2 34.7 %all-to-all-done = bf16[32,48,1024]{2,1,0:T(8,128)(2,1)} async-done(((bf16[32,48,1024]{2,1,0:T(8,128)(2,1)}), bf16[32,48,1024]{2,1,0:T(8,128)(2,1)}, u32[]{:S(2)}, u32[]{:S(2)}) %all-to-all-start) | async-done | bytes 3145760 | tf_op jit(solution)/shard_map/all_to_all | solution.py:92
  120.9 3.8 %fusion.32 = f32[1536,512]{1,0:T(8,128)S(1)} fusion(bf16[1536,1024]{1,0:T(8,128)(2,1)} %bitcast.6, bf16[1024,256]{1,0:T(8,128)(2,1)} %collective-permute-done.10, bf16[1024,256]{1,0:T(8,128)(2,1)S(1)} %get-tuple-element.39), kind=kOutput, calls=%fused_computation.47 | convolution fusion | flops 1612709888 | bytes 7340032 | tf_op jit(solution)/shard_map/dot_general | solution.py:17
  125.1 1.9 collective-permute-start.11
  127.1 2.1 collective-permute-done.11
  129.3 2.8 %collective-permute-start.12 = (bf16[192,256]{1,0:T(8,128)(2,1)S(1)}, bf16[192,256]{1,0:T(8,128)(2,1)S(1)}, u32[]{:S(2)}, u32[]{:S(2)}) collective-permute-start(bf16[192,256]{1,0:T(8,128)(2,1)S(1)} %get-tuple-element.49), channel_id=1, source_target_pairs={{0,2},{1,3},{2,0},{3,1},{4,6},{5,7},{6,4},{7,5},{8,10},{9,11},{10,... | collective-permute-start | bytes 294920 | tf_op jit(solution)/shard_map/ppermute | solution.py:13
  132.4 2.4 %collective-permute-start.14 = (bf16[192,256]{1,0:T(8,128)(2,1)S(1)}, bf16[192,256]{1,0:T(8,128)(2,1)S(1)}, u32[]{:S(2)}, u32[]{:S(2)}) collective-permute-start(bf16[192,256]{1,0:T(8,128)(2,1)S(1)} %get-tuple-element.50), channel_id=1, source_target_pairs={{0,3},{1,0},{2,1},{3,2},{4,7},{5,4},{6,5},{7,6},{8,11},{9,8},{10,9... | collective-permute-start | bytes 294920 | tf_op jit(solution)/shard_map/ppermute | solution.py:13
  135.0 2.2 %collective-permute-done.13 = bf16[192,256]{1,0:T(8,128)(2,1)S(1)} collective-permute-done((bf16[192,256]{1,0:T(8,128)(2,1)S(1)}, bf16[192,256]{1,0:T(8,128)(2,1)S(1)}, u32[]{:S(2)}, u32[]{:S(2)}) %collective-permute-start.13) | collective-permute-done | bytes 98336 | tf_op jit(solution)/shard_map/ppermute | solution.py:13
  137.3 1.8 collective-permute-start.15
  139.2 1.5 collective-permute-start.16
  142.4 3.1 %collective-permute-done.16 = bf16[192,256]{1,0:T(8,128)(2,1)S(1)} collective-permute-done((bf16[192,256]{1,0:T(8,128)(2,1)S(1)}, bf16[192,256]{1,0:T(8,128)(2,1)S(1)}, u32[]{:S(2)}, u32[]{:S(2)}) %collective-permute-start.16) | collective-permute-done | bytes 98336 | tf_op jit(solution)/shard_map/ppermute | solution.py:13
  145.6 1.9 collective-permute-start.18
  147.5 1.8 collective-permute-done.18
  150.4 2.2 %convolution_convert_fusion = bf16[1536,512]{1,0:T(8,128)(2,1)} fusion(bf16[512,512]{1,0:T(8,128)(2,1)S(1)} %copy-done.3, bf16[1536,256]{1,0:T(8,128)(2,1)S(1)} %get-tuple-element.42, bf16[1536,256]{1,0:T(8,128)(2,1)S(1)} %get-tuple-element.41), kind=kOutput, calls=%fused_computation.20 | convolution fusion | flops 809238528 | bytes 3670016 | tf_op jit(solution)/shard_map/dot_general | solution.py:17
  152.6 5.7 %all-to-all-start.1 = ((bf16[32,48,512]{2,1,0:T(8,128)(2,1)}), bf16[32,48,512]{2,1,0:T(8,128)(2,1)S(1)}, u32[]{:S(2)}, u32[]{:S(2)}) async-start(bf16[32,48,512]{2,1,0:T(8,128)(2,1)} %bitcast.8), calls=%async_computation.1 | async-start | bytes 3145728 | tf_op jit(solution)/shard_map/all_to_all | solution.py:92
  158.3 4.6 %fusion.4 = f32[384,1024]{1,0:T(8,128)S(1)} fusion(bf16[384,2048]{1,0:T(8,128)(2,1)} %collective-permute-done.3, bf16[4,2048,1024]{2,1,0:T(8,128)(2,1)} %bitcast.40, u32[]{:T(128)S(6)} %rem.59), kind=kOutput, calls=%fused_computation.5 | convolution fusion | flops 1610612736 | bytes 7340036 | tf_op jit(solution)/shard_map/dot_general | solution.py:17
  162.9 5.2 %fusion.6 = f32[384,1024]{1,0:T(8,128)S(1)} fusion(bf16[384,2048]{1,0:T(8,128)(2,1)} %collective-permute-done.2, bf16[4,2048,1024]{2,1,0:T(8,128)(2,1)} %bitcast.41, u32[]{:T(128)S(6)} %rem.60), kind=kOutput, calls=%fused_computation.7 | convolution fusion | flops 1610612736 | bytes 7340036 | tf_op jit(solution)/shard_map/dot_general | solution.py:17
  168.2 1.8 fusion.8
  170.0 3.2 %add_add_fusion = f32[384,1024]{1,0:T(8,128)S(1)} fusion(f32[384,1024]{1,0:T(8,128)S(1)} %fusion.4, f32[384,1024]{1,0:T(8,128)S(1)} %fusion.8, f32[384,1024]{1,0:T(8,128)S(1)} %fusion.6, bf16[4,2048,1024]{2,1,0:T(8,128)(2,1)S(1)} %bitcast.43, u32[]{:T(128)S(6)} %rem.58, bf16[192,2048]{1,0:T(8,128)(2,1)} %collective-permute-done.5, ...), kind=kOutput, calls=%fused_computation.39 | convolution fusion | flops 1614938112 | bytes 12058628 | tf_op jit(solution)/shard_map/dot_general | solution.py:17
  173.2 22.7 %all-to-all-done.1 = bf16[32,48,512]{2,1,0:T(8,128)(2,1)S(1)} async-done(((bf16[32,48,512]{2,1,0:T(8,128)(2,1)}), bf16[32,48,512]{2,1,0:T(8,128)(2,1)S(1)}, u32[]{:S(2)}, u32[]{:S(2)}) %all-to-all-start.1) | async-done | bytes 1572896 | tf_op jit(solution)/shard_map/all_to_all | solution.py:92
  195.9 1.4 fusion.29
  197.4 2.3 %collective-permute-start.19 = (bf16[384,512]{1,0:T(8,128)(2,1)S(1)}, bf16[384,512]{1,0:T(8,128)(2,1)S(1)}, u32[]{:S(2)}, u32[]{:S(2)}) collective-permute-start(bf16[384,512]{1,0:T(8,128)(2,1)S(1)} %slice.91), channel_id=1, source_target_pairs={{0,4},{4,0},{1,5},{5,1},{2,6},{6,2},{3,7},{7,3},{8,12},{12,8},{9,1... | collective-permute-start | bytes 1179656 | tf_op jit(solution)/shard_map/ppermute | solution.py:43
  (80 shorter events, 17.8 us)
Async XLA Ops:
  6.5 151.7 %all-gather.2.cloned.1.call-start = ((), (), s32[]{:S(2)}) async-start(), calls=%async_computation.2 | async-start | bytes 17039360 | tf_op jit(solution)/shard_map/all_gather | solution.py:54
  6.5 4.9 %copy-start.7 = (bf16[128,512]{1,0:T(8,128)(2,1)S(1)}, bf16[128,512]{1,0:T(8,128)(2,1)}, u32[]{:S(2)}) copy-start(bf16[128,512]{1,0:T(8,128)(2,1)} %param.9) | copy-start | bytes 393220
  6.5 6.8 %copy-start.9 = (s32[384,1]{0,1:T(1,128)S(1)}, s32[384,1]{0,1:T(1,128)}, u32[]{:S(2)}) copy-start(s32[384,1]{0,1:T(1,128)} %param.13) | copy-start | bytes 4612
  8.1 5.2 %collective-permute-start.1 = (bf16[384,1024]{1,0:T(8,128)(2,1)S(1)}, bf16[384,1024]{1,0:T(8,128)(2,1)S(1)}, u32[]{:S(2)}, u32[]{:S(2)}) collective-permute-start(bf16[384,1024]{1,0:T(8,128)(2,1)S(1)} %get-tuple-element.36), channel_id=1, source_target_pairs={{0,4},{4,0},{1,5},{5,1},{2,6},{6,2},{3,7},{7,3},{8,12},{12,8},{9,1... | collective-permute-start | bytes 2359304 | tf_op jit(solution)/shard_map/ppermute | solution.py:43
  13.4 1.3 collective-permute-start
  18.9 9.6 %copy-start.8 = (bf16[2048]{0:T(1024)(128)(2,1)S(1)}, bf16[2048]{0:T(1024)(128)(2,1)}, u32[]{:S(2)}) copy-start(bf16[2048]{0:T(1024)(128)(2,1)} %param.8) | copy-start | bytes 12292
  18.9 9.6 %copy-start = (bf16[384,2048]{1,0:T(8,128)(2,1)S(1)}, bf16[384,2048]{1,0:T(8,128)(2,1)}, u32[]{:S(2)}) copy-start(bf16[384,2048]{1,0:T(8,128)(2,1)} %param.7) | copy-start | bytes 4718596
  18.9 102.0 %all-to-all-start = ((bf16[32,48,1024]{2,1,0:T(8,128)(2,1)}), bf16[32,48,1024]{2,1,0:T(8,128)(2,1)}, u32[]{:S(2)}, u32[]{:S(2)}) async-start(bf16[32,48,1024]{2,1,0:T(8,128)(2,1)} %bitcast.38), calls=%async_computation | async-start | bytes 6291456 | tf_op jit(solution)/shard_map/all_to_all | solution.py:92
  28.5 7.1 %copy-start.4 = (bf16[1,2,128,512]{3,2,1,0:T(8,128)(2,1)S(1)}, bf16[1,2,128,512]{3,2,1,0:T(8,128)(2,1)}, u32[]{:S(2)}) copy-start(bf16[1,2,128,512]{3,2,1,0:T(8,128)(2,1)} %param.12) | copy-start | bytes 786436
  29.1 8.2 %copy-start.1 = (bf16[384,2048]{1,0:T(8,128)(2,1)}, bf16[384,2048]{1,0:T(8,128)(2,1)S(1)}, u32[]{:S(2)}) copy-start(bf16[384,2048]{1,0:T(8,128)(2,1)S(1)} %get-tuple-element.22) | copy-start | bytes 4718596
  29.1 36.9 %collective-permute-start.2 = (bf16[384,2048]{1,0:T(8,128)(2,1)S(1)}, bf16[384,2048]{1,0:T(8,128)(2,1)}, u32[]{:S(2)}, u32[]{:S(2)}) collective-permute-start(bf16[384,2048]{1,0:T(8,128)(2,1)S(1)} %get-tuple-element.22), channel_id=1, source_target_pairs={{0,1},{1,2},{2,3},{3,0},{4,5},{5,6},{6,7},{7,4},{8,9},{9,10},{10,1... | collective-permute-start | bytes 4718600 | tf_op jit(solution)/shard_map/ppermute | solution.py:13
  30.4 36.8 %collective-permute-start.3 = (bf16[384,2048]{1,0:T(8,128)(2,1)S(1)}, bf16[384,2048]{1,0:T(8,128)(2,1)}, u32[]{:S(2)}, u32[]{:S(2)}) collective-permute-start(bf16[384,2048]{1,0:T(8,128)(2,1)S(1)} %get-tuple-element.22), channel_id=1, source_target_pairs={{0,3},{1,0},{2,1},{3,2},{4,7},{5,4},{6,5},{7,6},{8,11},{9,8},{10,9... | collective-permute-start | bytes 4718600 | tf_op jit(solution)/shard_map/ppermute | solution.py:13
  32.0 39.2 %collective-permute-start.6 = (f32[384]{0:T(512)S(1)}, f32[384]{0:T(512)}, u32[]{:S(2)}, u32[]{:S(2)}) collective-permute-start(f32[384]{0:T(512)S(1)} %get-tuple-element.33), channel_id=1, source_target_pairs={{0,1},{1,2},{2,3},{3,0},{4,5},{5,6},{6,7},{7,4},{8,9},{9,10},{10,1... | collective-permute-start | bytes 4616 | tf_op jit(solution)/shard_map/ppermute | solution.py:13
  32.0 41.3 %collective-permute-start.7 = (f32[384]{0:T(512)S(1)}, f32[384]{0:T(512)}, u32[]{:S(2)}, u32[]{:S(2)}) collective-permute-start(f32[384]{0:T(512)S(1)} %get-tuple-element.33), channel_id=1, source_target_pairs={{0,2},{1,3},{2,0},{3,1},{4,6},{5,7},{6,4},{7,5},{8,10},{9,11},{10,... | collective-permute-start | bytes 4616 | tf_op jit(solution)/shard_map/ppermute | solution.py:13
  34.5 39.0 %collective-permute-start.8 = (f32[384]{0:T(512)S(1)}, f32[384]{0:T(512)}, u32[]{:S(2)}, u32[]{:S(2)}) collective-permute-start(f32[384]{0:T(512)S(1)} %get-tuple-element.33), channel_id=1, source_target_pairs={{0,3},{1,0},{2,1},{3,2},{4,7},{5,4},{6,5},{7,6},{8,11},{9,8},{10,9... | collective-permute-start | bytes 4616 | tf_op jit(solution)/shard_map/ppermute | solution.py:13
  37.3 33.9 %copy-start.5 = (bf16[1,2,128,512]{3,2,1,0:T(8,128)(2,1)S(1)}, bf16[1,2,128,512]{3,2,1,0:T(8,128)(2,1)}, u32[]{:S(2)}) copy-start(bf16[1,2,128,512]{3,2,1,0:T(8,128)(2,1)} %param.12) | copy-start | bytes 786436
  67.1 19.0 %collective-permute-start.4 = (bf16[192,2048]{1,0:T(8,128)(2,1)S(1)}, bf16[192,2048]{1,0:T(8,128)(2,1)}, u32[]{:S(2)}, u32[]{:S(2)}) collective-permute-start(bf16[192,2048]{1,0:T(8,128)(2,1)S(1)} %slice.82), channel_id=1, source_target_pairs={{0,1},{1,2},{2,3},{3,0},{4,5},{5,6},{6,7},{7,4},{8,9},{9,10},{10,1... | collective-permute-start | bytes 2359304 | tf_op jit(solution)/shard_map/ppermute | solution.py:13
  68.4 17.9 %collective-permute-start.5 = (bf16[192,2048]{1,0:T(8,128)(2,1)S(1)}, bf16[192,2048]{1,0:T(8,128)(2,1)}, u32[]{:S(2)}, u32[]{:S(2)}) collective-permute-start(bf16[192,2048]{1,0:T(8,128)(2,1)S(1)} %slice.83), channel_id=1, source_target_pairs={{0,3},{1,0},{2,1},{3,2},{4,7},{5,4},{6,5},{7,6},{8,11},{9,8},{10,9... | collective-permute-start | bytes 2359304 | tf_op jit(solution)/shard_map/ppermute | solution.py:13
  71.2 3.1 %collective-permute-start.9 = (bf16[2,128,256]{2,1,0:T(8,128)(2,1)S(1)}, bf16[2,128,256]{2,1,0:T(8,128)(2,1)S(1)}, u32[]{:S(2)}, u32[]{:S(2)}) collective-permute-start(bf16[2,128,256]{2,1,0:T(8,128)(2,1)S(1)} %dynamic-slice_bitcast_fusion), channel_id=1, source_target_pairs={{0,4},{4,0},{1,5},{5,1},{2,6},{6,2},{3,7},{7,3},{8,12},{12,8},{9,1... | collective-permute-start | bytes 393224 | tf_op jit(solution)/shard_map/ppermute | solution.py:43
  73.3 47.7 %collective-permute-start.10 = (bf16[1024,256]{1,0:T(8,128)(2,1)S(1)}, bf16[1024,256]{1,0:T(8,128)(2,1)}, u32[]{:S(2)}, u32[]{:S(2)}) collective-permute-start(bf16[1024,256]{1,0:T(8,128)(2,1)S(1)} %get-tuple-element.40), channel_id=1, source_target_pairs={{0,4},{4,0},{1,5},{5,1},{2,6},{6,2},{3,7},{7,3},{8,12},{12,8},{9,1... | collective-permute-start | bytes 1572872 | tf_op jit(solution)/shard_map/ppermute | solution.py:43
  125.1 4.0 %collective-permute-start.11 = (f32[768,256]{1,0:T(8,128)S(1)}, f32[768,256]{1,0:T(8,128)S(1)}, u32[]{:S(2)}, u32[]{:S(2)}) collective-permute-start(f32[768,256]{1,0:T(8,128)S(1)} %constant_dynamic-slice_fusion), channel_id=1, source_target_pairs={{0,4},{4,0},{1,5},{5,1},{2,6},{6,2},{3,7},{7,3},{8,12},{12,8},{9,1... | collective-permute-start | bytes 2359304 | tf_op jit(solution)/shard_map/ppermute | solution.py:43
  129.3 5.8 %collective-permute-start.12 = (bf16[192,256]{1,0:T(8,128)(2,1)S(1)}, bf16[192,256]{1,0:T(8,128)(2,1)S(1)}, u32[]{:S(2)}, u32[]{:S(2)}) collective-permute-start(bf16[192,256]{1,0:T(8,128)(2,1)S(1)} %get-tuple-element.49), channel_id=1, source_target_pairs={{0,2},{1,3},{2,0},{3,1},{4,6},{5,7},{6,4},{7,5},{8,10},{9,11},{10,... | collective-permute-start | bytes 294920 | tf_op jit(solution)/shard_map/ppermute | solution.py:13
  132.1 5.1 %collective-permute-start.13 = (bf16[192,256]{1,0:T(8,128)(2,1)S(1)}, bf16[192,256]{1,0:T(8,128)(2,1)S(1)}, u32[]{:S(2)}, u32[]{:S(2)}) collective-permute-start(bf16[192,256]{1,0:T(8,128)(2,1)S(1)} %get-tuple-element.51), channel_id=1, source_target_pairs={{0,1},{1,2},{2,3},{3,0},{4,5},{5,6},{6,7},{7,4},{8,9},{9,10},{10,1... | collective-permute-start | bytes 294920 | tf_op jit(solution)/shard_map/ppermute | solution.py:13
  132.4 4.8 %collective-permute-start.14 = (bf16[192,256]{1,0:T(8,128)(2,1)S(1)}, bf16[192,256]{1,0:T(8,128)(2,1)S(1)}, u32[]{:S(2)}, u32[]{:S(2)}) collective-permute-start(bf16[192,256]{1,0:T(8,128)(2,1)S(1)} %get-tuple-element.50), channel_id=1, source_target_pairs={{0,3},{1,0},{2,1},{3,2},{4,7},{5,4},{6,5},{7,6},{8,11},{9,8},{10,9... | collective-permute-start | bytes 294920 | tf_op jit(solution)/shard_map/ppermute | solution.py:13
  137.3 5.1 %collective-permute-start.15 = (bf16[192,256]{1,0:T(8,128)(2,1)S(1)}, bf16[192,256]{1,0:T(8,128)(2,1)S(1)}, u32[]{:S(2)}, u32[]{:S(2)}) collective-permute-start(bf16[192,256]{1,0:T(8,128)(2,1)S(1)} %get-tuple-element.32), channel_id=1, source_target_pairs={{0,2},{1,3},{2,0},{3,1},{4,6},{5,7},{6,4},{7,5},{8,10},{9,11},{10,... | collective-permute-start | bytes 294920 | tf_op jit(solution)/shard_map/ppermute | solution.py:13
  139.2 6.4 %collective-permute-start.16 = (bf16[192,256]{1,0:T(8,128)(2,1)S(1)}, bf16[192,256]{1,0:T(8,128)(2,1)S(1)}, u32[]{:S(2)}, u32[]{:S(2)}) collective-permute-start(bf16[192,256]{1,0:T(8,128)(2,1)S(1)} %get-tuple-element.32), channel_id=1, source_target_pairs={{0,1},{1,2},{2,3},{3,0},{4,5},{5,6},{6,7},{7,4},{8,9},{9,10},{10,1... | collective-permute-start | bytes 294920 | tf_op jit(solution)/shard_map/ppermute | solution.py:13
  140.7 4.9 %collective-permute-start.17 = (bf16[192,256]{1,0:T(8,128)(2,1)S(1)}, bf16[192,256]{1,0:T(8,128)(2,1)S(1)}, u32[]{:S(2)}, u32[]{:S(2)}) collective-permute-start(bf16[192,256]{1,0:T(8,128)(2,1)S(1)} %get-tuple-element.32), channel_id=1, source_target_pairs={{0,3},{1,0},{2,1},{3,2},{4,7},{5,4},{6,5},{7,6},{8,11},{9,8},{10,9... | collective-permute-start | bytes 294920 | tf_op jit(solution)/shard_map/ppermute | solution.py:13
  145.6 3.7 %collective-permute-start.18 = (bf16[768,256]{1,0:T(8,128)(2,1)S(1)}, bf16[768,256]{1,0:T(8,128)(2,1)S(1)}, u32[]{:S(2)}, u32[]{:S(2)}) collective-permute-start(bf16[768,256]{1,0:T(8,128)(2,1)S(1)} %constant_dynamic-update-slice_fusion), channel_id=1, source_target_pairs={{0,4},{4,0},{1,5},{5,1},{2,6},{6,2},{3,7},{7,3},{8,12},{12,8},{9,1... | collective-permute-start | bytes 1179656 | tf_op jit(solution)/shard_map/ppermute | solution.py:43
  152.6 43.3 %all-to-all-start.1 = ((bf16[32,48,512]{2,1,0:T(8,128)(2,1)}), bf16[32,48,512]{2,1,0:T(8,128)(2,1)S(1)}, u32[]{:S(2)}, u32[]{:S(2)}) async-start(bf16[32,48,512]{2,1,0:T(8,128)(2,1)} %bitcast.8), calls=%async_computation.1 | async-start | bytes 3145728 | tf_op jit(solution)/shard_map/all_to_all | solution.py:92
  158.3 9.9 %copy-start.10 = (bf16[8192,1024]{1,0:T(8,128)(2,1)S(1)}, bf16[8192,1024]{1,0:T(8,128)(2,1)}, u32[]{:S(2)}) copy-start(bf16[8192,1024]{1,0:T(8,128)(2,1)} %all-gather.2.cloned.1.call-done) | copy-start | bytes 50331652
  162.9 5.3 %copy-start.2 = (bf16[384,2048]{1,0:T(8,128)(2,1)S(1)}, bf16[384,2048]{1,0:T(8,128)(2,1)}, u32[]{:S(2)}) copy-start(bf16[384,2048]{1,0:T(8,128)(2,1)} %copy-done.1) | copy-start | bytes 4718596
  197.4 3.6 %collective-permute-start.19 = (bf16[384,512]{1,0:T(8,128)(2,1)S(1)}, bf16[384,512]{1,0:T(8,128)(2,1)S(1)}, u32[]{:S(2)}, u32[]{:S(2)}) collective-permute-start(bf16[384,512]{1,0:T(8,128)(2,1)S(1)} %slice.91), channel_id=1, source_target_pairs={{0,4},{4,0},{1,5},{5,1},{2,6},{6,2},{3,7},{7,3},{8,12},{12,8},{9,1... | collective-permute-start | bytes 1179656 | tf_op jit(solution)/shard_map/ppermute | solution.py:43
  (2 other events, 5.9 us)
Sparse Core Ops, SparseCore 0:
  13.4 137.1 all-gather.1
